TPU v7x, 32 devices: a whole 2x2x4 slice. The times are simulated.
32 devices in a mesh: blk: 8 (over y, x, core), head: 4 (over z).
Axes of the slice: x: 2, y: 2, z: 4, core: 2. Of those that a mesh axis runs over, the one named last changes fastest.
Arguments:
- tokens: bfloat16 [2, 8192, 768], P(None, ('blk', 'head')), may hold values from -6 to 6
- seq_lengths: int32 [2, 8], replicated, may hold values from 1 to 4096, 8192 in all within a row
- cluster_perm: int32 [2, 8192], replicated, may hold values from 0 to 8191, as said below
- out_grad: bfloat16 [2, 8192, 768], P(None, ('blk', 'head')), may hold values from -6 to 6
- qkv_weight: bfloat16 [768, 2304], P('blk', 'head'), may hold values from -0.3125 to 0.3125
- query_bias: bfloat16 [768], P('blk'), may hold values from -1.75 to 1.75
- value_bias: bfloat16 [768], P('blk'), may hold values from -1.75 to 1.75
- out_weight: bfloat16 [768, 768], P('blk', 'head'), may hold values from -0.875 to 0.875
- out_bias: bfloat16 [768], P('blk'), may hold values from -1.75 to 1.75
- attn_gain: bfloat16 [768], P('blk'), may hold values from 0.5 to 1.5
- attn_shift: bfloat16 [768], P('blk'), may hold values from -1.75 to 1.75
- up_weight: bfloat16 [768, 3072], P('blk', 'head'), may hold values from -0.21875 to 0.21875
- up_bias: bfloat16 [3072], P('blk'), may hold values from -1.75 to 1.75
- down_weight: bfloat16 [3072, 768], P('blk', 'head'), may hold values from -0.15625 to 0.15625
- down_bias: bfloat16 [768], P('blk'), may hold values from -1.75 to 1.75
- ffn_gain: bfloat16 [768], P('blk'), may hold values from 0.5 to 1.5
- ffn_shift: bfloat16 [768], P('blk'), may hold values from -1.75 to 1.75
Outputs:
- layer_out: bfloat16 [2, 8192, 768], P(None, ('blk', 'head'))
- tokens_grad: float32 [2, 8192, 768], P(None, ('blk', 'head'))
- qkv_weight_grad: float32 [768, 2304], P('blk', 'head')
- query_bias_grad: float32 [768], P('blk')
- value_bias_grad: float32 [768], P('blk')
- out_weight_grad: float32 [768, 768], P('blk', 'head')
- out_bias_grad: float32 [768], P('blk')
- attn_gain_grad: float32 [768], P('blk')
- attn_shift_grad: float32 [768], P('blk')
- up_weight_grad: float32 [768, 3072], P('blk', 'head')
- up_bias_grad: float32 [3072], P('blk')
- down_weight_grad: float32 [3072, 768], P('blk', 'head')
- down_bias_grad: float32 [768], P('blk')
- ffn_gain_grad: float32 [768], P('blk')
- ffn_shift_grad: float32 [768], P('blk')
Inputs may be any that keep to these rules, and one draw needn't show every extreme that they name: `seq_lengths`: row m holds the lengths of the 8 sequences of micro-batch m, laid end to end; each row sums to 8192 and its longest sequence has exactly 4096 positions. Each row is a permutation of the slots; position t of micro-batch m lies in cluster cluster_perm[m, t] // 128, so every cluster holds 128 positions. The slots deal positions evenly: for every b and c in 0 .. 7, exactly 128 positions t with t // 1024 == b have cluster_perm[m, t] // 1024 == c.
All inputs are finite; a program needn't handle non-finite values.
Results may differ from a plain program's by a relative error of at most 0.017.
Values may be sent and summed in bfloat16 or wider, within the bound.
A program may use at most 192 MiB of HBM per device.

v0:
```python
import jax
import jax.numpy as jnp
from jax import lax
from jax.sharding import PartitionSpec as P

HEAD_DIM = 64
CLUSTER = 128


masked_score = -1e30
norm_epsilon = 1e-05


def layer_norm(hidden, norm_gain, norm_shift):
    center = hidden - jnp.mean(hidden, axis=-1, keepdims=True)
    spread = jnp.mean(center * center, axis=-1, keepdims=True)
    return center * lax.rsqrt(spread + norm_epsilon) * norm_gain + norm_shift


def gelu_exact(values):
    return jax.nn.gelu(values, approximate=False)


def segment_of(positions, seq_ends):
    return jnp.sum((positions[:, None] >= seq_ends[None, :]).astype(jnp.int32), axis=1)


def cluster_scores(cluster_q, cluster_k, allowed):
    scores = (
        jnp.einsum("cqhd,ckhd->chqk", cluster_q, cluster_k, preferred_element_type=jnp.float32)
        * 0.125
    )
    return jnp.where(allowed[:, None], scores, masked_score)


def body(
    tokens,
    seq_lengths,
    cluster_perm,
    out_grad,
    qkv_weight,
    query_bias,
    value_bias,
    out_weight,
    out_bias,
    attn_gain,
    attn_shift,
    up_weight,
    up_bias,
    down_weight,
    down_bias,
    ffn_gain,
    ffn_shift,
):
    groups = lax.axis_size("head")
    micro_count, tok_rows, width = tokens.shape
    group_rows = tok_rows * groups
    heads_here = width // groups // HEAD_DIM
    clusters_here = group_rows // CLUSTER
    cluster_shape = (clusters_here, CLUSTER, heads_here, HEAD_DIM)
    flat_shape = (group_rows, heads_here * HEAD_DIM)
    total_rows = cluster_perm.shape[1]
    blk_index = lax.axis_index("blk")

    def reduce_grads(full):
        rows = (
            lax.psum_scatter(full[0], "blk", scatter_dimension=0, tiled=True),
            lax.psum_scatter(full[1], "blk", scatter_dimension=0, tiled=True),
            lax.psum_scatter(full[2], "blk", scatter_dimension=0, tiled=True),
            lax.psum_scatter(full[3], "blk", scatter_dimension=0, tiled=True),
            lax.psum_scatter(full[4], "blk", scatter_dimension=0, tiled=True),
            lax.psum_scatter(full[5], "blk", scatter_dimension=0, tiled=True),
            lax.psum_scatter(full[6], "blk", scatter_dimension=0, tiled=True),
            lax.psum_scatter(full[7], "blk", scatter_dimension=0, tiled=True),
            lax.psum_scatter(full[8], "blk", scatter_dimension=0, tiled=True),
            lax.psum_scatter(full[9], "blk", scatter_dimension=0, tiled=True),
            lax.psum_scatter(full[10], "blk", scatter_dimension=0, tiled=True),
            lax.psum_scatter(full[11], "blk", scatter_dimension=0, tiled=True),
            lax.psum_scatter(full[12], "blk", scatter_dimension=0, tiled=True),
        )
        tiled = [jnp.tile(member, groups) for member in rows[4:]]
        return (
            lax.psum_scatter(
                rows[0].astype(jnp.bfloat16), "head", scatter_dimension=1, tiled=True
            ).astype(jnp.float32),
            lax.psum_scatter(
                rows[1].astype(jnp.bfloat16), "head", scatter_dimension=1, tiled=True
            ).astype(jnp.float32),
            lax.psum_scatter(
                rows[2].astype(jnp.bfloat16), "head", scatter_dimension=1, tiled=True
            ).astype(jnp.float32),
            lax.psum_scatter(
                rows[3].astype(jnp.bfloat16), "head", scatter_dimension=1, tiled=True
            ).astype(jnp.float32),
            lax.psum_scatter(
                tiled[0].astype(jnp.bfloat16), "head", scatter_dimension=0, tiled=True
            ).astype(jnp.float32),
            lax.psum_scatter(
                tiled[1].astype(jnp.bfloat16), "head", scatter_dimension=0, tiled=True
            ).astype(jnp.float32),
            lax.psum_scatter(
                tiled[2].astype(jnp.bfloat16), "head", scatter_dimension=0, tiled=True
            ).astype(jnp.float32),
            lax.psum_scatter(
                tiled[3].astype(jnp.bfloat16), "head", scatter_dimension=0, tiled=True
            ).astype(jnp.float32),
            lax.psum_scatter(
                tiled[4].astype(jnp.bfloat16), "head", scatter_dimension=0, tiled=True
            ).astype(jnp.float32),
            lax.psum_scatter(
                tiled[5].astype(jnp.bfloat16), "head", scatter_dimension=0, tiled=True
            ).astype(jnp.float32),
            lax.psum_scatter(
                tiled[6].astype(jnp.bfloat16), "head", scatter_dimension=0, tiled=True
            ).astype(jnp.float32),
            lax.psum_scatter(
                tiled[7].astype(jnp.bfloat16), "head", scatter_dimension=0, tiled=True
            ).astype(jnp.float32),
            lax.psum_scatter(
                tiled[8].astype(jnp.bfloat16), "head", scatter_dimension=0, tiled=True
            ).astype(jnp.float32),
        )

    def one_micro(weights, micro):
        full_qkv, full_out, full_up, full_down = (weights[0], weights[1], weights[2], weights[3])
        vectors = [member.astype(jnp.float32) for member in weights[4:]]
        (
            bias_query,
            bias_value,
            bias_out,
            gain_attn,
            shift_attn,
            bias_up,
            bias_down,
            gain_ffn,
            shift_ffn,
        ) = vectors
        inputs = tokens[micro]
        proj = jnp.dot(inputs, full_qkv, preferred_element_type=jnp.float32)
        queries = (proj[:, 0:width] + bias_query).astype(jnp.bfloat16)
        keys = proj[:, width : 2 * width].astype(jnp.bfloat16)
        values = (proj[:, 2 * width : 3 * width] + bias_value).astype(jnp.bfloat16)
        q_heads, k_heads, v_heads = (
            lax.all_to_all(queries, "head", split_axis=1, concat_axis=0, tiled=True),
            lax.all_to_all(keys, "head", split_axis=1, concat_axis=0, tiled=True),
            lax.all_to_all(values, "head", split_axis=1, concat_axis=0, tiled=True),
        )
        perm_row = cluster_perm[micro]
        seq_ends = jnp.cumsum(seq_lengths[micro])
        own_slots = lax.dynamic_slice_in_dim(perm_row, blk_index * group_rows, group_rows)
        send_order = jnp.argsort(own_slots)
        send_inverse = jnp.argsort(send_order)
        slot_owner = (
            jnp.zeros((total_rows,), jnp.int32)
            .at[perm_row]
            .set(jnp.arange(total_rows, dtype=jnp.int32))
        )
        slot_pos = lax.dynamic_slice_in_dim(slot_owner, blk_index * group_rows, group_rows)
        recv_order = jnp.argsort(slot_pos // group_rows, stable=True)
        recv_inverse = jnp.argsort(recv_order)
        slot_segs = segment_of(slot_pos, seq_ends).reshape(clusters_here, CLUSTER)
        allowed = slot_segs[:, :, None] == slot_segs[:, None, :]
        got_q, got_k, got_v = (
            lax.all_to_all(q_heads[send_order], "blk", split_axis=0, concat_axis=0, tiled=True),
            lax.all_to_all(k_heads[send_order], "blk", split_axis=0, concat_axis=0, tiled=True),
            lax.all_to_all(v_heads[send_order], "blk", split_axis=0, concat_axis=0, tiled=True),
        )
        cluster_q = got_q[recv_inverse].reshape(cluster_shape)
        cluster_k = got_k[recv_inverse].reshape(cluster_shape)
        cluster_v = got_v[recv_inverse].reshape(cluster_shape)
        masked = cluster_scores(cluster_q, cluster_k, allowed)
        probs = jax.nn.softmax(masked, axis=-1)
        lse = jax.nn.logsumexp(masked, axis=-1)
        context_slot = (
            jnp.einsum(
                "chqk,ckhd->cqhd",
                probs.astype(jnp.bfloat16),
                cluster_v,
                preferred_element_type=jnp.float32,
            )
            .astype(jnp.bfloat16)
            .reshape(flat_shape)
        )
        returned = lax.all_to_all(
            context_slot[recv_order], "blk", split_axis=0, concat_axis=0, tiled=True
        )
        context_low = returned[send_inverse]
        context_rows = lax.all_to_all(context_low, "head", split_axis=0, concat_axis=1, tiled=True)
        attn_res = (
            inputs.astype(jnp.float32)
            + jnp.dot(context_rows, full_out, preferred_element_type=jnp.float32)
            + bias_out
        )
        normed, norm_back_attn = jax.vjp(layer_norm, attn_res, gain_attn, shift_attn)
        hidden_in = normed.astype(jnp.bfloat16)
        pre_act = jnp.dot(hidden_in, full_up, preferred_element_type=jnp.float32) + bias_up
        active_full, gelu_back = jax.vjp(gelu_exact, pre_act)
        active = active_full.astype(jnp.bfloat16)
        ffn_res = (
            normed + jnp.dot(active, full_down, preferred_element_type=jnp.float32) + bias_down
        )
        result, norm_back_ffn = jax.vjp(layer_norm, ffn_res, gain_ffn, shift_ffn)
        d_ffn, grad_gain_ffn, grad_shift_ffn = norm_back_ffn(out_grad[micro].astype(jnp.float32))
        g_down = d_ffn.astype(jnp.bfloat16)
        grad_down = jnp.einsum("tf,td->fd", active, g_down, preferred_element_type=jnp.float32)
        grad_bias_down = jnp.sum(g_down.astype(jnp.float32), axis=0)
        d_active = jnp.einsum("td,fd->tf", g_down, full_down, preferred_element_type=jnp.float32)
        (d_pre,) = gelu_back(d_active)
        g_pre = d_pre.astype(jnp.bfloat16)
        grad_up = jnp.einsum("td,tf->df", hidden_in, g_pre, preferred_element_type=jnp.float32)
        grad_bias_up = jnp.sum(g_pre.astype(jnp.float32), axis=0)
        d_normed = d_ffn + jnp.einsum(
            "tf,df->td", g_pre, full_up, preferred_element_type=jnp.float32
        )
        d_attn, grad_gain_attn, grad_shift_attn = norm_back_attn(d_normed)
        g_attn = d_attn.astype(jnp.bfloat16)
        grad_out = jnp.einsum("tc,td->cd", context_rows, g_attn, preferred_element_type=jnp.float32)
        grad_bias_out = jnp.sum(g_attn.astype(jnp.float32), axis=0)
        g_context = jnp.einsum(
            "td,cd->tc", g_attn, full_out, preferred_element_type=jnp.float32
        ).astype(jnp.bfloat16)
        dout_heads = lax.all_to_all(g_context, "head", split_axis=1, concat_axis=0, tiled=True)
        got_dout = lax.all_to_all(
            dout_heads[send_order], "blk", split_axis=0, concat_axis=0, tiled=True
        )
        cluster_dout = got_dout[recv_inverse].reshape(cluster_shape)
        again = cluster_scores(cluster_q, cluster_k, allowed)
        probs_back = jnp.where(allowed[:, None], jnp.exp(again - lse[:, :, :, None]), 0.0)
        dprob = jnp.einsum(
            "cqhd,ckhd->chqk", cluster_dout, cluster_v, preferred_element_type=jnp.float32
        )
        delta = jnp.sum(probs_back * dprob, axis=-1, keepdims=True)
        dscore = (probs_back * (dprob - delta)).astype(jnp.bfloat16)
        grad_q = (
            (
                jnp.einsum("chqk,ckhd->cqhd", dscore, cluster_k, preferred_element_type=jnp.float32)
                * 0.125
            )
            .astype(jnp.bfloat16)
            .reshape(flat_shape)
        )
        grad_k = (
            (
                jnp.einsum("chqk,cqhd->ckhd", dscore, cluster_q, preferred_element_type=jnp.float32)
                * 0.125
            )
            .astype(jnp.bfloat16)
            .reshape(flat_shape)
        )
        grad_v = (
            jnp.einsum(
                "chqk,cqhd->ckhd",
                probs_back.astype(jnp.bfloat16),
                cluster_dout,
                preferred_element_type=jnp.float32,
            )
            .astype(jnp.bfloat16)
            .reshape(flat_shape)
        )
        back_q, back_k, back_v = (
            lax.all_to_all(grad_q[recv_order], "blk", split_axis=0, concat_axis=0, tiled=True),
            lax.all_to_all(grad_k[recv_order], "blk", split_axis=0, concat_axis=0, tiled=True),
            lax.all_to_all(grad_v[recv_order], "blk", split_axis=0, concat_axis=0, tiled=True),
        )
        rows_q, rows_k, rows_v = (
            lax.all_to_all(back_q[send_inverse], "head", split_axis=0, concat_axis=1, tiled=True),
            lax.all_to_all(back_k[send_inverse], "head", split_axis=0, concat_axis=1, tiled=True),
            lax.all_to_all(back_v[send_inverse], "head", split_axis=0, concat_axis=1, tiled=True),
        )
        g_proj = jnp.concatenate([rows_q, rows_k, rows_v], axis=1)
        grad_qkv = jnp.einsum("td,tc->dc", inputs, g_proj, preferred_element_type=jnp.float32)
        grad_bias_query = jnp.sum(rows_q.astype(jnp.float32), axis=0)
        grad_bias_value = jnp.sum(rows_v.astype(jnp.float32), axis=0)
        input_grad = d_attn + jnp.einsum(
            "tc,dc->td", g_proj, full_qkv, preferred_element_type=jnp.float32
        )
        full = (
            grad_qkv,
            grad_out,
            grad_up,
            grad_down,
            grad_bias_query,
            grad_bias_value,
            grad_bias_out,
            grad_gain_attn,
            grad_shift_attn,
            grad_bias_up,
            grad_bias_down,
            grad_gain_ffn,
            grad_shift_ffn,
        )
        return (result.astype(jnp.bfloat16), input_grad, full)

    outputs = []
    input_grads = []
    shards = None
    for micro in range(micro_count):
        weights = (
            lax.all_gather(
                lax.all_gather(qkv_weight, "head", axis=1, tiled=True), "blk", axis=0, tiled=True
            ),
            lax.all_gather(
                lax.all_gather(out_weight, "head", axis=1, tiled=True), "blk", axis=0, tiled=True
            ),
            lax.all_gather(
                lax.all_gather(up_weight, "head", axis=1, tiled=True), "blk", axis=0, tiled=True
            ),
            lax.all_gather(
                lax.all_gather(down_weight, "head", axis=1, tiled=True), "blk", axis=0, tiled=True
            ),
            lax.all_gather(query_bias, "blk", axis=0, tiled=True),
            lax.all_gather(value_bias, "blk", axis=0, tiled=True),
            lax.all_gather(out_bias, "blk", axis=0, tiled=True),
            lax.all_gather(attn_gain, "blk", axis=0, tiled=True),
            lax.all_gather(attn_shift, "blk", axis=0, tiled=True),
            lax.all_gather(up_bias, "blk", axis=0, tiled=True),
            lax.all_gather(down_bias, "blk", axis=0, tiled=True),
            lax.all_gather(ffn_gain, "blk", axis=0, tiled=True),
            lax.all_gather(ffn_shift, "blk", axis=0, tiled=True),
        )
        result, input_grad, full = one_micro(weights, micro)
        outputs.append(result)
        input_grads.append(input_grad)
        reduced = reduce_grads(full)
        shards = (
            reduced
            if shards is None
            else tuple((earlier + later for earlier, later in zip(shards, reduced)))
        )
    return (
        jnp.stack(outputs),
        jnp.stack(input_grads),
        shards[0],
        shards[4],
        shards[5],
        shards[1],
        shards[6],
        shards[7],
        shards[8],
        shards[2],
        shards[9],
        shards[3],
        shards[10],
        shards[11],
        shards[12],
    )


def solution(mesh):
    return jax.shard_map(
        body,
        mesh=mesh,
        in_specs=(
            P(None, ("blk", "head"), None),
            P(),
            P(),
            P(None, ("blk", "head"), None),
            P("blk", "head"),
            P("blk"),
            P("blk"),
            P("blk", "head"),
            P("blk"),
            P("blk"),
            P("blk"),
            P("blk", "head"),
            P("blk"),
            P("blk", "head"),
            P("blk"),
            P("blk"),
            P("blk"),
        ),
        out_specs=(
            P(None, ("blk", "head"), None),
            P(None, ("blk", "head"), None),
            P("blk", "head"),
            P("blk"),
            P("blk"),
            P("blk", "head"),
            P("blk"),
            P("blk"),
            P("blk"),
            P("blk", "head"),
            P("blk"),
            P("blk", "head"),
            P("blk"),
            P("blk"),
            P("blk"),
        ),
        check_vma=False,
    )
```

profile of v0, /device:TPU:8, one launch (start us, length us, event | category | flops | bytes accessed | tf_op | source)
XLA Modules:
  0.0 1367.3 jit_solution(16341263764255371883)
XLA Ops:
  7.3 16.5 %all-gather = bf16[4,576,96]{1,2,0:T(8,128)(2,1)S(1)} all-gather(bf16[1,576,96]{1,2,0:T(8,128)(2,1)} %bitcast.456), channel_id=1, replica_groups=mesh['blk'=8,'head'=4] {'head'}, dimensions={0}, use_global_device_ids=true | all-gather | bytes 552960 | tf_op jit(solution)/shard_map/all_gather | solution.py:300
  26.2 14.2 %all_gather.72 = bf16[96,768]{0,1:T(8,128)(2,1)S(1)} all-gather(bf16[96,192]{0,1:T(8,128)(2,1)S(1)} %copy.383), channel_id=1, replica_groups=mesh['blk'=8,'head'=4] {'head'}, dimensions={1}, use_global_device_ids=true | all-gather | bytes 184320 | tf_op jit(solution)/shard_map/all_gather | solution.py:303
  41.3 16.4 %all_gather.77 = bf16[96,3072]{1,0:T(8,128)(2,1)} all-gather(bf16[96,768]{1,0:T(8,128)(2,1)S(1)} %copy-done.62), channel_id=1, replica_groups=mesh['blk'=8,'head'=4] {'head'}, dimensions={1}, use_global_device_ids=true | all-gather | bytes 737280 | tf_op jit(solution)/shard_map/all_gather | solution.py:306
  60.9 23.0 %all-reduce.45 = (bf16[768]{0:T(1024)(128)(2,1)S(1)}, bf16[768]{0:T(1024)(128)(2,1)S(1)}, bf16[768]{0:T(1024)(128)(2,1)}, bf16[768]{0:T(1024)(128)(2,1)}, bf16[7...) all-reduce(bf16[768]{0:T(1024)(128)(2,1)S(1)} %dynamic-update-slice, ...), channel_id=1, replica_groups=mesh['blk'=8,'head'=4] {'blk'}, use_global_device_ids=true, to_apply=%add.1 | all-reduce | flops 6144 | bytes 24576
  180.0 17.2 %all_gather.80 = bf16[384,768]{0,1:T(8,128)(2,1)} all-gather(bf16[384,192]{0,1:T(8,128)(2,1)S(1)} %copy-done.63), channel_id=1, replica_groups=mesh['blk'=8,'head'=4] {'head'}, dimensions={1}, use_global_device_ids=true | all-gather | bytes 737280 | tf_op jit(solution)/shard_map/all_gather | solution.py:309
  212.0 30.7 %scatter_custom_fusion = s32[8192]{0:T(1024)S(1)} fusion(s32[8192]{0:T(1024)S(1)} %bitcast.462, s32[8192]{0:T(1024)S(1)} %iota.33, s32[]{:T(128)} %constant.46.clone.1), kind=kCustom, calls=%fused_computation.248 | custom fusion | bytes 32772 | tf_op jit(solution)/shard_map/scatter | solution.py:156
  242.8 30.5 %scatter_custom_fusion.1 = s32[8192]{0:T(1024)S(1)} fusion(s32[8192]{0:T(1024)S(1)} %bitcast.461, s32[8192]{0:T(1024)S(1)} %iota.38, s32[]{:T(128)} %constant.46.clone.1), kind=kCustom, calls=%fused_computation.246 | custom fusion | bytes 32772 | tf_op jit(solution)/shard_map/scatter | solution.py:156
  346.8 15.1 %all-to-all-start.9 = ((bf16[8,128,192]{1,2,0:T(8,128)(2,1)}), bf16[8,128,192]{1,2,0:T(8,128)(2,1)S(1)}, u32[]{:S(2)}, u32[]{:S(2)}) async-start(bf16[8,128,192]{1,2,0:T(8,128)(2,1)} %copy.387), calls=%async_computation.9 | async-start | bytes 786432 | tf_op jit(solution)/shard_map/all_to_all | solution.py:166
  628.4 12.5 all_to_all.496
  768.8 13.6 all_to_all.498
  830.9 31.8 %reduce-scatter.49.cloned.1.call-done = f32[96,2304]{1,0:T(8,128)} async-done(((f32[768,2304]{1,0:T(8,128)}), f32[96,2304]{1,0:T(8,128)}) %reduce-scatter.49.cloned.1.call-update) | async-done | bytes 884752
  865.1 77.7 %reduce-scatter.47.cloned.1.call-done = f32[384,768]{1,0:T(8,128)} async-done(((f32[3072,768]{1,0:T(8,128)}), f32[384,768]{1,0:T(8,128)}) %reduce-scatter.47.cloned.1.call-update) | async-done | bytes 1179664 | tf_op jit(solution)/shard_map/reduce_scatter | solution.py:70
  945.2 77.4 %reduce-scatter.45.cloned.1.call-done = f32[384,768]{1,0:T(8,128)} async-done(((f32[3072,768]{1,0:T(8,128)}), f32[384,768]{1,0:T(8,128)}) %reduce-scatter.45.cloned.1.call-update) | async-done | bytes 1179664 | tf_op jit(solution)/shard_map/reduce_scatter | solution.py:70
  1044.3 26.1 %all-reduce.44 = (bf16[768]{0:T(1024)(128)(2,1)}, bf16[768]{0:T(1024)(128)(2,1)}, bf16[768]{0:T(1024)(128)(2,1)}, bf16[768]{0:T(1024)(128)(2,1)}, bf16[768]{0:T(...) all-reduce(f32[768]{0:T(1024)} %reduce_sum.477, ...), channel_id=8, replica_groups=mesh['blk'=8,'head'=4] {'blk'}, use_global_device_ids=true, to_apply=%region_46.47.clone | all-reduce | flops 18432 | bytes 110592
  1095.2 16.7 %all-reduce.46 = (bf16[384]{0:T(512)(128)(2,1)}, bf16[384]{0:T(512)(128)(2,1)}, bf16[384]{0:T(512)(128)(2,1)}, bf16[384]{0:T(512)(128)(2,1)}, bf16[384]{0:T(512)...) all-reduce(bf16[384]{0:T(512)(128)(2,1)S(1)} %convert_element_type., ...), channel_id=9, replica_groups=mesh['blk'=8,'head'=4] {'head'}, use_global_device_ids=true, to_apply=%region_47.48.clone | all-reduce | flops 9216 | bytes 36864
  1129.5 54.1 %reduce-scatter.37.cloned.1.call-done = f32[96,3072]{1,0:T(8,128)} async-done(((f32[768,3072]{1,0:T(8,128)}), f32[96,3072]{1,0:T(8,128)}) %reduce-scatter.37.cloned.1.call-update) | async-done | bytes 1179664 | tf_op jit(solution)/shard_map/reduce_scatter | solution.py:69
  1189.7 13.2 reduce-scatter.55.cloned.1.call-done
  1203.8 19.4 %reduce-scatter.53.cloned.1.call-done = bf16[192,96]{1,0:T(8,128)(2,1)} async-done(((bf16[768,96]{1,0:T(8,128)(2,1)}), bf16[192,96]{1,0:T(8,128)(2,1)}) %reduce-scatter.53.cloned.1.call-update) | async-done | bytes 36880
  1224.8 21.0 %reduce-scatter.31.cloned.1.call-done = bf16[96,576]{0,1:T(8,128)(2,1)} async-done(((bf16[96,2304]{0,1:T(8,128)(2,1)}), bf16[96,576]{0,1:T(8,128)(2,1)}) %reduce-scatter.31.cloned.1.call-update) | async-done | bytes 110608 | tf_op jit(solution)/shard_map/reduce_scatter | solution.py:83
  1245.8 22.5 %reduce-scatter.29.cloned.1.call-done = bf16[96,576]{0,1:T(8,128)(2,1)} async-done(((bf16[96,2304]{0,1:T(8,128)(2,1)}), bf16[96,576]{0,1:T(8,128)(2,1)}) %reduce-scatter.29.cloned.1.call-update) | async-done | bytes 110608 | tf_op jit(solution)/shard_map/reduce_scatter | solution.py:83
  1270.2 20.7 %reduce-scatter.59.cloned.1.call-done = bf16[192,384]{1,0:T(8,128)(2,1)} async-done(((bf16[768,384]{1,0:T(8,128)(2,1)}), bf16[192,384]{1,0:T(8,128)(2,1)}) %reduce-scatter.59.cloned.1.call-update) | async-done | bytes 147472
  1291.9 21.5 %reduce-scatter.57.cloned.1.call-done = bf16[192,384]{1,0:T(8,128)(2,1)} async-done(((bf16[768,384]{1,0:T(8,128)(2,1)}), bf16[192,384]{1,0:T(8,128)(2,1)}) %reduce-scatter.57.cloned.1.call-update) | async-done | bytes 147472
  1315.3 20.7 %reduce-scatter.43.cloned.1.call-done = bf16[96,768]{1,0:T(8,128)(2,1)} async-done(((bf16[96,3072]{1,0:T(8,128)(2,1)}), bf16[96,768]{1,0:T(8,128)(2,1)}) %reduce-scatter.43.cloned.1.call-update) | async-done | bytes 147472 | tf_op jit(solution)/shard_map/reduce_scatter | solution.py:89
  1336.0 22.5 %reduce-scatter.39.cloned.1.call-done = bf16[96,768]{1,0:T(8,128)(2,1)} async-done(((bf16[96,3072]{1,0:T(8,128)(2,1)}), bf16[96,768]{1,0:T(8,128)(2,1)}) %reduce-scatter.39.cloned.1.call-update) | async-done | bytes 147472 | tf_op jit(solution)/shard_map/reduce_scatter | solution.py:89
  (723 shorter events, 712.1 us)
Async XLA Ops:
  7.3 76.6 %all-gather.7.cloned.1.call-start = ((), (), s32[]{:S(2)}) async-start(), calls=%async_computation.48 | async-start | bytes 3981312 | tf_op jit(solution)/shard_map/all_gather | solution.py:299
  25.2 419.6 %all-gather.9.cloned.1.call-start = ((), (), s32[]{:S(2)}) async-start(), calls=%async_computation.49 | async-start | bytes 1327104 | tf_op jit(solution)/shard_map/all_gather | solution.py:302
  41.2 415.7 %all-gather.11.cloned.1.call-start = ((), (), s32[]{:S(2)}) async-start(), calls=%async_computation.50 | async-start | bytes 5308416 | tf_op jit(solution)/shard_map/all_gather | solution.py:305
  175.2 32.5 %all-to-all-start.13 = ((bf16[8,128,192]{1,2,0:T(8,128)(2,1)}), bf16[8,128,192]{1,2,0:T(8,128)(2,1)S(1)}, u32[]{:S(2)}, u32[]{:S(2)}) async-start(bf16[8,128,192]{1,2,0:T(8,128)(2,1)} %copy.397), calls=%async_computation.13 | async-start | bytes 786432 | tf_op jit(solution)/shard_map/all_to_all | solution.py:165
  179.9 289.1 %all-gather.13.cloned.1.call-start = ((), (), s32[]{:S(2)}) async-start(), calls=%async_computation.51 | async-start | bytes 5308416 | tf_op jit(solution)/shard_map/all_gather | solution.py:308
  207.7 83.8 %all-to-all-start.5 = ((bf16[8,128,192]{1,2,0:T(8,128)(2,1)}), bf16[8,128,192]{1,2,0:T(8,128)(2,1)}, u32[]{:S(2)}, u32[]{:S(2)}) async-start(bf16[8,128,192]{1,2,0:T(8,128)(2,1)} %copy.371), calls=%async_computation.5 | async-start | bytes 786432 | tf_op jit(solution)/shard_map/all_to_all | solution.py:165
  346.8 30.4 %all-to-all-start.9 = ((bf16[8,128,192]{1,2,0:T(8,128)(2,1)}), bf16[8,128,192]{1,2,0:T(8,128)(2,1)S(1)}, u32[]{:S(2)}, u32[]{:S(2)}) async-start(bf16[8,128,192]{1,2,0:T(8,128)(2,1)} %copy.387), calls=%async_computation.9 | async-start | bytes 786432 | tf_op jit(solution)/shard_map/all_to_all | solution.py:166
  410.4 29.4 %all-to-all-start.7 = ((bf16[4,256,192]{1,2,0:T(8,128)(2,1)}), bf16[4,256,192]{1,2,0:T(8,128)(2,1)S(1)}, u32[]{:S(2)}, u32[]{:S(2)}) async-start(bf16[4,256,192]{1,2,0:T(8,128)(2,1)} %copy.382), calls=%async_computation.7 | async-start | bytes 786432 | tf_op jit(solution)/shard_map/all_to_all | solution.py:188
  444.9 380.0 %reduce-scatter.35.cloned.1.call-start = ((), (), s32[]{:S(2)}) async-start(), calls=%async_computation.55 | async-start | bytes 2654208 | tf_op jit(solution)/shard_map/reduce_scatter | solution.py:68
  531.2 295.6 %reduce-scatter.33.cloned.1.call-start = ((), (), s32[]{:S(2)}) async-start(), calls=%async_computation.54 | async-start | bytes 2654208 | tf_op jit(solution)/shard_map/reduce_scatter | solution.py:68
  620.9 207.7 %reduce-scatter.51.cloned.1.call-start = ((), (), s32[]{:S(2)}) async-start(), calls=%async_computation.63 | async-start | bytes 7962624
  761.4 101.3 %reduce-scatter.49.cloned.1.call-start = ((), (), s32[]{:S(2)}) async-start(), calls=%async_computation.62 | async-start | bytes 7962624
  795.2 147.5 %reduce-scatter.47.cloned.1.call-start = ((), (), s32[]{:S(2)}) async-start(), calls=%async_computation.61 | async-start | bytes 10616832 | tf_op jit(solution)/shard_map/reduce_scatter | solution.py:70
  801.8 220.8 %reduce-scatter.45.cloned.1.call-start = ((), (), s32[]{:S(2)}) async-start(), calls=%async_computation.60 | async-start | bytes 10616832 | tf_op jit(solution)/shard_map/reduce_scatter | solution.py:70
  810.0 304.4 %reduce-scatter.41.cloned.1.call-start = ((), (), s32[]{:S(2)}) async-start(), calls=%async_computation.58 | async-start | bytes 10616832 | tf_op jit(solution)/shard_map/reduce_scatter | solution.py:69
  817.3 366.3 %reduce-scatter.37.cloned.1.call-start = ((), (), s32[]{:S(2)}) async-start(), calls=%async_computation.56 | async-start | bytes 10616832 | tf_op jit(solution)/shard_map/reduce_scatter | solution.py:69
  824.8 378.2 %reduce-scatter.55.cloned.1.call-start = ((), (), s32[]{:S(2)}) async-start(), calls=%async_computation.65 | async-start | bytes 245760
  826.7 396.6 %reduce-scatter.53.cloned.1.call-start = ((), (), s32[]{:S(2)}) async-start(), calls=%async_computation.64 | async-start | bytes 245760
  828.6 417.2 %reduce-scatter.31.cloned.1.call-start = ((), (), s32[]{:S(2)}) async-start(), calls=%async_computation.53 | async-start | bytes 737280 | tf_op jit(solution)/shard_map/reduce_scatter | solution.py:83
  830.9 437.4 %reduce-scatter.29.cloned.1.call-start = ((), (), s32[]{:S(2)}) async-start(), calls=%async_computation.52 | async-start | bytes 737280 | tf_op jit(solution)/shard_map/reduce_scatter | solution.py:83
  865.1 425.8 %reduce-scatter.59.cloned.1.call-start = ((), (), s32[]{:S(2)}) async-start(), calls=%async_computation.67 | async-start | bytes 737280
  945.2 368.1 %reduce-scatter.57.cloned.1.call-start = ((), (), s32[]{:S(2)}) async-start(), calls=%async_computation.66 | async-start | bytes 737280
  1025.1 310.9 %reduce-scatter.43.cloned.1.call-start = ((), (), s32[]{:S(2)}) async-start(), calls=%async_computation.59 | async-start | bytes 737280 | tf_op jit(solution)/shard_map/reduce_scatter | solution.py:89
  1116.9 241.6 %reduce-scatter.39.cloned.1.call-start = ((), (), s32[]{:S(2)}) async-start(), calls=%async_computation.57 | async-start | bytes 737280 | tf_op jit(solution)/shard_map/reduce_scatter | solution.py:89
  (148 other events, 2952.5 us)
Sparse Core Ops, SparseCore 0:
  25.4 35.1 all-gather.6
  63.0 24.0 all-gather.8
  89.0 38.8 all-gather.10
  197.4 44.6 all-gather.12
  505.1 45.5 reduce-scatter.34
  554.2 42.4 reduce-scatter.32
  654.3 76.1 reduce-scatter.50
  795.3 67.3 reduce-scatter.48
  866.3 76.4 reduce-scatter.46
  946.1 76.4 reduce-scatter.44
  1026.1 77.5 reduce-scatter.40
  1107.1 76.4 reduce-scatter.36
  1186.4 16.4 reduce-scatter.54
  1205.7 17.5 reduce-scatter.52
  1225.4 20.3 reduce-scatter.30
  1247.9 20.3 reduce-scatter.28
  1270.4 20.3 reduce-scatter.58
  1293.0 20.3 reduce-scatter.56
  1315.6 20.3 reduce-scatter.42
  1338.1 20.3 reduce-scatter.38
where the time goes:
time: 1380 us; the launch traced here: 1370 us
  waiting for transfers between devices  489 us (35%)
  local copies, waits for them, and re-layouts  331 us (24%)
  blocking collectives  177 us (13%)
  starting transfers between devices  152 us (11%)
  matrix products  103 us (7%)
  other arithmetic  94.9 us (7%)
  between operations  20.3 us (1%)
    reduce_scatter x2, waiting for transfers between devices, reduce_grads(): lax.psum_scatter(full[3], 'blk', scatter_dimension=0, tiled=True)  155 us
    unnamed x26, waiting for transfers between devices  107 us
    unnamed x315, local copies, waits for them, and re-layouts  66.7 us
    unnamed x3, blocking collectives  65.8 us
    scatter x2, local copies, waits for them, and re-layouts, one_micro(): slot_owner = jnp.zeros((total_rows,), jnp.int32).at[perm_row].set(jnp.ara...  61.2 us
    reduce_scatter x2, waiting for transfers between devices, reduce_grads(): lax.psum_scatter(full[2], 'blk', scatter_dimension=0, tiled=True)  54.1 us
    reduce_scatter x2, waiting for transfers between devices, reduce_grads(): lax.psum_scatter(rows[0].astype(jnp.bfloat16), 'head', scatter_dimension=...  43.5 us
    reduce_scatter x2, waiting for transfers between devices, reduce_grads(): lax.psum_scatter(rows[2].astype(jnp.bfloat16), 'head', scatter_dimension=...  43.2 us
  transfers between devices with their start and end apart: 49, of which 31 were waited for; matrix products, arithmetic and copies ran while one was open for 35% of the time, Pallas kernels for 0%

commit v1 on v0

v1 whole, which is shorter than its diff:
```python
import functools

import jax
import jax.numpy as jnp
from jax import lax
from jax.experimental import pallas as pl
from jax.experimental.pallas import tpu as pltpu
from jax.sharding import PartitionSpec as P

HEAD_DIM = 64
CLUSTER = 128
MESH = pl.DeviceIdType.MESH
BF16 = jnp.bfloat16
F32 = jnp.float32

masked_score = -1e30
norm_epsilon = 1e-05


def bits_of(index, count):
    return [(index // (1 << i)) % 2 for i in range(count)]


def flip(index, mask, bits):
    for i, bit in enumerate(bits):
        if mask & (1 << i):
            index = index + (1 - 2 * bit) * (1 << i)
    return index


def submasks(dims):
    masks = [0]
    for dim in dims:
        masks = masks + [mask | (1 << dim) for mask in masks]
    return masks


def choose(index, values):
    result = values[-1]
    for position in range(len(values) - 2, -1, -1):
        result = jnp.where(index == position, values[position], result)
    return result


class Sends:
    def __init__(self):
        self.pending = []

    def start(self, make, when=None):
        if when is None:
            make().start()
        else:

            @pl.when(when)
            def _():
                make().start()

        self.pending.append((make, when))

    def finish(self):
        for make, when in self.pending:
            if when is None:
                make().wait_send()
            else:

                @pl.when(when)
                def _(make=make):
                    make().wait_send()


def remote(src, dst, send_sem, recv_sem, device):
    return pltpu.make_async_remote_copy(
        src_ref=src,
        dst_ref=dst,
        send_sem=send_sem,
        recv_sem=recv_sem,
        device_id=device,
        device_id_type=MESH,
    )


def enter(blk, head, blks, heads):
    barrier = pltpu.get_barrier_semaphore()
    for other in range(blks):

        @pl.when(other != blk)
        def _():
            pl.semaphore_signal(barrier, inc=1, device_id=(other, head), device_id_type=MESH)

    for other in range(heads):

        @pl.when(other != head)
        def _():
            pl.semaphore_signal(barrier, inc=1, device_id=(blk, other), device_id_type=MESH)

    pl.semaphore_wait(barrier, blks + heads - 2)


def iota(shape, dim):
    return lax.broadcasted_iota(jnp.int32, shape, dim)


def permute_rows(one_hot_tile, source, target, rows):
    @pl.loop(0, rows // CLUSTER)
    def _(tile):
        start = pl.multiple_of(tile * CLUSTER, CLUSTER)
        chosen = jnp.dot(one_hot_tile(start), source[...], preferred_element_type=F32)
        target[pl.ds(start, CLUSTER), :] = chosen.astype(BF16)


def one_hot_from_row(row_ref):
    def tile(start):
        row = row_ref[0:1, :]
        count = row.shape[1]
        return jnp.where(iota((CLUSTER, count), 0) + start == row, 1.0, 0.0).astype(BF16)

    return tile


def one_hot_from_column(column_ref, count):
    def tile(start):
        column = column_ref[pl.ds(start, CLUSTER), 0:1]
        return jnp.where(iota((CLUSTER, count), 1) == column, 1.0, 0.0).astype(BF16)

    return tile


class RowExchange:
    def __init__(self, sends, blk, head, blks, heads, sems, tensor):
        self.sends, self.blk, self.head, self.blks, self.heads = sends, blk, head, blks, heads
        self.head_send, self.head_recv, self.blk_send, self.blk_recv, self.local = sems
        self.tensor = tensor

    def over_head(self, step, source, target):
        for other in range(self.heads):
            make = lambda other=other: remote(
                source(other),
                target(self.head),
                self.head_send.at[self.tensor, step, other],
                self.head_recv.at[self.tensor, step, self.head],
                (self.blk, other),
            )
            self.sends.start(make, when=other != self.head)

            @pl.when(other == self.head)
            def _():
                pltpu.make_async_copy(
                    source(other), target(other), self.local.at[self.tensor, step]
                ).start()

    def wait_head(self, step, target):
        for other in range(self.heads):

            @pl.when(other != self.head)
            def _():
                remote(
                    target(other),
                    target(other),
                    self.head_send.at[self.tensor, step, other],
                    self.head_recv.at[self.tensor, step, other],
                    (self.blk, other),
                ).wait_recv()

        pltpu.make_async_copy(
            target(self.head), target(self.head), self.local.at[self.tensor, step]
        ).wait()

    def over_blk(self, source, target):
        for other in range(self.blks):
            make = lambda other=other: remote(
                source(other),
                target(self.blk),
                self.blk_send.at[self.tensor, other],
                self.blk_recv.at[self.tensor, self.blk],
                (other, self.head),
            )
            self.sends.start(make, when=other != self.blk)

            @pl.when(other == self.blk)
            def _():
                pltpu.make_async_copy(
                    source(other), target(other), self.local.at[self.tensor, 2]
                ).start()

    def wait_blk(self, target):
        for other in range(self.blks):

            @pl.when(other != self.blk)
            def _():
                remote(
                    target(other),
                    target(other),
                    self.blk_send.at[self.tensor, other],
                    self.blk_recv.at[self.tensor, other],
                    (other, self.head),
                ).wait_recv()

        pltpu.make_async_copy(
            target(self.blk), target(self.blk), self.local.at[self.tensor, 2]
        ).wait()


def exchange_sems(blks, heads):
    dma = pltpu.SemaphoreType.DMA
    return [dma((2, 2, heads)), dma((2, 2, heads)), dma((2, blks)), dma((2, blks)), dma((2, 3))]


def cumulative(ones_ref, sums_ref, count):
    upper = jnp.where(iota((128, 128), 0) <= iota((128, 128), 1), 1.0, 0.0).astype(BF16)
    carry = jnp.zeros((ones_ref.shape[0], 1), F32)
    for tile in range(count // 128):
        part = ones_ref[:, tile * 128 : (tile + 1) * 128].astype(BF16)
        sums = jnp.dot(part, upper, preferred_element_type=F32) + carry
        sums_ref[:, tile * 128 : (tile + 1) * 128] = sums
        carry = sums[:, 127:128]


def gather_kernel(
    blks,
    heads,
    tokens,
    out_grad,
    shard,
    vectors,
    perm,
    full,
    full_vectors,
    slots_x,
    slots_g,
    dest_col,
    slot_col,
    arrived,
    sorted_rows,
    landed,
    ordered,
    dest_row,
    slot_row,
    ones,
    sums,
    rank_rows,
    head_send,
    head_recv,
    blk_send,
    blk_recv,
    local,
    z_send,
    z_recv,
    tree_send,
    tree_recv,
    vec_send,
    vec_recv,
    own_sem,
):
    blk, head = lax.axis_index("blk"), lax.axis_index("head")
    micros, rows, width = tokens.shape
    splits = heads // micros
    part = width // splits
    group = rows * heads
    pair = group // blks
    levels = blks.bit_length() - 1
    bits = bits_of(blk, levels)
    half = shard.shape[1] // 2
    sends = Sends()
    sems = (head_send, head_recv, blk_send, blk_recv, local)

    enter(blk, head, blks, heads)

    exchanges = [RowExchange(sends, blk, head, blks, heads, sems, i) for i in range(2)]
    sources = (tokens, out_grad)

    def send_rows(i):
        exchanges[i].over_head(
            0,
            lambda other: sources[i].at[
                other // splits, :, (other % splits) * part : (other % splits + 1) * part
            ],
            lambda other: arrived.at[i, pl.ds(pl.multiple_of(other * rows, rows), rows), :],
        )

    send_rows(0)

    def vec_copy(other):
        return remote(
            vectors, full_vectors.at[blk], vec_send.at[other], vec_recv.at[blk], (other, head)
        )

    for other in range(blks):
        sends.start(lambda other=other: vec_copy(other), when=other != blk)
    own_vec = pltpu.make_async_copy(vectors, full_vectors.at[blk], own_sem.at[0])
    own_vec.start()

    orders = [list(range(1, levels)) + [0], list(range(2, levels)) + [1, 0]]
    arrival = [
        choose(
            head,
            [
                sorted([x for x in range(heads) if x != own], key=lambda x: (abs(x - own), x))[j - 1]
                for own in range(heads)
            ],
        )
        if j
        else head
        for j in range(heads)
    ]

    def halves(ref, which):
        return ref.at[:, which * half : (which + 1) * half]

    def tree_step(j, step):
        for which in range(2):
            dims = orders[which]
            if step:
                tree_wait(j, which, step - 1)
            other = flip(blk, 1 << dims[step], bits)
            for mask in submasks(dims[:step]):
                piece = flip(blk, mask, bits)
                target = halves(full.at[arrival[j], piece], which)
                source = halves(shard, which) if j == 0 and mask == 0 else target
                slot = (1 << step) - 1 + submasks(dims[:step]).index(mask)
                make = lambda source=source, target=target, piece=piece, other=other, slot=slot, which=which: remote(
                    source,
                    target,
                    tree_send.at[j, which, slot],
                    tree_recv.at[j, which, piece],
                    (other, head),
                )
                sends.start(make)

    def tree_wait(j, which, step):
        dims = orders[which]
        other = flip(blk, 1 << dims[step], bits)
        for mask in submasks(dims[:step]):
            piece = flip(blk, mask | (1 << dims[step]), bits)
            target = halves(full.at[arrival[j], piece], which)
            remote(
                target,
                target,
                tree_send.at[j, which, 0],
                tree_recv.at[j, which, piece],
                (other, head),
            ).wait_recv()

    def chain(j):
        if j == 0:
            source = shard
            left, right = head > 0, head < heads - 1
        else:
            source = full.at[arrival[j], blk]
            left = (arrival[j] > head) & (head > 0)
            right = (arrival[j] < head) & (head < heads - 1)
            remote(
                source, source, z_send.at[0, 0], z_recv.at[arrival[j]], (blk, head)
            ).wait_recv()
        for side, (condition, step) in enumerate(((left, -1), (right, 1))):
            make = lambda source=source, side=side, step=step: remote(
                source,
                full.at[arrival[j], blk],
                z_send.at[j, side],
                z_recv.at[arrival[j]],
                (blk, jnp.clip(head + step, 0, heads - 1)),
            )
            sends.start(make, when=condition)

    tree_step(0, 0)
    chain(0)
    own_shard = pltpu.make_async_copy(shard, full.at[head, blk], own_sem.at[1])
    own_shard.start()
    send_rows(1)

    micro = head // splits
    own_slots = perm[micro, pl.ds(blk, 1), :]
    ones[...] = jnp.where(iota((blks, group), 0) == own_slots // group, 1.0, 0.0)
    cumulative(ones, sums, group)
    rank = jnp.sum(ones[...] * sums[...], axis=0, keepdims=True).astype(jnp.int32) - 1
    dest = own_slots // group * pair + rank
    dest_row[...] = jnp.broadcast_to(dest, dest_row.shape)
    for tile in range(group // 128):
        block = jnp.broadcast_to(dest[:, tile * 128 : (tile + 1) * 128].astype(F32), (128, 128))
        dest_col[tile * 128 : (tile + 1) * 128, :] = block.T.astype(jnp.int32)

    all_slots = perm[micro]
    ones[...] = jnp.where(all_slots // group == blk, 1.0, 0.0)
    cumulative(ones, sums, group)
    rank_rows[...] = jnp.where(ones[...] > 0, sums[...] - 1, -1.0).astype(jnp.int32)

    @pl.loop(0, blks)
    def _(other):
        ranks = rank_rows[pl.ds(other, 1), :]
        inner = (perm[micro, pl.ds(other, 1), :] % group).astype(F32)
        found = jnp.where(iota((pair, group), 0) == ranks, inner, 0.0)
        column = jnp.sum(found, axis=1, keepdims=True).astype(jnp.int32)
        slot_col[pl.ds(pl.multiple_of(other * pair, pair), pair), :] = jnp.broadcast_to(
            column, (pair, 128)
        )

    for tile in range(group // 128):
        block = slot_col[tile * 128 : (tile + 1) * 128, :].astype(F32)
        slot_row[:, tile * 128 : (tile + 1) * 128] = block.T[0:8, :].astype(jnp.int32)

    def to_groups(i):
        exchanges[i].wait_head(
            0, lambda other: arrived.at[i, pl.ds(pl.multiple_of(other * rows, rows), rows), :]
        )
        permute_rows(one_hot_from_row(dest_row), arrived.at[i], sorted_rows.at[i], group)
        exchanges[i].over_blk(
            lambda other: sorted_rows.at[i, pl.ds(other * pair, pair), :],
            lambda other: landed.at[i, pl.ds(pl.multiple_of(other * pair, pair), pair), :],
        )

    outs = (slots_x, slots_g)

    def to_slots(i):
        exchanges[i].wait_blk(
            lambda other: landed.at[i, pl.ds(pl.multiple_of(other * pair, pair), pair), :]
        )
        permute_rows(one_hot_from_row(slot_row), landed.at[i], ordered.at[i], group)
        exchanges[i].over_head(
            1,
            lambda other: ordered.at[i, pl.ds(other * rows, rows), :],
            lambda other: outs[i].at[other],
        )

    to_groups(0)
    for step in range(1, levels):
        tree_step(0, step)
    for j in range(1, heads):
        chain(j)
        tree_step(j, 0)
        if j == 1:
            to_slots(0)
            to_groups(1)
        if j == 2:
            to_slots(1)
        for step in range(1, levels):
            tree_step(j, step)
    for j in range(heads):
        for which in range(2):
            tree_wait(j, which, levels - 1)

    for i in range(2):
        exchanges[i].wait_head(1, lambda other: outs[i].at[other])
    for other in range(blks):

        @pl.when(other != blk)
        def _():
            remote(
                vectors,
                full_vectors.at[other],
                vec_send.at[other],
                vec_recv.at[other],
                (other, head),
            ).wait_recv()

    own_vec.wait()
    own_shard.wait()
    sends.finish()


def gather_all(blks, heads, tokens, out_grad, shard, vectors, perm):
    micros, rows, width = tokens.shape
    part = width * micros // heads
    group = rows * heads
    dma = pltpu.SemaphoreType.DMA
    any_space, vmem = pl.BlockSpec(memory_space=pl.ANY), pl.BlockSpec(memory_space=pltpu.VMEM)
    return pl.pallas_call(
        functools.partial(gather_kernel, blks, heads),
        name="gather_all",
        out_shape=(
            jax.ShapeDtypeStruct((heads, blks) + shard.shape, BF16),
            jax.ShapeDtypeStruct((blks,) + vectors.shape, BF16),
            jax.ShapeDtypeStruct((heads, rows, part), BF16),
            jax.ShapeDtypeStruct((heads, rows, part), BF16),
            jax.ShapeDtypeStruct((group, 128), jnp.int32),
            jax.ShapeDtypeStruct((group, 128), jnp.int32),
        ),
        in_specs=[any_space, any_space, any_space, any_space, vmem],
        out_specs=(any_space, any_space, any_space, any_space, vmem, vmem),
        scratch_shapes=[
            pltpu.VMEM((2, group, part), BF16),
            pltpu.VMEM((2, group, part), BF16),
            pltpu.VMEM((2, group, part), BF16),
            pltpu.VMEM((2, group, part), BF16),
            pltpu.VMEM((8, group), jnp.int32),
            pltpu.VMEM((8, group), jnp.int32),
            pltpu.VMEM((blks, group), F32),
            pltpu.VMEM((blks, group), F32),
            pltpu.VMEM((blks, group), jnp.int32),
        ]
        + exchange_sems(blks, heads)
        + [
            dma((heads, 2)),
            dma((heads,)),
            dma((heads, 2, blks)),
            dma((heads, 2, blks)),
            dma((blks,)),
            dma((blks,)),
            dma((2,)),
        ],
        compiler_params=pltpu.CompilerParams(
            collective_id=0, has_side_effects=True, vmem_limit_bytes=32 << 20
        ),
    )(tokens, out_grad, shard, vectors, perm)


def add_into(target, source, width):
    rows = target.shape[0]
    step = 16 if rows % 16 == 0 else rows

    @pl.loop(0, rows // step)
    def _(i):
        at = pl.ds(pl.multiple_of(i * step, step), step)
        for column in range(0, target.shape[1], width):
            cols = slice(column, column + width)
            target[at, cols] = (
                target[at, cols].astype(F32) + source[at, cols].astype(F32)
            ).astype(BF16)


def reduce_kernel(
    blks,
    heads,
    layer_out,
    x_grad,
    partial,
    vectors,
    dest_col,
    slot_col,
    out_rows,
    grad_rows,
    shard,
    vec_sum,
    total,
    from_core,
    from_tree,
    from_left,
    from_right,
    vec_parts,
    vec_mid,
    vec_heads,
    arrived,
    sorted_rows,
    landed,
    ordered,
    final,
    head_send,
    head_recv,
    blk_send,
    blk_recv,
    local,
    load_sem,
    core_send,
    core_recv,
    tree_send,
    tree_recv,
    left_send,
    left_recv,
    right_send,
    right_recv,
    vec_send,
    vec_recv,
    vec_head_send,
    vec_head_recv,
):
    blk, head = lax.axis_index("blk"), lax.axis_index("head")
    micros, rows, width = out_rows.shape
    splits = heads // micros
    part = width // splits
    group = rows * heads
    pair = group // blks
    levels = blks.bit_length() - 1
    bits = bits_of(blk, levels)
    half = shard.shape[1] // 2
    sends = Sends()
    sems = (head_send, head_recv, blk_send, blk_recv, local)
    exchanges = [RowExchange(sends, blk, head, blks, heads, sems, i) for i in range(2)]
    sources = (layer_out, x_grad)

    enter(blk, head, blks, heads)

    order = []
    for i in range(heads):
        order.append(heads - 1 - i // 2 if i % 2 == 0 else i // 2)

    even = submasks(range(1, levels))
    loads = {}
    for other in order:
        for mask in even:
            piece = flip(blk, mask, bits)
            loads[other, mask] = pltpu.make_async_copy(
                partial.at[other, piece], total.at[other, mask // 2], load_sem.at[other, mask // 2]
            )
            loads[other, mask].start()
            sends.start(
                lambda other=other, mask=mask: remote(
                    partial.at[other, flip(blk, mask | 1, bits)],
                    from_core.at[other, mask // 2],
                    core_send.at[other, mask // 2],
                    core_recv.at[other, mask // 2],
                    (flip(blk, 1, bits), head),
                )
            )

    def rows_to_heads(i):
        exchanges[i].over_head(
            0,
            lambda other: sources[i].at[other],
            lambda other: arrived.at[i, pl.ds(pl.multiple_of(other * rows, rows), rows), :],
        )

    rows_to_heads(0)
    rows_to_heads(1)

    for other in range(blks):
        sends.start(
            lambda other=other: remote(
                vectors.at[other],
                vec_parts.at[blk],
                vec_send.at[other],
                vec_recv.at[blk],
                (other, head),
            ),
            when=other != blk,
        )

    def add_core(other):
        for mask in even:
            loads[other, mask].wait()
            target = from_core.at[other, mask // 2]
            remote(
                target,
                target,
                core_send.at[other, mask // 2],
                core_recv.at[other, mask // 2],
                (flip(blk, 1, bits), head),
            ).wait_recv()
            add_into(total.at[other, mask // 2], target, half)

    orders = [list(range(levels - 1, 0, -1)), [1] + list(range(levels - 1, 1, -1))]

    def cols(ref, which):
        return ref.at[:, which * half : (which + 1) * half]

    def tree_parts(which, step):
        dims = orders[which]
        free = dims[step + 1 :]
        base = sum(1 << (levels - 2 - earlier) for earlier in range(step))
        return dims[step], [(mask, base + i) for i, mask in enumerate(submasks(free))]

    def tree_start(other, step):
        for which in range(2):
            dim, parts = tree_parts(which, step)
            for mask, slot in parts:
                sends.start(
                    lambda which=which, dim=dim, mask=mask, slot=slot: remote(
                        cols(total.at[other, (mask | (1 << dim)) // 2], which),
                        from_tree.at[which, other, slot],
                        tree_send.at[which, other, slot],
                        tree_recv.at[which, other, slot],
                        (flip(blk, 1 << dim, bits), head),
                    )
                )

    def tree_add(other, step):
        for which in range(2):
            dim, parts = tree_parts(which, step)
            for mask, slot in parts:
                source = from_tree.at[which, other, slot]
                remote(
                    source,
                    source,
                    tree_send.at[which, other, slot],
                    tree_recv.at[which, other, slot],
                    (flip(blk, 1 << dim, bits), head),
                ).wait_recv()
                add_into(cols(total.at[other, mask // 2], which), source, half)

    def pass_right(goal):
        target = from_left.at[goal]

        @pl.when((head > 0) & (head <= goal))
        def _():
            remote(
                target, target, left_send.at[goal], left_recv.at[goal], (blk, head)
            ).wait_recv()
            add_into(total.at[goal, 0], target, half)

        sends.start(
            lambda: remote(
                total.at[goal, 0],
                target,
                left_send.at[goal],
                left_recv.at[goal],
                (blk, jnp.minimum(head + 1, heads - 1)),
            ),
            when=head < goal,
        )

    def pass_left(goal):
        target = from_right.at[goal]

        @pl.when((head < heads - 1) & (head >= goal))
        def _():
            remote(
                target, target, right_send.at[goal], right_recv.at[goal], (blk, head)
            ).wait_recv()
            add_into(total.at[goal, 0], target, half)

        sends.start(
            lambda: remote(
                total.at[goal, 0],
                target,
                right_send.at[goal],
                right_recv.at[goal],
                (blk, jnp.maximum(head - 1, 0)),
            ),
            when=head > goal,
        )

    def to_groups(i):
        exchanges[i].wait_head(
            0, lambda other: arrived.at[i, pl.ds(pl.multiple_of(other * rows, rows), rows), :]
        )
        permute_rows(one_hot_from_column(slot_col, group), arrived.at[i], sorted_rows.at[i], group)
        exchanges[i].over_blk(
            lambda other: sorted_rows.at[i, pl.ds(other * pair, pair), :],
            lambda other: landed.at[i, pl.ds(pl.multiple_of(other * pair, pair), pair), :],
        )

    def to_positions(i):
        exchanges[i].wait_blk(
            lambda other: landed.at[i, pl.ds(pl.multiple_of(other * pair, pair), pair), :]
        )
        permute_rows(one_hot_from_column(dest_col, group), landed.at[i], ordered.at[i], group)
        exchanges[i].over_head(
            1,
            lambda other: ordered.at[i, pl.ds(other * rows, rows), :],
            lambda other: final.at[i, other],
        )

    for other in order[:2]:
        add_core(other)
        tree_start(other, 0)
    to_groups(0)
    for other in order[2:]:
        add_core(other)
        tree_start(other, 0)
    to_groups(1)
    for other in order[:2]:
        for step in range(levels - 1):
            tree_add(other, step)
            if step < levels - 2:
                tree_start(other, step + 1)
    to_positions(0)
    for position, other in enumerate(order):
        if position >= 2:
            for step in range(levels - 1):
                tree_add(other, step)
                if step < levels - 2:
                    tree_start(other, step + 1)
        if position == 2:
            to_positions(1)

    vec_mid[...] = vectors[pl.ds(blk, 1)][0]
    for other in range(blks):

        @pl.when(other != blk)
        def _():
            remote(
                vec_parts.at[other],
                vec_parts.at[other],
                vec_send.at[other],
                vec_recv.at[other],
                (other, head),
            ).wait_recv()
            vec_mid[...] += vec_parts[other]

    for other in range(heads):
        sends.start(
            lambda other=other: remote(
                vec_mid,
                vec_heads.at[head],
                vec_head_send.at[other],
                vec_head_recv.at[head],
                (blk, other),
            ),
            when=other != head,
        )

    for i in range(heads):
        goal = heads - 1 - i
        pass_right(goal)
        pass_left(i)

    for own in range(heads):

        @pl.when(own == head)
        def _():
            shard[...] = total[own, 0].astype(F32)

    vec_sum[...] = vec_mid[...]
    for other in range(heads):

        @pl.when(other != head)
        def _():
            remote(
                vec_heads.at[other],
                vec_heads.at[other],
                vec_head_send.at[other],
                vec_head_recv.at[other],
                (blk, other),
            ).wait_recv()
            vec_sum[...] += vec_heads[other]

    for i in range(2):
        exchanges[i].wait_head(1, lambda other: final.at[i, other])
    for source in range(heads):
        micro, which = source // splits, source % splits
        out_rows[micro, :, which * part : (which + 1) * part] = final[0, source]
        grad_rows[micro, :, which * part : (which + 1) * part] = final[1, source].astype(F32)
    sends.finish()


def reduce_all(blks, heads, layer_out, x_grad, partial, vectors, dest_col, slot_col):
    _, rows, part = layer_out.shape
    micros = 2
    group = rows * heads
    width = part * heads // micros
    size = partial.shape[2:]
    half = size[1] // 2
    dma = pltpu.SemaphoreType.DMA
    any_space, vmem = pl.BlockSpec(memory_space=pl.ANY), pl.BlockSpec(memory_space=pltpu.VMEM)
    vec = vectors.shape[1:]
    return pl.pallas_call(
        functools.partial(reduce_kernel, blks, heads),
        name="reduce_all",
        out_shape=(
            jax.ShapeDtypeStruct((micros, rows, width), BF16),
            jax.ShapeDtypeStruct((micros, rows, width), F32),
            jax.ShapeDtypeStruct(size, F32),
            jax.ShapeDtypeStruct(vec, F32),
        ),
        in_specs=[any_space, any_space, any_space, vmem, vmem, vmem],
        out_specs=(vmem, vmem, vmem, vmem),
        scratch_shapes=[
            pltpu.VMEM((heads, blks // 2) + size, BF16),
            pltpu.VMEM((heads, blks // 2) + size, BF16),
            pltpu.VMEM((2, heads, blks // 2 - 1, size[0], half), BF16),
            pltpu.VMEM((heads,) + size, BF16),
            pltpu.VMEM((heads,) + size, BF16),
            pltpu.VMEM((blks,) + vec, F32),
            pltpu.VMEM(vec, F32),
            pltpu.VMEM((heads,) + vec, F32),
            pltpu.VMEM((2, group, part), BF16),
            pltpu.VMEM((2, group, part), BF16),
            pltpu.VMEM((2, group, part), BF16),
            pltpu.VMEM((2, group, part), BF16),
            pltpu.VMEM((2, heads, rows, part), BF16),
        ]
        + exchange_sems(blks, heads)
        + [
            dma((heads, blks // 2)),
            dma((heads, blks // 2)),
            dma((heads, blks // 2)),
            dma((2, heads, blks // 2 - 1)),
            dma((2, heads, blks // 2 - 1)),
            dma((heads,)),
            dma((heads,)),
            dma((heads,)),
            dma((heads,)),
            dma((blks,)),
            dma((blks,)),
            dma((heads,)),
            dma((heads,)),
        ],
        compiler_params=pltpu.CompilerParams(
            collective_id=1, has_side_effects=True, vmem_limit_bytes=56 << 20
        ),
    )(layer_out, x_grad, partial, vectors, dest_col, slot_col)


def layer_norm(hidden, norm_gain, norm_shift):
    center = hidden - jnp.mean(hidden, axis=-1, keepdims=True)
    spread = jnp.mean(center * center, axis=-1, keepdims=True)
    return center * lax.rsqrt(spread + norm_epsilon) * norm_gain + norm_shift


def gelu_exact(values):
    return jax.nn.gelu(values, approximate=False)


def cluster_scores(cluster_q, cluster_k, allowed):
    scores = (
        jnp.einsum("cqhd,ckhd->chqk", cluster_q, cluster_k, preferred_element_type=F32) * 0.125
    )
    return jnp.where(allowed[:, None], scores, masked_score)


def layer_step(x, out_grad, segments, weights, vectors):
    rows, width = x.shape
    full_qkv, full_out, full_up, full_down = weights
    (
        bias_query,
        bias_value,
        bias_out,
        gain_attn,
        shift_attn,
        bias_down,
        gain_ffn,
        shift_ffn,
        bias_up,
    ) = vectors
    heads = width // HEAD_DIM
    cluster_shape = (rows // CLUSTER, CLUSTER, heads, HEAD_DIM)
    proj = jnp.dot(x, full_qkv, preferred_element_type=F32)
    cluster_q = (proj[:, 0:width] + bias_query).astype(BF16).reshape(cluster_shape)
    cluster_k = proj[:, width : 2 * width].astype(BF16).reshape(cluster_shape)
    cluster_v = (proj[:, 2 * width :] + bias_value).astype(BF16).reshape(cluster_shape)
    segments = segments.reshape(rows // CLUSTER, CLUSTER)
    allowed = segments[:, :, None] == segments[:, None, :]
    masked = cluster_scores(cluster_q, cluster_k, allowed)
    probs = jax.nn.softmax(masked, axis=-1)
    context = (
        jnp.einsum("chqk,ckhd->cqhd", probs.astype(BF16), cluster_v, preferred_element_type=F32)
        .astype(BF16)
        .reshape(rows, width)
    )
    attn_res = x.astype(F32) + jnp.dot(context, full_out, preferred_element_type=F32) + bias_out
    normed, norm_back_attn = jax.vjp(layer_norm, attn_res, gain_attn, shift_attn)
    hidden_in = normed.astype(BF16)
    pre_act = jnp.dot(hidden_in, full_up, preferred_element_type=F32) + bias_up
    active_full, gelu_back = jax.vjp(gelu_exact, pre_act)
    active = active_full.astype(BF16)
    ffn_res = normed + jnp.dot(active, full_down, preferred_element_type=F32) + bias_down
    result, norm_back_ffn = jax.vjp(layer_norm, ffn_res, gain_ffn, shift_ffn)
    d_ffn, grad_gain_ffn, grad_shift_ffn = norm_back_ffn(out_grad.astype(F32))
    g_down = d_ffn.astype(BF16)
    grad_down = jnp.einsum("tf,td->fd", active, g_down, preferred_element_type=F32)
    grad_bias_down = jnp.sum(g_down.astype(F32), axis=0)
    d_active = jnp.einsum("td,fd->tf", g_down, full_down, preferred_element_type=F32)
    (d_pre,) = gelu_back(d_active)
    g_pre = d_pre.astype(BF16)
    grad_up = jnp.einsum("td,tf->df", hidden_in, g_pre, preferred_element_type=F32)
    grad_bias_up = jnp.sum(g_pre.astype(F32), axis=0)
    d_normed = d_ffn + jnp.einsum("tf,df->td", g_pre, full_up, preferred_element_type=F32)
    d_attn, grad_gain_attn, grad_shift_attn = norm_back_attn(d_normed)
    g_attn = d_attn.astype(BF16)
    grad_out = jnp.einsum("tc,td->cd", context, g_attn, preferred_element_type=F32)
    grad_bias_out = jnp.sum(g_attn.astype(F32), axis=0)
    cluster_dout = (
        jnp.einsum("td,cd->tc", g_attn, full_out, preferred_element_type=F32)
        .astype(BF16)
        .reshape(cluster_shape)
    )
    dprob = jnp.einsum("cqhd,ckhd->chqk", cluster_dout, cluster_v, preferred_element_type=F32)
    delta = jnp.sum(probs * dprob, axis=-1, keepdims=True)
    dscore = (probs * (dprob - delta)).astype(BF16)
    grad_q = jnp.einsum("chqk,ckhd->cqhd", dscore, cluster_k, preferred_element_type=F32) * 0.125
    grad_k = jnp.einsum("chqk,cqhd->ckhd", dscore, cluster_q, preferred_element_type=F32) * 0.125
    grad_v = jnp.einsum(
        "chqk,cqhd->ckhd", probs.astype(BF16), cluster_dout, preferred_element_type=F32
    )
    g_proj = jnp.concatenate(
        [member.astype(BF16).reshape(rows, width) for member in (grad_q, grad_k, grad_v)], axis=1
    )
    grad_qkv = jnp.einsum("td,tc->dc", x, g_proj, preferred_element_type=F32)
    sums = jnp.sum(g_proj.astype(F32), axis=0)
    x_grad = d_attn + jnp.einsum("tc,dc->td", g_proj, full_qkv, preferred_element_type=F32)
    return (
        result.astype(BF16),
        x_grad.astype(BF16),
        (grad_qkv, grad_out, grad_up, grad_down),
        (
            sums[:width],
            sums[2 * width :],
            grad_bias_out,
            grad_gain_attn,
            grad_shift_attn,
            grad_bias_down,
            grad_gain_ffn,
            grad_shift_ffn,
            grad_bias_up,
        ),
    )


def body(
    tokens,
    seq_lengths,
    cluster_perm,
    out_grad,
    qkv_weight,
    query_bias,
    value_bias,
    out_weight,
    out_bias,
    attn_gain,
    attn_shift,
    up_weight,
    up_bias,
    down_weight,
    down_bias,
    ffn_gain,
    ffn_shift,
):
    blks, heads = lax.axis_size("blk"), lax.axis_size("head")
    blk, head = lax.axis_index("blk"), lax.axis_index("head")
    micros, rows, width = tokens.shape
    group = rows * heads
    total_rows = cluster_perm.shape[1]
    share = qkv_weight.shape[0]
    folds = down_weight.shape[0] // share
    short = down_weight.shape[1]
    widths = [qkv_weight.shape[1], out_weight.shape[1], up_weight.shape[1], folds * short]
    edges = [sum(widths[:i]) for i in range(5)]

    shard = jnp.concatenate(
        [qkv_weight, out_weight, up_weight]
        + [down_weight[i * share : (i + 1) * share] for i in range(folds)],
        axis=1,
    )
    lanes = -(-share // 128) * 128
    small = [
        query_bias,
        value_bias,
        out_bias,
        attn_gain,
        attn_shift,
        down_bias,
        ffn_gain,
        ffn_shift,
    ]
    stacked = jnp.concatenate([jnp.stack(small), up_bias.reshape(folds, share)], axis=0)
    count = stacked.shape[0]
    vectors = jnp.pad(stacked, ((0, -count % 16), (0, lanes - share)))
    perm = cluster_perm.reshape(micros, blks, group)
    full, full_vectors, slots_x, slots_g, dest_col, slot_col = gather_all(
        blks, heads, tokens, out_grad, shard, vectors, perm
    )

    first = blk * group + head * rows
    slots = first + jnp.arange(rows, dtype=jnp.int32)
    ends = jnp.cumsum(seq_lengths, axis=1)
    positions = jnp.arange(total_rows, dtype=jnp.int32)
    segs = jnp.sum((positions[None, :, None] >= ends[:, None, :]).astype(jnp.int32), axis=2)
    slot_segs = jnp.sum(
        jnp.where(cluster_perm[:, None, :] == slots[None, :, None], segs[:, None, :], 0), axis=2
    )

    def unpack(which):
        piece = full[:, :, :, edges[which] : edges[which + 1]]
        if which == 3:
            piece = piece.reshape(heads, blks, share, folds, short)
            return piece.transpose(1, 3, 2, 0, 4).reshape(blks * folds * share, heads * short)
        return piece.transpose(1, 2, 0, 3).reshape(blks * share, heads * widths[which])

    weights = [unpack(i) for i in range(4)]
    spread = full_vectors[:, :count, :share]
    vecs = [spread[:, i].reshape(-1).astype(F32) for i in range(8)]
    vecs.append(spread[:, 8:count].reshape(-1).astype(F32))

    def join(member):
        splits = heads // micros
        return (
            member.reshape(micros, splits, rows, width // splits)
            .transpose(0, 2, 1, 3)
            .reshape(micros * rows, width)
        )

    def split(member):
        splits = heads // micros
        return (
            member.reshape(micros, rows, splits, width // splits)
            .transpose(0, 2, 1, 3)
            .reshape(heads, rows, width // splits)
        )

    result, x_grad, grads, vec_grads = layer_step(
        join(slots_x), join(slots_g), slot_segs.reshape(-1), weights, vecs
    )

    def pack(which, grad):
        grad = grad.astype(BF16)
        if which == 3:
            grad = grad.reshape(blks, folds, share, heads, short).transpose(3, 0, 2, 1, 4)
            return grad.reshape(heads, blks, share, folds * short)
        return grad.reshape(blks, share, heads, widths[which]).transpose(2, 0, 1, 3)

    partial = jnp.concatenate([pack(i, grads[i]) for i in range(4)], axis=3)
    vec_parts = jnp.concatenate(
        [jnp.stack([v.reshape(blks, share) for v in vec_grads[:8]], axis=1)]
        + [vec_grads[8].reshape(blks, folds, share)],
        axis=1,
    )
    vec_parts = jnp.pad(vec_parts, ((0, 0), (0, -count % 16), (0, lanes - share)))
    out_rows, grad_rows, shard_grad, vec_sum = reduce_all(
        blks, heads, split(result), split(x_grad), partial, vec_parts, dest_col, slot_col
    )
    down_grad = shard_grad[:, edges[3] : edges[4]]
    down_grad = jnp.concatenate(
        [down_grad[:, i * short : (i + 1) * short] for i in range(folds)], axis=0
    )
    vec = [vec_sum[i, :share] for i in range(8)]
    return (
        out_rows,
        grad_rows,
        shard_grad[:, edges[0] : edges[1]],
        vec[0],
        vec[1],
        shard_grad[:, edges[1] : edges[2]],
        vec[2],
        vec[3],
        vec[4],
        shard_grad[:, edges[2] : edges[3]],
        vec_sum[8:count, :share].reshape(-1),
        down_grad,
        vec[5],
        vec[6],
        vec[7],
    )


def solution(mesh):
    return jax.shard_map(
        body,
        mesh=mesh,
        in_specs=(
            P(None, ("blk", "head"), None),
            P(),
            P(),
            P(None, ("blk", "head"), None),
            P("blk", "head"),
            P("blk"),
            P("blk"),
            P("blk", "head"),
            P("blk"),
            P("blk"),
            P("blk"),
            P("blk", "head"),
            P("blk"),
            P("blk", "head"),
            P("blk"),
            P("blk"),
            P("blk"),
        ),
        out_specs=(
            P(None, ("blk", "head"), None),
            P(None, ("blk", "head"), None),
            P("blk", "head"),
            P("blk"),
            P("blk"),
            P("blk", "head"),
            P("blk"),
            P("blk"),
            P("blk"),
            P("blk", "head"),
            P("blk"),
            P("blk", "head"),
            P("blk"),
            P("blk"),
            P("blk"),
        ),
        check_vma=False,
    )
```

time: 1380 us -> 649 us (0.47)
  waiting for transfers between devices: 489 us -> 0 us
  Pallas kernels: 0 us -> 328 us
  blocking collectives: 177 us -> 0 us
  starting transfers between devices: 152 us -> 0 us
  local copies, waits for them, and re-layouts: 331 us -> 222 us
  other arithmetic: 94.9 us -> 16.2 us
  matrix products: 103 us -> 67.6 us
  between operations: 20.3 us -> 2 us
    pallas_call x0 -> x2, Pallas kernels: none -> 328 us  [the longest x1 212 us: reduce_all(): pl.pallas_call(functools.partial(reduce_kernel, blks, heads), name='reduc...]
    reduce_scatter x10 -> x0, waiting for transfers between devices: 296 us -> none  [the longest x2 155 us: reduce_grads(): lax.psum_scatter(full[3], 'blk', scatter_dimension=0, tiled=True)]
    all_to_all x29 -> x0, starting transfers between devices: 151 us -> none  [the longest x2 19.2 us: one_micro(): lax.all_to_all(v_heads[send_order], 'blk', split_axis=0, concat_axis=0, t...]
    gather x40 -> x0, local copies, waits for them, and re-layouts: 134 us -> none  [the longest x4 11.4 us: one_micro(): cluster_dout = got_dout[recv_inverse].reshape(cluster_shape)]
    reshape x8 -> x25, local copies, waits for them, and re-layouts: 2.62 us -> 129 us  [the longest x6 30.9 us: pack(): return grad.reshape(blks, share, heads, widths[which]).transpose(2, 0, 1, 3)]
    unnamed x26 -> x0, waiting for transfers between devices: 107 us -> none
    all_to_all x29 -> x0, waiting for transfers between devices: 86.3 us -> none  [the longest x2 18 us: one_micro(): lax.all_to_all(dout_heads[send_order], 'blk', split_axis=0, concat_axis=0...]
    all_gather x5 -> x0, blocking collectives: 73.7 us -> none  [the longest x1 17.2 us: body(): lax.all_gather(down_weight, 'head', axis=1, tiled=True)]
  transfers between devices with their start and end apart: 49 -> 0, of which waited for: 31 -> 0; matrix products, arithmetic and copies ran while one was open for 35% -> 0% of each run, Pallas kernels for 0% -> 0%
where the time goes in v1:
time: 649 us; the launch traced here: 636 us
  Pallas kernels  328 us (51%)
  local copies, waits for them, and re-layouts  222 us (34%)
  matrix products  67.6 us (10%)
  other arithmetic  16.2 us (2%)
    pallas_call x1, Pallas kernels, reduce_all(): pl.pallas_call(functools.partial(reduce_kernel, blks, heads), name='reduc...  212 us
    pallas_call x1, Pallas kernels, gather_all(): pl.pallas_call(functools.partial(gather_kernel, blks, heads), name='gathe...  117 us
    reshape x6, local copies, waits for them, and re-layouts, pack(): return grad.reshape(blks, share, heads, widths[which]).transpose(2, 0, 1, 3)  30.9 us
    reshape x2, local copies, waits for them, and re-layouts, unpack(): piece = piece.reshape(heads, blks, share, folds, short)  24.8 us
    reshape x2, local copies, waits for them, and re-layouts, pack(): grad.reshape(blks, folds, share, heads, short).transpose(3, 0, 2, 1, 4)  23.7 us
    concatenate x1, local copies, waits for them, and re-layouts, body(): partial = jnp.concatenate([pack(i, grads[i]) for i in range(4)], axis=3)  21.4 us
    unnamed x123, local copies, waits for them, and re-layouts  21.1 us
    dot_general x1, matrix products, layer_step(): pre_act = jnp.dot(hidden_in, full_up, preferred_element_type=F32) + bias_up  18.7 us

profile of v1, /device:TPU:8, one launch (start us, length us, event | category | flops | bytes accessed | tf_op | source)
XLA Modules:
  0.0 636.3 jit_solution(4948855970298815648)
XLA Ops:
  12.2 116.5 %gather_all.1 = (bf16[4,8,96,2304]{3,2,1,0:T(8,128)(2,1)S(1)}, bf16[8,16,128]{2,1,0:T(8,128)(2,1)S(1)}, bf16[4,256,384]{2,1,0:T(8,128)(2,1)S(1)}, bf16[4,256,384...) custom-call(bf16[2,256,768]{2,1,0:T(8,128)(2,1)S(1)} %copy-done.1, ...), custom_call_target="tpu_custom_call" | custom-call | tf_op jit(solution)/shard_map/gather_all/pallas_call | solution.py:465
  128.7 5.0 copy-done
  149.5 8.0 %fusion.44 = (bf16[4,8,96,768]{3,2,1,0:T(8,128)(2,1)}, bf16[8,96,4,768]{3,1,0,2:T(8,128)(2,1)}) fusion(bf16[4,8,96,2304]{3,2,1,0:T(8,128)(2,1)} %copy-done), kind=kLoop, calls=%fused_computation.133 | loop fusion | bytes 18874368 | tf_op jit(solution)/shard_map/slice | solution.py:1050
  157.5 4.9 copy.97
  162.4 7.8 %reshape.287 = bf16[768,2304]{1,0:T(8,128)(2,1)} reshape(bf16[8,96,4,576]{3,2,1,0:T(4,128)(2,1)} %copy.97) | data formatting | bytes 7077888 | tf_op jit(solution)/shard_map/reshape | solution.py:1054
  170.3 13.3 %reshape.294 = bf16[4,8,96,4,192]{4,3,2,1,0:T(4,128)(2,1)} reshape(bf16[4,8,96,768]{3,2,1,0:T(8,128)(2,1)} %get-tuple-element.105) | data formatting | bytes 9437184 | tf_op jit(solution)/shard_map/reshape | solution.py:1052
  183.6 11.5 %copy.188 = bf16[4,8,96,4,192]{4,0,2,3,1:T(4,128)(2,1)} copy(bf16[4,8,96,4,192]{4,3,2,1,0:T(4,128)(2,1)} %reshape.294) | data formatting | bytes 9437184 | tf_op jit(solution)/shard_map/reshape | solution.py:1052
  195.1 11.7 %reshape.295 = bf16[3072,768]{1,0:T(8,128)(2,1)} reshape(bf16[8,4,96,4,192]{4,3,2,1,0:T(4,128)(2,1)} %bitcast.145) | data formatting | bytes 9437184 | tf_op jit(solution)/shard_map/reshape | solution.py:1053
  206.8 4.0 fusion.51
  234.5 18.7 %multiply_convert_fusion = (bf16[512,3072]{1,0:T(8,128)(2,1)S(1)}, f32[512,3072]{1,0:T(8,128)}, f32[512,3072]{1,0:T(8,128)}) fusion(f32[3072]{0:T(1024)S(1)} %reshape.316, bf16[768,3072]{1,0:T(8,128)(2,1)S(1)} %bitcast.157, f32[512,768]{1,0:T(8,128)S(1)} %get-tuple-element.132, f32[768]{0:T(1024)S(1)} %reshape.315, f32[768]{0:T(1024)S(1)} %reshape.314, ...), kind=kOutput, calls=%fused_computation.8 | convolution fusion | flops 2521694208 | bytes 22042624 | tf_op jit(solution)/shard_map/dot_general | solution.py:930
  263.2 9.1 %convert_reduce_fusion = (f32[3072]{0:T(1024)S(1)}, bf16[512,3072]{1,0:T(8,128)(2,1)S(1)}) fusion(f32[512,3072]{1,0:T(8,128)} %get-tuple-element.104, f32[512,3072]{1,0:T(8,128)} %get-tuple-element.133, f32[3072]{0:T(1024)S(1)} %reshape.316, bf16[512,768]{1,0:T(8,128)(2,1)S(1)} %get-tuple-element.96, bf16[3072,768]{1,0:T(8,128)(2,1)} %reshape.295), kind=kOutput, calls=%fused_computation.6 | convolution fusion | flops 2442654720 | bytes 21258240 | tf_op jit(solution)/shard_map/td,fd->tf/dot_general | solution.py:939
  272.3 4.1 multiply_reduce_fusion.2
  280.2 4.9 convolution_convert_fusion.1
  285.1 9.9 %reshape.306 = bf16[8,96,4,768]{3,2,1,0:T(4,128)(2,1)} reshape(bf16[768,3072]{1,0:T(8,128)(2,1)} %convolution_convert_fusion.1) | data formatting | bytes 9437184 | tf_op jit(solution)/shard_map/reshape | solution.py:1086
  295.0 5.4 copy.189
  312.9 4.4 convolution_convert_fusion
  317.4 12.9 %reshape.307 = bf16[8,4,96,4,192]{4,3,2,1,0:T(4,128)(2,1)} reshape(bf16[3072,768]{1,0:T(8,128)(2,1)} %convolution_convert_fusion) | data formatting | bytes 9437184 | tf_op jit(solution)/shard_map/reshape | solution.py:1084
  330.3 10.8 %copy.187 = bf16[8,4,96,4,192]{4,1,2,0,3:T(4,128)(2,1)} copy(bf16[8,4,96,4,192]{4,3,2,1,0:T(4,128)(2,1)} %reshape.307) | data formatting | bytes 9437184 | tf_op jit(solution)/shard_map/reshape | solution.py:1084
  341.0 11.9 %reshape.308 = bf16[4,8,96,768]{3,2,1,0:T(8,128)(2,1)} reshape(bf16[4,8,96,4,192]{4,3,2,1,0:T(4,128)(2,1)} %bitcast.146) | data formatting | bytes 9437184 | tf_op jit(solution)/shard_map/reshape | solution.py:1085
  372.0 5.5 convolution_convert_fusion.2
  377.5 9.3 %reshape.304 = bf16[8,96,4,576]{3,2,1,0:T(4,128)(2,1)} reshape(bf16[768,2304]{1,0:T(8,128)(2,1)} %convolution_convert_fusion.2) | data formatting | bytes 7077888 | tf_op jit(solution)/shard_map/reshape | solution.py:1086
  386.8 4.6 copy.190
  391.4 21.4 %concatenate.21.partial = bf16[4,8,96,2304]{3,2,1,0:T(8,128)(2,1)} concatenate(bf16[4,8,96,576]{3,2,1,0:T(8,128)(2,1)} %bitcast.151, bf16[4,8,96,192]{3,2,1,0:T(8,128)(2,1)S(1)} %bitcast.154, bf16[4,8,96,768]{3,2,1,0:T(8,128)(2,1)} %bitcast.147, bf16[4,8,96,768]{3,2,1,0:T(8,128)(2,1)} %reshape.308), dimensions={3} | concatenate | bytes 28311552 | tf_op jit(solution)/shard_map/concatenate | solution.py:1088
  412.8 211.8 %reduce_all.1 = (bf16[2,256,768]{2,1,0:T(8,128)(2,1)}, f32[2,256,768]{2,1,0:T(8,128)}, f32[96,2304]{1,0:T(8,128)}, f32[16,128]{1,0:T(8,128)}) custom-call(bf16[4,256,384]{2,1,0:T(8,128)(2,1)} %bitcast.163, bf16[4,256,384]{2,1,0:T(8,128)(2,1)} %bitcast.164, bf16[4,8,96,2304]{3,2,1,0:T(8,128)(2,1)} %concatenate.21.partial, f32[8,16,128]{2,1,0:T(8,128)} %pad.9.vectors, ...), custom_call_target="tpu_custom_call" | custom-call | tf_op jit(solution)/shard_map/reduce_all/pallas_call | solution.py:833
  (227 shorter events, 106.8 us)
Async XLA Ops:
  195.1 11.7 %copy-start.23 = (bf16[64,8,2,384]{3,1,2,0:T(8,128)(2,1)S(1)}, bf16[64,8,2,384]{3,1,2,0:T(8,128)(2,1)}, u32[]{:S(2)}) copy-start(bf16[64,8,2,384]{3,1,2,0:T(8,128)(2,1)} %copy.141) | copy-start | bytes 2359300
  214.9 8.0 %copy-start.5 = (bf16[4,128,12,64]{1,0,3,2:T(4,128)(2,1)}, bf16[4,128,12,64]{1,0,3,2:T(4,128)(2,1)S(1)}, u32[]{:S(2)}) copy-start(bf16[4,128,12,64]{1,0,3,2:T(4,128)(2,1)S(1)} %reshape.289) | copy-start | bytes 2359300
  217.9 5.7 copy-start.7
  229.4 23.8 %copy-start.9 = (f32[512,768]{1,0:T(8,128)}, f32[512,768]{1,0:T(8,128)S(1)}, u32[]{:S(2)}) copy-start(f32[512,768]{1,0:T(8,128)S(1)} %get-tuple-element.132) | copy-start | bytes 4718596
  233.4 19.8 %slice-start.4 = ((s8[4718592]{0:T(1024)(128)(4,1)}), s8[4194304]{0:T(1024)(128)(4,1)S(1)}, s32[]{:S(2)}) async-start(s8[4718592]{0:T(1024)(128)(4,1)} %bitcast.161), calls=%async_computation.4 | async-start | bytes 8388608
  234.5 18.7 %copy-start.14 = (bf16[96,8,4,768]{3,1,2,0:T(8,128)(2,1)}, bf16[96,8,4,768]{3,1,2,0:T(8,128)(2,1)S(1)}, u32[]{:S(2)}) copy-start(bf16[96,8,4,768]{3,1,2,0:T(8,128)(2,1)S(1)} %copy.143) | copy-start | bytes 14155780
  234.5 18.8 %slice-start.5 = ((s8[4718592]{0:T(1024)(128)(4,1)}), s8[524288]{0:T(1024)(128)(4,1)S(1)}, s32[]{:S(2)}) async-start(s8[4718592]{0:T(1024)(128)(4,1)} %bitcast.161), calls=%async_computation.5 | async-start | bytes 1048576
  263.0 9.3 %slice-start.2 = ((s8[4718592]{0:T(1024)(128)(4,1)}), s8[4194304]{0:T(1024)(128)(4,1)S(1)}, s32[]{:S(2)}) async-start(s8[4718592]{0:T(1024)(128)(4,1)} %bitcast.158), calls=%async_computation.2 | async-start | bytes 8388608
  263.2 9.1 %copy-start.31 = (bf16[512,768]{1,0:T(8,128)(2,1)}, bf16[512,768]{1,0:T(8,128)(2,1)S(1)}, u32[]{:S(2)}) copy-start(bf16[512,768]{1,0:T(8,128)(2,1)S(1)} %get-tuple-element.96) | copy-start | bytes 2359300
  263.2 9.1 %copy-start.10 = (f32[512,768]{1,0:T(8,128)S(1)}, f32[512,768]{1,0:T(8,128)}, u32[]{:S(2)}) copy-start(f32[512,768]{1,0:T(8,128)} %copy-done.9) | copy-start | bytes 4718596
  263.2 9.1 %slice-start.3 = ((s8[4718592]{0:T(1024)(128)(4,1)}), s8[524288]{0:T(1024)(128)(4,1)S(1)}, s32[]{:S(2)}) async-start(s8[4718592]{0:T(1024)(128)(4,1)} %bitcast.158), calls=%async_computation.3 | async-start | bytes 1048576
  280.2 21.0 %copy-start.11 = (f32[512,768]{1,0:T(8,128)}, f32[512,768]{1,0:T(8,128)S(1)}, u32[]{:S(2)}) copy-start(f32[512,768]{1,0:T(8,128)S(1)} %get-tuple-element.100) | copy-start | bytes 4718596
  285.1 16.1 %copy-start.43 = (f32[512]{0:T(512)}, f32[512]{0:T(512)S(1)}, u32[]{:S(2)}) copy-start(f32[512]{0:T(512)S(1)} %negate_multiply_fusion.1) | copy-start | bytes 6148
  295.0 7.0 %copy-start.22 = (bf16[768,768]{0,1:T(8,128)(2,1)S(1)}, bf16[768,768]{0,1:T(8,128)(2,1)}, u32[]{:S(2)}) copy-start(bf16[768,768]{0,1:T(8,128)(2,1)} %reshape.292) | copy-start | bytes 3538948
  341.0 11.9 %copy-start.27 = (bf16[4,128,12,64]{1,0,3,2:T(4,128)(2,1)S(1)}, bf16[4,128,12,64]{1,0,3,2:T(4,128)(2,1)}, u32[]{:S(2)}) copy-start(bf16[4,128,12,64]{1,0,3,2:T(4,128)(2,1)} %reshape.288) | copy-start | bytes 2359300
  365.8 5.4 copy-start.37
  365.8 5.4 copy-start.38
  365.8 5.4 copy-start.39
  365.8 5.4 copy-start.40
  365.8 5.4 copy-start.41
  365.8 5.4 copy-start.42
  365.9 6.1 copy-start.25
  624.6 9.2 %copy-start.30 = (bf16[2,256,768]{2,1,0:T(8,128)(2,1)S(1)}, bf16[2,256,768]{2,1,0:T(8,128)(2,1)}, u32[]{:S(2)}) copy-start(bf16[2,256,768]{2,1,0:T(8,128)(2,1)} %get-tuple-element.154) | copy-start | bytes 2359300
  624.6 10.0 %copy-start.20 = (f32[2,256,768]{2,1,0:T(8,128)S(1)}, f32[2,256,768]{2,1,0:T(8,128)}, u32[]{:S(2)}) copy-start(f32[2,256,768]{2,1,0:T(8,128)} %get-tuple-element.155) | copy-start | bytes 4718596
  (31 other events, 77.6 us)

commit v2 on v1

--- a/solution.py
+++ b/solution.py
@@ -878,109 +878,468 @@
     )(layer_out, x_grad, partial, vectors, dest_col, slot_col)
 
 
-def layer_norm(hidden, norm_gain, norm_shift):
-    center = hidden - jnp.mean(hidden, axis=-1, keepdims=True)
-    spread = jnp.mean(center * center, axis=-1, keepdims=True)
-    return center * lax.rsqrt(spread + norm_epsilon) * norm_gain + norm_shift
-
-
-def gelu_exact(values):
-    return jax.nn.gelu(values, approximate=False)
-
-
-def cluster_scores(cluster_q, cluster_k, allowed):
-    scores = (
-        jnp.einsum("cqhd,ckhd->chqk", cluster_q, cluster_k, preferred_element_type=F32) * 0.125
-    )
-    return jnp.where(allowed[:, None], scores, masked_score)
-
-
-def layer_step(x, out_grad, segments, weights, vectors):
-    rows, width = x.shape
-    full_qkv, full_out, full_up, full_down = weights
-    (
-        bias_query,
-        bias_value,
-        bias_out,
-        gain_attn,
-        shift_attn,
-        bias_down,
-        gain_ffn,
-        shift_ffn,
-        bias_up,
-    ) = vectors
-    heads = width // HEAD_DIM
-    cluster_shape = (rows // CLUSTER, CLUSTER, heads, HEAD_DIM)
-    proj = jnp.dot(x, full_qkv, preferred_element_type=F32)
-    cluster_q = (proj[:, 0:width] + bias_query).astype(BF16).reshape(cluster_shape)
-    cluster_k = proj[:, width : 2 * width].astype(BF16).reshape(cluster_shape)
-    cluster_v = (proj[:, 2 * width :] + bias_value).astype(BF16).reshape(cluster_shape)
-    segments = segments.reshape(rows // CLUSTER, CLUSTER)
-    allowed = segments[:, :, None] == segments[:, None, :]
-    masked = cluster_scores(cluster_q, cluster_k, allowed)
-    probs = jax.nn.softmax(masked, axis=-1)
-    context = (
-        jnp.einsum("chqk,ckhd->cqhd", probs.astype(BF16), cluster_v, preferred_element_type=F32)
-        .astype(BF16)
-        .reshape(rows, width)
-    )
-    attn_res = x.astype(F32) + jnp.dot(context, full_out, preferred_element_type=F32) + bias_out
-    normed, norm_back_attn = jax.vjp(layer_norm, attn_res, gain_attn, shift_attn)
-    hidden_in = normed.astype(BF16)
-    pre_act = jnp.dot(hidden_in, full_up, preferred_element_type=F32) + bias_up
-    active_full, gelu_back = jax.vjp(gelu_exact, pre_act)
-    active = active_full.astype(BF16)
-    ffn_res = normed + jnp.dot(active, full_down, preferred_element_type=F32) + bias_down
-    result, norm_back_ffn = jax.vjp(layer_norm, ffn_res, gain_ffn, shift_ffn)
-    d_ffn, grad_gain_ffn, grad_shift_ffn = norm_back_ffn(out_grad.astype(F32))
-    g_down = d_ffn.astype(BF16)
-    grad_down = jnp.einsum("tf,td->fd", active, g_down, preferred_element_type=F32)
-    grad_bias_down = jnp.sum(g_down.astype(F32), axis=0)
-    d_active = jnp.einsum("td,fd->tf", g_down, full_down, preferred_element_type=F32)
-    (d_pre,) = gelu_back(d_active)
-    g_pre = d_pre.astype(BF16)
-    grad_up = jnp.einsum("td,tf->df", hidden_in, g_pre, preferred_element_type=F32)
-    grad_bias_up = jnp.sum(g_pre.astype(F32), axis=0)
-    d_normed = d_ffn + jnp.einsum("tf,df->td", g_pre, full_up, preferred_element_type=F32)
-    d_attn, grad_gain_attn, grad_shift_attn = norm_back_attn(d_normed)
-    g_attn = d_attn.astype(BF16)
-    grad_out = jnp.einsum("tc,td->cd", context, g_attn, preferred_element_type=F32)
-    grad_bias_out = jnp.sum(g_attn.astype(F32), axis=0)
-    cluster_dout = (
-        jnp.einsum("td,cd->tc", g_attn, full_out, preferred_element_type=F32)
-        .astype(BF16)
-        .reshape(cluster_shape)
-    )
-    dprob = jnp.einsum("cqhd,ckhd->chqk", cluster_dout, cluster_v, preferred_element_type=F32)
-    delta = jnp.sum(probs * dprob, axis=-1, keepdims=True)
-    dscore = (probs * (dprob - delta)).astype(BF16)
-    grad_q = jnp.einsum("chqk,ckhd->cqhd", dscore, cluster_k, preferred_element_type=F32) * 0.125
-    grad_k = jnp.einsum("chqk,cqhd->ckhd", dscore, cluster_q, preferred_element_type=F32) * 0.125
-    grad_v = jnp.einsum(
-        "chqk,cqhd->ckhd", probs.astype(BF16), cluster_dout, preferred_element_type=F32
-    )
-    g_proj = jnp.concatenate(
-        [member.astype(BF16).reshape(rows, width) for member in (grad_q, grad_k, grad_v)], axis=1
-    )
-    grad_qkv = jnp.einsum("td,tc->dc", x, g_proj, preferred_element_type=F32)
-    sums = jnp.sum(g_proj.astype(F32), axis=0)
-    x_grad = d_attn + jnp.einsum("tc,dc->td", g_proj, full_qkv, preferred_element_type=F32)
-    return (
-        result.astype(BF16),
-        x_grad.astype(BF16),
-        (grad_qkv, grad_out, grad_up, grad_down),
-        (
-            sums[:width],
-            sums[2 * width :],
-            grad_bias_out,
-            grad_gain_attn,
-            grad_shift_attn,
-            grad_bias_down,
-            grad_gain_ffn,
-            grad_shift_ffn,
-            grad_bias_up,
+def contract(left, right, dims):
+    return lax.dot_general(left, right, ((dims[:1], dims[1:]), ((), ())), preferred_element_type=F32)
+
+
+def assemble_attention(packed, qkv, out):
+    heads, width, _ = packed.shape
+    wide, narrow = qkv.shape[1] // heads, out.shape[1] // heads
+
+    @pl.loop(0, width // CLUSTER)
+    def _(tile):
+        rows = pl.ds(pl.multiple_of(tile * CLUSTER, CLUSTER), CLUSTER)
+        for head in range(heads):
+            qkv[rows, head * wide : (head + 1) * wide] = packed[head, rows, 0:wide]
+            out[rows, head * narrow : (head + 1) * narrow] = packed[
+                head, rows, wide : wide + narrow
+            ]
+
+
+def column_sum(values):
+    return jnp.sum(values, axis=0, keepdims=True)
+
+
+def row_mean(values):
+    return jnp.mean(values, axis=1, keepdims=True)
+
+
+def normalize(hidden):
+    center = hidden - row_mean(hidden)
+    scale = lax.rsqrt(row_mean(center * center) + norm_epsilon)
+    return center * scale, scale
+
+
+def norm_derivative(normal, scale, cotangent, gain):
+    scaled = cotangent * gain
+    return scale * (scaled - row_mean(scaled) - normal * row_mean(scaled * normal))
+
+
+def forward_kernel(
+    slots_x,
+    weights,
+    bias_qkv,
+    vectors,
+    seg_col,
+    seg_row,
+    x,
+    proj,
+    probs,
+    context,
+    attn_res,
+    qkv,
+    out,
+    packed,
+    sem,
+):
+    heads, rows, part = slots_x.shape
+    tokens, width = x.shape
+    splits = width // part
+    load = pltpu.make_async_copy(weights.at[:, :, 0 : packed.shape[2]], packed, sem.at[0])
+    load.start()
+    for source in range(heads):
+        micro, which = source // splits, source % splits
+        x[micro * rows : (micro + 1) * rows, which * part : (which + 1) * part] = slots_x[source]
+    load.wait()
+    assemble_attention(packed, qkv, out)
+    project(x, qkv, bias_qkv, proj)
+    attend(proj, probs, context, seg_col, seg_row)
+    leave_attention(x, context, out, vectors, attn_res)
+
+
+def project(x, qkv, bias_qkv, proj):
+    @pl.loop(0, proj.shape[1] // 256)
+    def _(tile):
+        cols = pl.ds(pl.multiple_of(tile * 256, 256), 256)
+        sums = jnp.dot(x[...], qkv[:, cols], preferred_element_type=F32)
+        proj[:, cols] = (sums + bias_qkv[:, cols]).astype(BF16)
+
+
+def two_heads(tile, first):
+    zero = jnp.zeros_like(tile)
+    return jnp.concatenate([jnp.where(first, tile, zero), jnp.where(first, zero, tile)], axis=0)
+
+
+def attend(proj, probs, context, seg_col, seg_row):
+    tokens, width = context.shape
+    first = iota((CLUSTER, 128), 1) < HEAD_DIM
+
+    @pl.loop(0, tokens // CLUSTER)
+    def _(cluster):
+        rows = pl.ds(pl.multiple_of(cluster * CLUSTER, CLUSTER), CLUSTER)
+        column = seg_col[rows, 0:1]
+        allowed = jnp.concatenate([column, column], axis=0) == seg_row[pl.ds(cluster, 1), :]
+        for pair in range(width // 128):
+            at = pair * 128
+            q = two_heads(proj[rows, at : at + 128], first)
+            k = proj[rows, width + at : width + at + 128]
+            v = proj[rows, 2 * width + at : 2 * width + at + 128]
+            scores = contract(q, k, (1, 1)) * 0.125
+            scores = jnp.where(allowed, scores, masked_score)
+            weight = jnp.exp(scores - jnp.max(scores, axis=1, keepdims=True))
+            p = (weight / jnp.sum(weight, axis=1, keepdims=True)).astype(BF16)
+            probs[cluster, pair] = p
+            both = jnp.dot(p, v, preferred_element_type=F32)
+            context[rows, at : at + 128] = jnp.where(
+                first, both[:CLUSTER], both[CLUSTER:]
+            ).astype(BF16)
+
+
+def leave_attention(x, context, out, vectors, attn_res):
+    @pl.loop(0, x.shape[1] // 256)
+    def _(tile):
+        cols = pl.ds(pl.multiple_of(tile * 256, 256), 256)
+        sums = jnp.dot(context[...], out[:, cols], preferred_element_type=F32)
+        attn_res[:, cols] = x[:, cols].astype(F32) + sums + vectors[2:3, cols]
+
+
+def forward_part(slots_x, weights, bias_qkv, vectors, seg_col, seg_row):
+    heads, rows, part = slots_x.shape
+    width = weights.shape[1]
+    tokens = heads * part * rows // width
+    vmem = pl.BlockSpec(memory_space=pltpu.VMEM)
+    return pl.pallas_call(
+        forward_kernel,
+        name="forward_part",
+        out_shape=(
+            jax.ShapeDtypeStruct((tokens, width), BF16),
+            jax.ShapeDtypeStruct((tokens, 3 * width), BF16),
+            jax.ShapeDtypeStruct((tokens // CLUSTER, width // 128, 2 * CLUSTER, CLUSTER), BF16),
+            jax.ShapeDtypeStruct((tokens, width), BF16),
+            jax.ShapeDtypeStruct((tokens, width), F32),
+            jax.ShapeDtypeStruct((width, 3 * width), BF16),
+            jax.ShapeDtypeStruct((width, width), BF16),
         ),
-    )
+        in_specs=[vmem, pl.BlockSpec(memory_space=pl.ANY), vmem, vmem, vmem, vmem],
+        out_specs=(vmem,) * 7,
+        scratch_shapes=[
+            pltpu.VMEM((heads, width, width), BF16),
+            pltpu.SemaphoreType.DMA((1,)),
+        ],
+        compiler_params=pltpu.CompilerParams(vmem_limit_bytes=48 << 20),
+    )(slots_x, weights, bias_qkv, vectors, seg_col, seg_row)
+
+
+def ffn_kernel(
+    share,
+    attn_res,
+    slots_g,
+    weights,
+    vectors,
+    up_bias,
+    layer_out,
+    d_attn,
+    g_attn,
+    partial,
+    vec_grads,
+    up_bias_grad,
+    packed,
+    down,
+    normed,
+    hidden,
+    hidden_t,
+    active,
+    slope,
+    g_pre,
+    ffn_res,
+    g_down,
+    sem,
+):
+    heads, rows, part = slots_g.shape
+    tokens, width = attn_res.shape
+    ff = active.shape[1]
+    fold = ff // width
+    short = width // heads
+    splits = width // part
+    load = pltpu.make_async_copy(weights.at[:, :, width : 3 * width], packed, sem.at[0])
+    load.start()
+    gain_attn, shift_attn = vectors[3:4, :], vectors[4:5, :]
+    bias_down, gain_ffn, shift_ffn = vectors[5:6, :], vectors[6:7, :], vectors[7:8, :]
+    vec_grads[...] = jnp.zeros_like(vec_grads)
+
+    def row_tiles(body):
+        @pl.loop(0, tokens // CLUSTER)
+        def _(tile):
+            body(tile, pl.ds(pl.multiple_of(tile * CLUSTER, CLUSTER), CLUSTER))
+
+    def first_norm(tile, at):
+        normal, _ = normalize(attn_res[at, :])
+        values = normal * gain_attn + shift_attn
+        normed[at, :] = values
+        hidden[at, :] = values.astype(BF16)
+
+    row_tiles(first_norm)
+    hidden_t[...] = hidden[...].T
+    load.wait()
+
+    blks = width // share
+
+    @pl.loop(0, blks)
+    def _(blk):
+        source = pl.ds(pl.multiple_of(blk * share, share), share)
+        for j in range(fold):
+            target = pl.ds(pl.multiple_of(blk * share * fold + j * share, share), share)
+            for head in range(heads):
+                down[target, head * short : (head + 1) * short] = packed[
+                    head, source, width + j * short : width + (j + 1) * short
+                ]
+
+    per_head = width // 256
+
+    @pl.loop(0, ff // 256)
+    def _(tile):
+        cols = pl.ds(pl.multiple_of(tile * 256, 256), 256)
+        inner = pl.ds(pl.multiple_of(tile % per_head * 256, 256), 256)
+        pre = jnp.dot(
+            hidden[...], packed[tile // per_head, :, inner], preferred_element_type=F32
+        )
+        pre = pre + up_bias[:, cols]
+        below = 0.5 + 0.5 * lax.erf(pre * (0.5**0.5))
+        active[:, cols] = (pre * below).astype(BF16)
+        slope[:, cols] = below + pre * jnp.exp(-0.5 * pre * pre) * (0.5 / jnp.pi) ** 0.5
+
+    @pl.loop(0, width // 256)
+    def _(tile):
+        cols = pl.ds(pl.multiple_of(tile * 256, 256), 256)
+        sums = jnp.dot(active[...], down[:, cols], preferred_element_type=F32)
+        ffn_res[:, cols] = normed[:, cols] + sums + vectors[5:6, cols]
+
+    def second_norm(tile, at):
+        normal, scale = normalize(ffn_res[at, :])
+        result = (normal * gain_ffn + shift_ffn).astype(BF16)
+        micro = tile * CLUSTER // rows
+        inner = pl.ds(pl.multiple_of(tile * CLUSTER % rows, CLUSTER), CLUSTER)
+        for which in range(splits):
+            layer_out[micro * splits + which, inner, :] = result[
+                :, which * part : (which + 1) * part
+            ]
+        cotangent = jnp.concatenate(
+            [slots_g[micro * splits + which, inner, :] for which in range(splits)], axis=1
+        ).astype(F32)
+        d_ffn = norm_derivative(normal, scale, cotangent, gain_ffn)
+        low = d_ffn.astype(BF16)
+        g_down[at, :] = low
+        ffn_res[at, :] = d_ffn
+        vec_grads[5:6, :] += column_sum(low.astype(F32))
+        vec_grads[6:7, :] += column_sum(cotangent * normal)
+        vec_grads[7:8, :] += column_sum(cotangent)
+
+    row_tiles(second_norm)
+
+    @pl.loop(0, ff // 256)
+    def _(tile):
+        cols = pl.ds(pl.multiple_of(tile * 256, 256), 256)
+        inner = pl.ds(pl.multiple_of(tile % per_head * 256, 256), 256)
+        d_active = contract(g_down[...], down[cols, :], (1, 1))
+        low = (d_active * slope[:, cols]).astype(BF16)
+        g_pre[:, cols] = low
+        up_bias_grad[:, cols] = column_sum(low.astype(F32))
+        up_grad = jnp.dot(hidden_t[...], low, preferred_element_type=F32)
+        partial[tile // per_head, :, inner] = up_grad.astype(BF16)
+
+    @pl.loop(0, blks)
+    def _(blk):
+        wide = share * fold
+        cols = pl.ds(pl.multiple_of(blk * wide, wide), wide)
+        down_grad = contract(active[:, cols], g_down[...], (0, 0)).astype(BF16)
+        target = pl.ds(pl.multiple_of(blk * share, share), share)
+        for j in range(fold):
+            for head in range(heads):
+                partial[head, target, width + j * short : width + (j + 1) * short] = down_grad[
+                    j * share : (j + 1) * share, head * short : (head + 1) * short
+                ]
+
+    @pl.loop(0, width // 256)
+    def _(tile):
+        cols = pl.ds(pl.multiple_of(tile * 256, 256), 256)
+        sums = ffn_res[:, cols]
+        for head in range(heads):
+            sums = sums + contract(
+                g_pre[:, head * width : (head + 1) * width], packed[head, cols, 0:width], (1, 1)
+            )
+        normed[:, cols] = sums
+
+    def first_norm_back(tile, at):
+        normal, scale = normalize(attn_res[at, :])
+        cotangent = normed[at, :]
+        grad = norm_derivative(normal, scale, cotangent, gain_attn)
+        low = grad.astype(BF16)
+        d_attn[at, :] = grad
+        g_attn[at, :] = low
+        vec_grads[2:3, :] += column_sum(low.astype(F32))
+        vec_grads[3:4, :] += column_sum(cotangent * normal)
+        vec_grads[4:5, :] += column_sum(cotangent)
+
+    row_tiles(first_norm_back)
+
+
+def ffn_part(share, attn_res, slots_g, weights, vectors, up_bias):
+    heads = weights.shape[0]
+    tokens, width = attn_res.shape
+    ff = up_bias.shape[1]
+    vmem = pl.BlockSpec(memory_space=pltpu.VMEM)
+    return pl.pallas_call(
+        functools.partial(ffn_kernel, share),
+        name="ffn_part",
+        out_shape=(
+            jax.ShapeDtypeStruct(slots_g.shape, BF16),
+            jax.ShapeDtypeStruct((tokens, width), F32),
+            jax.ShapeDtypeStruct((tokens, width), BF16),
+            jax.ShapeDtypeStruct((heads, width, 2 * width), BF16),
+            jax.ShapeDtypeStruct((8, width), F32),
+            jax.ShapeDtypeStruct((1, ff), F32),
+        ),
+        in_specs=[vmem, vmem, pl.BlockSpec(memory_space=pl.ANY), vmem, vmem],
+        out_specs=(vmem,) * 6,
+        scratch_shapes=[
+            pltpu.VMEM((heads, width, 2 * width), BF16),
+            pltpu.VMEM((ff, width), BF16),
+            pltpu.VMEM((tokens, width), F32),
+            pltpu.VMEM((tokens, width), BF16),
+            pltpu.VMEM((width, tokens), BF16),
+            pltpu.VMEM((tokens, ff), BF16),
+            pltpu.VMEM((tokens, ff), F32),
+            pltpu.VMEM((tokens, ff), BF16),
+            pltpu.VMEM((tokens, width), F32),
+            pltpu.VMEM((tokens, width), BF16),
+            pltpu.SemaphoreType.DMA((1,)),
+        ],
+        compiler_params=pltpu.CompilerParams(vmem_limit_bytes=60 << 20),
+    )(attn_res, slots_g, weights, vectors, up_bias)
+
+
+def attend_back(proj, probs, g_context, g_proj):
+    tokens, width = g_context.shape
+    first = iota((CLUSTER, 128), 1) < HEAD_DIM
+
+    @pl.loop(0, tokens // CLUSTER)
+    def _(cluster):
+        rows = pl.ds(pl.multiple_of(cluster * CLUSTER, CLUSTER), CLUSTER)
+        for pair in range(width // 128):
+            at = pair * 128
+            q = two_heads(proj[rows, at : at + 128], first)
+            k = proj[rows, width + at : width + at + 128]
+            v = proj[rows, 2 * width + at : 2 * width + at + 128]
+            g = two_heads(g_context[rows, at : at + 128], first)
+            low = probs[cluster, pair]
+            p = low.astype(F32)
+            dprob = contract(g, v, (1, 1))
+            delta = jnp.sum(p * dprob, axis=1, keepdims=True)
+            dscore = (p * (dprob - delta)).astype(BF16)
+            both = jnp.dot(dscore, k, preferred_element_type=F32)
+            g_q = jnp.where(first, both[:CLUSTER], both[CLUSTER:]) * 0.125
+            g_k = contract(dscore, q, (0, 0)) * 0.125
+            g_v = contract(low, g, (0, 0))
+            g_proj[rows, at : at + 128] = g_q.astype(BF16)
+            g_proj[rows, width + at : width + at + 128] = g_k.astype(BF16)
+            g_proj[rows, 2 * width + at : 2 * width + at + 128] = g_v.astype(BF16)
+
+
+def backward_kernel(
+    x,
+    proj,
+    probs,
+    context,
+    qkv,
+    out,
+    d_attn,
+    g_attn,
+    x_grad,
+    partial,
+    vec_grads,
+    g_context,
+    g_proj,
+    x_t,
+    natural,
+):
+    heads, rows, part = x_grad.shape
+    tokens, width = x.shape
+    splits = width // part
+    wide, narrow = 3 * width // heads, width // heads
+    g_context[...] = contract(g_attn[...], out[...], (1, 1)).astype(BF16)
+    x_t[...] = context[...].T
+
+    def tiles(count, body):
+        @pl.loop(0, count)
+        def _(tile):
+            body(pl.ds(pl.multiple_of(tile * 256, 256), 256))
+
+    def out_grad(cols):
+        natural[:, cols] = jnp.dot(
+            x_t[...], g_attn[:, cols], preferred_element_type=F32
+        ).astype(BF16)
+
+    tiles(width // 256, out_grad)
+
+    @pl.loop(0, width // CLUSTER)
+    def _(tile):
+        at = pl.ds(pl.multiple_of(tile * CLUSTER, CLUSTER), CLUSTER)
+        for head in range(heads):
+            partial[head, at, wide : wide + narrow] = natural[
+                at, head * narrow : (head + 1) * narrow
+            ]
+
+    attend_back(proj, probs, g_context, g_proj)
+    x_t[...] = x[...].T
+
+    def qkv_grad(cols):
+        natural[:, cols] = jnp.dot(
+            x_t[...], g_proj[:, cols], preferred_element_type=F32
+        ).astype(BF16)
+
+    tiles(3 * width // 256, qkv_grad)
+
+    @pl.loop(0, width // CLUSTER)
+    def _(tile):
+        at = pl.ds(pl.multiple_of(tile * CLUSTER, CLUSTER), CLUSTER)
+        for head in range(heads):
+            partial[head, at, 0:wide] = natural[at, head * wide : (head + 1) * wide]
+
+    vec_grads[...] = jnp.zeros_like(vec_grads)
+    vec_grads[0:1, :] = column_sum(g_proj[:, 0:width].astype(F32))
+    vec_grads[1:2, :] = column_sum(g_proj[:, 2 * width :].astype(F32))
+    for which in range(splits):
+        for piece in range(part // 128):
+            at = which * part + piece * 128
+            sums = d_attn[:, at : at + 128] + contract(g_proj[...], qkv[at : at + 128, :], (1, 1))
+            for micro in range(heads // splits):
+                x_grad[micro * splits + which, :, piece * 128 : (piece + 1) * 128] = sums[
+                    micro * rows : (micro + 1) * rows
+                ].astype(BF16)
+
+
+def backward_part(heads, rows, x, proj, probs, context, qkv, out, d_attn, g_attn):
+    tokens, width = x.shape
+    part = tokens * width // (heads * rows)
+    vmem = pl.BlockSpec(memory_space=pltpu.VMEM)
+    return pl.pallas_call(
+        backward_kernel,
+        name="backward_part",
+        out_shape=(
+            jax.ShapeDtypeStruct((heads, rows, part), BF16),
+            jax.ShapeDtypeStruct((heads, width, width), BF16),
+            jax.ShapeDtypeStruct((8, width), F32),
+        ),
+        in_specs=[vmem] * 8,
+        out_specs=(vmem,) * 3,
+        scratch_shapes=[
+            pltpu.VMEM((tokens, width), BF16),
+            pltpu.VMEM((tokens, 3 * width), BF16),
+            pltpu.VMEM((width, tokens), BF16),
+            pltpu.VMEM((width, 3 * width), BF16),
+        ],
+        compiler_params=pltpu.CompilerParams(vmem_limit_bytes=48 << 20),
+    )(x, proj, probs, context, qkv, out, d_attn, g_attn)
+
+
+def refold(packed, share, other, fold):
+    if share == other:
+        return packed
+    heads, width, wide = packed.shape
+    short = wide // fold
+    rows = packed.reshape(heads, width // share, share, fold, short).transpose(0, 1, 3, 2, 4)
+    rows = rows.reshape(heads, width // other, fold, other, short).transpose(0, 1, 3, 2, 4)
+    return rows.reshape(packed.shape)
 
 
 def body(
@@ -1046,54 +1405,42 @@
         jnp.where(cluster_perm[:, None, :] == slots[None, :, None], segs[:, None, :], 0), axis=2
     )
 
-    def unpack(which):
-        piece = full[:, :, :, edges[which] : edges[which + 1]]
-        if which == 3:
-            piece = piece.reshape(heads, blks, share, folds, short)
-            return piece.transpose(1, 3, 2, 0, 4).reshape(blks * folds * share, heads * short)
-        return piece.transpose(1, 2, 0, 3).reshape(blks * share, heads * widths[which])
-
-    weights = [unpack(i) for i in range(4)]
-    spread = full_vectors[:, :count, :share]
-    vecs = [spread[:, i].reshape(-1).astype(F32) for i in range(8)]
-    vecs.append(spread[:, 8:count].reshape(-1).astype(F32))
-
-    def join(member):
-        splits = heads // micros
-        return (
-            member.reshape(micros, splits, rows, width // splits)
-            .transpose(0, 2, 1, 3)
-            .reshape(micros * rows, width)
-        )
-
-    def split(member):
-        splits = heads // micros
-        return (
-            member.reshape(micros, rows, splits, width // splits)
-            .transpose(0, 2, 1, 3)
-            .reshape(heads, rows, width // splits)
-        )
-
-    result, x_grad, grads, vec_grads = layer_step(
-        join(slots_x), join(slots_g), slot_segs.reshape(-1), weights, vecs
+    weights = full.reshape(heads, blks * share, -1)
+    tall = share if share % 16 == 0 else width // 8
+    if tall != share:
+        weights = jnp.concatenate(
+            [weights[:, :, : edges[3]], refold(weights[:, :, edges[3] :], share, tall, folds)],
+            axis=2,
+        )
+    spread = full_vectors[:, :count, :share].astype(F32)
+    vecs = spread[:, :8].transpose(1, 0, 2).reshape(8, width)
+    up_vec = spread[:, 8:count].reshape(1, -1)
+    bias_qkv = jnp.concatenate([vecs[0:1], jnp.zeros((1, width), F32), vecs[1:2]], axis=1)
+    seg_col = jnp.broadcast_to(slot_segs.reshape(-1, 1), (micros * rows, 128))
+    seg_row = slot_segs.reshape(-1, CLUSTER)
+    x, proj, probs, context, attn_res, qkv, out = forward_part(
+        slots_x, weights, bias_qkv, vecs, seg_col, seg_row
     )
-
-    def pack(which, grad):
-        grad = grad.astype(BF16)
-        if which == 3:
-            grad = grad.reshape(blks, folds, share, heads, short).transpose(3, 0, 2, 1, 4)
-            return grad.reshape(heads, blks, share, folds * short)
-        return grad.reshape(blks, share, heads, widths[which]).transpose(2, 0, 1, 3)
-
-    partial = jnp.concatenate([pack(i, grads[i]) for i in range(4)], axis=3)
+    layer_out, d_attn, g_attn, partial_ffn, vec_ffn, up_vec_grad = ffn_part(
+        tall, attn_res, slots_g, weights, vecs, up_vec
+    )
+    x_grad, partial_attn, vec_attn = backward_part(
+        heads, rows, x, proj, probs, context, qkv, out, d_attn, g_attn
+    )
+    if tall != share:
+        partial_ffn = jnp.concatenate(
+            [partial_ffn[:, :, :width], refold(partial_ffn[:, :, width:], tall, share, folds)],
+            axis=2,
+        )
+    partial = jnp.concatenate([partial_attn, partial_ffn], axis=2).reshape(full.shape)
+    vec_grads = vec_ffn + vec_attn
     vec_parts = jnp.concatenate(
-        [jnp.stack([v.reshape(blks, share) for v in vec_grads[:8]], axis=1)]
-        + [vec_grads[8].reshape(blks, folds, share)],
+        [vec_grads.reshape(8, blks, share).transpose(1, 0, 2), up_vec_grad.reshape(blks, folds, share)],
         axis=1,
     )
     vec_parts = jnp.pad(vec_parts, ((0, 0), (0, -count % 16), (0, lanes - share)))
     out_rows, grad_rows, shard_grad, vec_sum = reduce_all(
-        blks, heads, split(result), split(x_grad), partial, vec_parts, dest_col, slot_col
+        blks, heads, layer_out, x_grad, partial, vec_parts, dest_col, slot_col
     )
     down_grad = shard_grad[:, edges[3] : edges[4]]
     down_grad = jnp.concatenate(

time: 649 us -> 471 us (0.73); the launches traced: 636 us -> 468 us
  local copies, waits for them, and re-layouts: 222 us -> 38.6 us
  Pallas kernels: 328 us -> 409 us
  matrix products: 67.6 us -> 0 us
    reshape x23 -> x6, local copies, waits for them, and re-layouts: 128 us -> 0.96 us  [the longest x1 0.7 us: body(): up_vec = spread[:, 8:count].reshape(1, -1)]
    pallas_call x0 -> x3, Pallas kernels: none -> 80.9 us  [the longest x1 43.5 us: ffn_part(): pl.pallas_call(functools.partial(ffn_kernel, share), name='ffn_part', out...]
    dot_general x18 -> x0, matrix products: 67.6 us -> none  [the longest x1 18.7 us: layer_step(): pre_act = jnp.dot(hidden_in, full_up, preferred_element_type=F32) + bias_up]
    concatenate x3 -> x1, local copies, waits for them, and re-layouts: 21.6 us -> 0.01 us  [body(): jnp.concatenate([vecs[0:1], jnp.zeros((1, width), F32), vecs[1:2]], axis=1)]
    transpose x6 -> x2, local copies, waits for them, and re-layouts: 16.3 us -> 0.01 us  [body(): vecs = spread[:, :8].transpose(1, 0, 2).reshape(8, width)]
    concatenate x0 -> x3, other arithmetic: none -> 13.2 us  [the longest x1 12.5 us: body(): jnp.concatenate([partial_attn, partial_ffn], axis=2).reshape(full.shape)]
    reduce_sum x10 -> x0, other arithmetic: 8.57 us -> none  [the longest x2 4.2 us: layer_norm(): center = hidden - jnp.mean(hidden, axis=-1, keepdims=True)]
    convert_element_type x17 -> x0, local copies, waits for them, and re-layouts: 8.38 us -> none  [the longest x1 2.59 us: layer_step(): (proj[:, 2 * width:] + bias_value).astype(BF16).reshape(cluster_shape)]
where the time goes in v2:
time: 471 us; the launch traced here: 468 us
  Pallas kernels  409 us (87%)
  local copies, waits for them, and re-layouts  38.6 us (8%)
  other arithmetic  19.3 us (4%)
    pallas_call x1, Pallas kernels, reduce_all(): pl.pallas_call(functools.partial(reduce_kernel, blks, heads), name='reduc...  212 us
    pallas_call x1, Pallas kernels, gather_all(): pl.pallas_call(functools.partial(gather_kernel, blks, heads), name='gathe...  117 us
    pallas_call x1, Pallas kernels, ffn_part(): pl.pallas_call(functools.partial(ffn_kernel, share), name='ffn_part', out...  43.5 us
    unnamed x41, local copies, waits for them, and re-layouts  24 us
    pallas_call x1, Pallas kernels, backward_part(): pl.pallas_call(backward_kernel, name='backward_part', out_shape=(jax.Shap...  22.5 us
    pallas_call x1, Pallas kernels, forward_part(): pl.pallas_call(forward_kernel, name='forward_part', out_shape=(jax.ShapeD...  14.9 us
    concatenate x1, other arithmetic, body(): jnp.concatenate([partial_attn, partial_ffn], axis=2).reshape(full.shape)  12.5 us

profile of v2, /device:TPU:8, one launch (start us, length us, event | category | flops | bytes accessed | tf_op | source)
XLA Modules:
  0.0 467.9 jit_solution(16384776258455960490)
XLA Ops:
  0.6 1.1 fusion.2
  2.1 1.1 concatenate.18.shard
  5.7 1.1 copy-done.10
  6.9 1.1 copy-done.11
  8.0 116.5 %gather_all.1 = (bf16[4,8,96,2304]{3,2,1,0:T(8,128)(2,1)S(1)}, bf16[8,16,128]{2,1,0:T(8,128)(2,1)S(1)}, bf16[4,256,384]{2,1,0:T(8,128)(2,1)S(1)}, bf16[4,256,384...) custom-call(bf16[2,256,768]{2,1,0:T(8,128)(2,1)S(1)} %copy-done.10, ...), custom_call_target="tpu_custom_call" | custom-call | tf_op jit(solution)/shard_map/gather_all/pallas_call | solution.py:465
  124.6 4.9 %copy-done = bf16[4,8,96,2304]{3,2,1,0:T(8,128)(2,1)} copy-done((bf16[4,8,96,2304]{3,2,1,0:T(8,128)(2,1)}, bf16[4,8,96,2304]{3,2,1,0:T(8,128)(2,1)S(1)}, u32[]{:S(2)}) %copy-start) | copy-done | bytes 14155800
  129.5 0.9 copy-done.1
  134.9 2.8 select_reduce_fusion
  137.9 1.1 copy-done.3
  139.1 14.9 %forward_part.1 = (bf16[512,768]{1,0:T(8,128)(2,1)S(1)}, bf16[512,2304]{1,0:T(8,128)(2,1)}, bf16[4,6,256,128]{3,2,1,0:T(8,128)(2,1)S(1)}, bf16[512,768]{1,0:T(8,...) custom-call(bf16[4,256,384]{2,1,0:T(8,128)(2,1)S(1)} %copy-done.3, ...), custom_call_target="tpu_custom_call" | custom-call | tf_op jit(solution)/shard_map/forward_part/pallas_call | solution.py:1001
  154.8 0.9 copy-done.7
  157.3 43.5 %ffn_part.1 = (bf16[4,256,384]{2,1,0:T(8,128)(2,1)}, f32[512,768]{1,0:T(8,128)}, bf16[512,768]{1,0:T(8,128)(2,1)}, bf16[4,768,1536]{2,1,0:T(8,128)(2,1)}, f32[8,768]{1,0:T(8,128)}, /*index=5*/f32[1,3072]{1,0:T(1,128)}) custom-call(f32[512,768]{1,0:T(8,128)} %get-tuple-element.44.attn_res, bf16[4,256,384]{2,1,0:T(8,128)(2,1)} %copy-done.1, ...), custom_call_target="tpu_custom_call" | custom-call | tf_op jit(solution)/shard_map/ffn_part/pallas_call | solution.py:1181
  200.8 1.1 copy-done.8
  201.9 1.1 copy-done.9
  203.1 22.5 %backward_part.1 = (bf16[4,256,384]{2,1,0:T(8,128)(2,1)S(1)}, bf16[4,768,768]{2,1,0:T(8,128)(2,1)}, f32[8,768]{1,0:T(8,128)S(1)}) custom-call(bf16[512,768]{1,0:T(8,128)(2,1)S(1)} %copy-done.6, bf16[512,2304]{1,0:T(8,128)(2,1)} %get-tuple-element.48.proj, bf16[4,6,256,128]{3,2,1,0:T(8,128)(2,1)S(1)} %get-tuple-element.49.probs, ...), custom_call_target="tpu_custom_call" | custom-call | tf_op jit(solution)/shard_map/backward_part/pallas_call | solution.py:1315
  227.8 1.4 reduce.11
  229.9 12.5 %pad_maximum_fusion = bf16[4,768,2304]{2,1,0:T(8,128)(2,1)} fusion(bf16[4,768,1536]{2,1,0:T(8,128)(2,1)} %get-tuple-element.57, bf16[4,768,768]{2,1,0:T(8,128)(2,1)} %get-tuple-element.56), kind=kLoop, calls=%fused_computation.1 | loop fusion | flops 28311552 | bytes 28311552 | tf_op jit(solution)/shard_map/concatenate | solution.py:1435
  242.4 211.8 %reduce_all.1 = (bf16[2,256,768]{2,1,0:T(8,128)(2,1)}, f32[2,256,768]{2,1,0:T(8,128)}, f32[96,2304]{1,0:T(8,128)}, f32[16,128]{1,0:T(8,128)}) custom-call(bf16[4,256,384]{2,1,0:T(8,128)(2,1)} %get-tuple-element.46.layer_out, bf16[4,256,384]{2,1,0:T(8,128)(2,1)} %copy-done.4, bf16[4,8,96,2304]{3,2,1,0:T(8,128)(2,1)} %bitcast.40, ...), custom_call_target="tpu_custom_call" | custom-call | tf_op jit(solution)/shard_map/reduce_all/pallas_call | solution.py:833
  454.2 1.9 fusion.1
  457.0 1.7 slice.104
  458.7 1.7 slice.97
  460.4 1.5 slice_bitcast_fusion.1
  463.2 2.1 copy.64
  465.3 2.7 copy.65
  (60 shorter events, 15.1 us)
Async XLA Ops:
  5.7 1.1 copy-start.10
  6.9 1.1 copy-start.11
  124.5 4.9 %copy-start = (bf16[4,8,96,2304]{3,2,1,0:T(8,128)(2,1)}, bf16[4,8,96,2304]{3,2,1,0:T(8,128)(2,1)S(1)}, u32[]{:S(2)}) copy-start(bf16[4,8,96,2304]{3,2,1,0:T(8,128)(2,1)S(1)} %get-tuple-element.42) | copy-start | bytes 42467332
  129.5 0.9 copy-start.1
  130.4 0.9 copy-start.2
  131.3 0.8 copy-start.12
  132.0 0.8 copy-start.13
  132.8 0.6 copy-start.15
  133.8 20.2 %copy-start.14 = (f32[8,768]{1,0:T(8,128)}, f32[8,768]{1,0:T(8,128)S(1)}, u32[]{:S(2)}) copy-start(f32[8,768]{1,0:T(8,128)S(1)} %reshape.76.vectors) | copy-start | bytes 73732
  137.9 1.1 copy-start.3
  154.0 0.9 copy-start.5
  154.8 0.9 copy-start.7
  155.7 45.0 %copy-start.6 = (bf16[512,768]{1,0:T(8,128)(2,1)S(1)}, bf16[512,768]{1,0:T(8,128)(2,1)}, u32[]{:S(2)}) copy-start(bf16[512,768]{1,0:T(8,128)(2,1)} %copy-done.5) | copy-start | bytes 2359300
  200.8 1.1 copy-start.8
  201.9 1.1 copy-start.9
  225.6 0.9 copy-start.4

commit v3 on v2

--- a/solution.py
+++ b/solution.py
@@ -1,4 +1,5 @@
 import functools
+import types
 
 import jax
 import jax.numpy as jnp
@@ -58,7 +59,8 @@
         self.pending.append((make, when))
 
     def finish(self):
-        for make, when in self.pending:
+        pending, self.pending = self.pending, []
+        for make, when in pending:
             if when is None:
                 make().wait_send()
             else:
@@ -1332,6 +1334,852 @@
     )(x, proj, probs, context, qkv, out, d_attn, g_attn)
 
 
+def fused_scratch(micros, rows, width, blks, heads, share, fold):
+    dma = pltpu.SemaphoreType.DMA
+    vmem = pltpu.VMEM
+    tokens = micros * rows
+    part = width * micros // heads
+    group = rows * heads
+    ff = width * fold
+    half = width // 2
+    kept = blks // 2
+    levels = blks.bit_length() - 1
+    return dict(
+        arrived=vmem((2, group, part), BF16),
+        sorted_rows=vmem((2, group, part), BF16),
+        landed=vmem((2, group, part), BF16),
+        ordered=vmem((2, group, part), BF16),
+        slots=vmem((2, heads, rows, part), BF16),
+        dest_row=vmem((8, group), jnp.int32),
+        slot_row=vmem((8, group), jnp.int32),
+        dest_col=vmem((group, 128), jnp.int32),
+        slot_col=vmem((group, 128), jnp.int32),
+        ones=vmem((blks, group), F32),
+        sums=vmem((blks, group), F32),
+        rank_rows=vmem((blks, group), jnp.int32),
+        seg_col=vmem((tokens, 128), F32),
+        seg_row=vmem((8 * (-(-tokens // CLUSTER // 8)), CLUSTER), F32),
+        packed=vmem((heads, width, 3 * width), BF16),
+        qkv=vmem((width, 3 * width), BF16),
+        out=vmem((width, width), BF16),
+        down=vmem((ff, width), BF16),
+        full_vectors=vmem((blks, 16, 128), BF16),
+        vectors=vmem((8, width), F32),
+        bias_qkv=vmem((1, 3 * width), F32),
+        up_bias=vmem((1, ff), F32),
+        vec_grads=vmem((8, width), F32),
+        up_bias_grad=vmem((1, ff), F32),
+        x=vmem((tokens, width), BF16),
+        proj=vmem((tokens, 3 * width), BF16),
+        probs=vmem((tokens // CLUSTER, width // 128, 2 * CLUSTER, CLUSTER), BF16),
+        context=vmem((tokens, width), BF16),
+        attn_res=vmem((tokens, width), F32),
+        normed=vmem((tokens, width), F32),
+        hidden=vmem((tokens, width), BF16),
+        turned=vmem((width, tokens), BF16),
+        active=vmem((tokens, ff), BF16),
+        slope=vmem((tokens, ff), BF16),
+        ffn_res=vmem((tokens, width), F32),
+        g_down=vmem((tokens, width), BF16),
+        g_attn=vmem((tokens, width), BF16),
+        staged=vmem((2, kept, share, width), BF16),
+        from_tree=vmem((3, 2, heads, kept - 1, share, half), BF16),
+        from_left=vmem((3, heads, share, width), BF16),
+        from_right=vmem((3, heads, share, width), BF16),
+        vec_split=vmem((blks, 16, 128), F32),
+        vec_parts=vmem((blks, 16, 128), F32),
+        vec_mid=vmem((16, 128), F32),
+        vec_heads=vmem((heads, 16, 128), F32),
+        head_send=dma((4, 2, heads)),
+        head_recv=dma((4, 2, heads)),
+        blk_send=dma((4, blks)),
+        blk_recv=dma((4, blks)),
+        local=dma((4, 3)),
+        z_send=dma((2, heads, 2)),
+        z_recv=dma((2, heads)),
+        tree_send=dma((2, heads, 2, blks)),
+        tree_recv=dma((2, heads, 2, blks)),
+        gain_send=dma((blks,)),
+        gain_recv=dma((blks,)),
+        own_sem=dma((2,)),
+        core_send=dma((3, heads, kept)),
+        core_recv=dma((3, heads, kept)),
+        stage_sem=dma((3, heads)),
+        down_send=dma((3, 2, heads, kept)),
+        down_recv=dma((3, 2, heads, kept)),
+        left_send=dma((3, heads)),
+        left_recv=dma((3, heads)),
+        right_send=dma((3, heads)),
+        right_recv=dma((3, heads)),
+        vec_send=dma((blks,)),
+        vec_recv=dma((blks,)),
+        vec_head_send=dma((heads,)),
+        vec_head_recv=dma((heads,)),
+        out_sem=dma((3, max(heads, 3))),
+    )
+
+
+def fused_kernel(names, blks, heads, share, fold, *refs):
+    r = types.SimpleNamespace(**dict(zip(names, refs)))
+    blk, head = lax.axis_index("blk"), lax.axis_index("head")
+    micros, rows, width = r.tokens.shape
+    tokens = micros * rows
+    splits = heads // micros
+    part = width // splits
+    group = rows * heads
+    pair = group // blks
+    ff = width * fold
+    short = width // heads
+    levels = blks.bit_length() - 1
+    bits = bits_of(blk, levels)
+    sends = Sends()
+    sems = (r.head_send, r.head_recv, r.blk_send, r.blk_recv, r.local)
+    exchanges = [RowExchange(sends, blk, head, blks, heads, sems, i) for i in range(4)]
+
+    def tiles(count, size):
+        def run(body):
+            @pl.loop(0, count)
+            def _(tile):
+                body(tile, pl.ds(pl.multiple_of(tile * size, size), size))
+
+        return run
+
+    row_tiles = tiles(tokens // CLUSTER, CLUSTER)
+
+
+    def head_block(ref, i):
+        return lambda other: ref.at[i, pl.ds(pl.multiple_of(other * rows, rows), rows), :]
+
+    def blk_block(ref, i):
+        return lambda other: ref.at[i, pl.ds(pl.multiple_of(other * pair, pair), pair), :]
+
+    def row_source(ref):
+        return lambda other: ref.at[
+            other // splits, :, (other % splits) * part : (other % splits + 1) * part
+        ]
+
+    def own_rows(ref):
+        return lambda other: ref.at[
+            other // splits * rows : (other // splits + 1) * rows,
+            (other % splits) * part : (other % splits + 1) * part,
+        ]
+
+    def to_heads(i, source):
+        exchanges[i].over_head(0, source, head_block(r.arrived, i % 2))
+
+    def to_groups(i, one_hot):
+        exchanges[i].wait_head(0, head_block(r.arrived, i % 2))
+        permute_rows(one_hot, r.arrived.at[i % 2], r.sorted_rows.at[i % 2], group)
+        exchanges[i].over_blk(blk_block(r.sorted_rows, i % 2), blk_block(r.landed, i % 2))
+
+    def to_owners(i, one_hot):
+        exchanges[i].wait_blk(blk_block(r.landed, i % 2))
+        permute_rows(one_hot, r.landed.at[i % 2], r.ordered.at[i % 2], group)
+        exchanges[i].over_head(
+            1, head_block(r.ordered, i % 2), lambda other: r.slots.at[i % 2, other]
+        )
+
+    def rows_here(i):
+        exchanges[i].wait_head(1, lambda other: r.slots.at[i % 2, other])
+
+
+    parts = ((0, width), (width, 2 * width))
+    orders = [list(range(1, levels)) + [0], list(range(2, levels)) + [1, 0]]
+    arrival = [
+        choose(
+            head,
+            [
+                sorted([x for x in range(heads) if x != own], key=lambda x: (abs(x - own), x))[j - 1]
+                for own in range(heads)
+            ],
+        )
+        if j
+        else head
+        for j in range(heads)
+    ]
+
+    def piece_rows(piece):
+        return pl.ds(pl.multiple_of(piece * share, share), share)
+
+    def part_cols(p, which=None):
+        base, size = parts[p]
+        if which is None:
+            return slice(base, base + size)
+        return slice(base + which * size // 2, base + (which + 1) * size // 2)
+
+    def tree_wait(p, j, which, step):
+        dims = orders[which]
+        other = flip(blk, 1 << dims[step], bits)
+        for mask in submasks(dims[:step]):
+            piece = flip(blk, mask | (1 << dims[step]), bits)
+            target = r.packed.at[arrival[j], piece_rows(piece), part_cols(p, which)]
+            remote(
+                target,
+                target,
+                r.tree_send.at[p, j, which, 0],
+                r.tree_recv.at[p, j, which, piece],
+                (other, head),
+            ).wait_recv()
+
+    def tree_step(p, j, step):
+        for which in range(2):
+            dims = orders[which]
+            if step:
+                tree_wait(p, j, which, step - 1)
+            if step == levels:
+                continue
+            other = flip(blk, 1 << dims[step], bits)
+            for index, mask in enumerate(submasks(dims[:step])):
+                piece = flip(blk, mask, bits)
+                target = r.packed.at[arrival[j], piece_rows(piece), part_cols(p, which)]
+                first = j == 0 and mask == 0
+                source = r.shard.at[:, part_cols(p, which)] if first else target
+                sends.start(
+                    lambda source=source, target=target, piece=piece, other=other, which=which, slot=(1 << step) - 1 + index: remote(
+                        source,
+                        target,
+                        r.tree_send.at[p, j, which, slot],
+                        r.tree_recv.at[p, j, which, piece],
+                        (other, head),
+                    )
+                )
+
+    def chain(p, j):
+        target = r.packed.at[arrival[j], piece_rows(blk), part_cols(p)]
+        if j == 0:
+            source = r.shard.at[:, part_cols(p)]
+            left, right = head > 0, head < heads - 1
+        else:
+            source = target
+            left = (arrival[j] > head) & (head > 0)
+            right = (arrival[j] < head) & (head < heads - 1)
+            remote(
+                target, target, r.z_send.at[p, 0, 0], r.z_recv.at[p, arrival[j]], (blk, head)
+            ).wait_recv()
+        for side, (condition, step) in enumerate(((left, -1), (right, 1))):
+            sends.start(
+                lambda side=side, step=step: remote(
+                    source,
+                    target,
+                    r.z_send.at[p, j, side],
+                    r.z_recv.at[p, arrival[j]],
+                    (blk, jnp.clip(head + step, 0, heads - 1)),
+                ),
+                when=condition,
+            )
+
+    def gain_copy(other, slot):
+        return remote(
+            r.small, r.full_vectors.at[slot], r.gain_send.at[other], r.gain_recv.at[slot], (other, head)
+        )
+
+
+    order = []
+    for i in range(heads):
+        order.append(heads - 1 - i // 2 if i % 2 == 0 else i // 2)
+    even = submasks(range(1, levels))
+    down_orders = [list(range(levels - 1, 0, -1)), [1] + list(range(levels - 1, 1, -1))]
+    sibling = flip(blk, 1, bits)
+
+    def group_cols(g, which=None):
+        if which is None:
+            return slice(g * width, (g + 1) * width)
+        return slice(g * width + which * width // 2, g * width + (which + 1) * width // 2)
+
+    def total(g, other, mask, which=None):
+        return r.packed.at[other, piece_rows(flip(blk, mask, bits)), group_cols(g, which)]
+
+    def core_start(g):
+        for other in order:
+            for mask in even:
+                sends.start(
+                    lambda other=other, mask=mask: remote(
+                        total(g, other, mask | 1),
+                        r.from_core.at[g, other, mask // 2],
+                        r.core_send.at[g, other, mask // 2],
+                        r.core_recv.at[g, other, mask // 2],
+                        (sibling, head),
+                    )
+                )
+
+    def core_load(g, i):
+        other = order[i]
+        return pltpu.make_async_copy(
+            r.from_core.at[g, other], r.staged.at[i % 2], r.stage_sem.at[g, i]
+        )
+
+    def core_arrived(g, i):
+        other = order[i]
+        for mask in even:
+            target = r.from_core.at[g, other, mask // 2]
+            remote(
+                target,
+                target,
+                r.core_send.at[g, other, mask // 2],
+                r.core_recv.at[g, other, mask // 2],
+                (sibling, head),
+            ).wait_recv()
+        core_load(g, i).start()
+
+    def core_add(g):
+        core_arrived(g, 0)
+        for i, other in enumerate(order):
+            if i + 1 < heads:
+                core_arrived(g, i + 1)
+            core_load(g, i).wait()
+            for mask in even:
+                add_into(total(g, other, mask), r.staged.at[i % 2, mask // 2], width)
+            tree_start(g, other, 0)
+
+    def tree_slots(which, step):
+        dims = down_orders[which]
+        base = sum(1 << (levels - 2 - earlier) for earlier in range(step))
+        return dims[step], [(mask, base + i) for i, mask in enumerate(submasks(dims[step + 1 :]))]
+
+    def tree_copy(g, other, which, dim, mask, slot):
+        return remote(
+            total(g, other, mask | (1 << dim), which),
+            r.from_tree.at[g, which, other, slot],
+            r.down_send.at[g, which, other, slot],
+            r.down_recv.at[g, which, other, slot],
+            (flip(blk, 1 << dim, bits), head),
+        )
+
+    def tree_start(g, other, step):
+        for which in range(2):
+            dim, slots = tree_slots(which, step)
+            for mask, slot in slots:
+                sends.start(
+                    lambda which=which, dim=dim, mask=mask, slot=slot: tree_copy(
+                        g, other, which, dim, mask, slot
+                    )
+                )
+
+    def tree_add(g, other, step):
+        for which in range(2):
+            dim, slots = tree_slots(which, step)
+            for mask, slot in slots:
+                tree_copy(g, other, which, dim, mask, slot).wait_recv()
+                add_into(
+                    total(g, other, mask, which), r.from_tree.at[g, which, other, slot], width // 2
+                )
+        if step < levels - 2:
+            tree_start(g, other, step + 1)
+
+    def tree_down(g, step):
+        for other in order:
+            tree_add(g, other, step)
+
+    def pass_on(g, goal):
+        for target, send_sem, recv_sem, step in (
+            (r.from_left.at[g, goal], r.left_send, r.left_recv, 1),
+            (r.from_right.at[g, goal], r.right_send, r.right_recv, -1),
+        ):
+            if step == 1:
+                arrives = (head > 0) & (head <= goal)
+                leaves = head < goal
+            else:
+                arrives = (head < heads - 1) & (head >= goal)
+                leaves = head > goal
+
+            @pl.when(arrives)
+            def _(target=target, send_sem=send_sem, recv_sem=recv_sem):
+                remote(
+                    target, target, send_sem.at[g, goal], recv_sem.at[g, goal], (blk, head)
+                ).wait_recv()
+                add_into(total(g, goal, 0), target, width)
+
+            sends.start(
+                lambda target=target, send_sem=send_sem, recv_sem=recv_sem, step=step: remote(
+                    total(g, goal, 0),
+                    target,
+                    send_sem.at[g, goal],
+                    recv_sem.at[g, goal],
+                    (blk, jnp.clip(head + step, 0, heads - 1)),
+                ),
+                when=leaves,
+            )
+
+
+    micro = head // splits
+
+    def find_destinations():
+        own_slots = r.perm[micro, pl.ds(blk, 1), :]
+        r.ones[...] = jnp.where(iota((blks, group), 0) == own_slots // group, 1.0, 0.0)
+        cumulative(r.ones, r.sums, group)
+        rank = column_sum(r.ones[...] * r.sums[...]).astype(jnp.int32) - 1
+        dest = own_slots // group * pair + rank
+        r.dest_row[...] = jnp.broadcast_to(dest, r.dest_row.shape)
+        for tile in range(group // 128):
+            block = jnp.broadcast_to(dest[:, tile * 128 : (tile + 1) * 128].astype(F32), (128, 128))
+            r.dest_col[tile * 128 : (tile + 1) * 128, :] = block.T.astype(jnp.int32)
+
+    def find_slots():
+        r.ones[...] = jnp.where(r.perm[micro] // group == blk, 1.0, 0.0)
+        cumulative(r.ones, r.sums, group)
+        r.rank_rows[...] = jnp.where(r.ones[...] > 0, r.sums[...] - 1, -1.0).astype(jnp.int32)
+
+        @pl.loop(0, blks)
+        def _(other):
+            ranks = r.rank_rows[pl.ds(other, 1), :]
+            inner = (r.perm[micro, pl.ds(other, 1), :] % group).astype(F32)
+            found = jnp.where(iota((pair, group), 0) == ranks, inner, 0.0)
+            column = jnp.sum(found, axis=1, keepdims=True).astype(jnp.int32)
+            r.slot_col[pl.ds(pl.multiple_of(other * pair, pair), pair), :] = jnp.broadcast_to(
+                column, (pair, 128)
+            )
+
+        for tile in range(group // 128):
+            block = r.slot_col[tile * 128 : (tile + 1) * 128, :].astype(F32)
+            r.slot_row[:, tile * 128 : (tile + 1) * 128] = block.T[0:8, :].astype(jnp.int32)
+
+    def find_segments():
+        first = blk * group + head * rows
+        for m in range(micros):
+            ends = []
+            for s in range(r.seq_lengths.shape[1]):
+                ends.append(r.seq_lengths[m, s] + (ends[-1] if ends else 0))
+            for tile in range(rows // CLUSTER):
+                slot = iota((CLUSTER, group), 0) + (first + tile * CLUSTER)
+
+                def add(other, sums):
+                    position = iota((1, group), 1) + other * group
+                    segment = jnp.zeros((1, group), F32)
+                    for end in ends:
+                        segment = segment + jnp.where(position >= end, 1.0, 0.0)
+                    here = r.perm[m, pl.ds(other, 1), :] == slot
+                    found = jnp.where(here, segment, 0.0)
+                    return sums + sum(
+                        found[:, i * 128 : (i + 1) * 128] for i in range(group // 128)
+                    )
+
+                sums = lax.fori_loop(0, blks, add, jnp.zeros((CLUSTER, 128), F32))
+                column = jnp.broadcast_to(
+                    jnp.sum(sums, axis=1, keepdims=True), (CLUSTER, 128)
+                )
+                cluster = m * (rows // CLUSTER) + tile
+                r.seg_col[cluster * CLUSTER : (cluster + 1) * CLUSTER, :] = column
+                r.seg_row[cluster : cluster + 1, :] = column.T[0:1, :]
+
+    def spread_vectors():
+        for b in range(blks):
+            small = r.full_vectors[b].astype(F32)
+            r.vectors[:, b * share : (b + 1) * share] = small[0:8, 0:share]
+            for j in range(fold):
+                at = (b * fold + j) * share
+                r.up_bias[:, at : at + share] = small[8 + j : 9 + j, 0:share]
+        r.bias_qkv[:, 0:width] = r.vectors[0:1, :]
+        r.bias_qkv[:, width : 2 * width] = jnp.zeros((1, width), F32)
+        r.bias_qkv[:, 2 * width :] = r.vectors[1:2, :]
+
+
+    def take_rows():
+        for source in range(heads):
+            m, which = source // splits, source % splits
+            r.x[m * rows : (m + 1) * rows, which * part : (which + 1) * part] = r.slots[0, source]
+
+    def assemble_down():
+        @pl.loop(0, width // share)
+        def _(b):
+            source = piece_rows(b)
+            for j in range(fold):
+                at = b * share * fold + j * share
+                target = pl.ds(pl.multiple_of(at, share), share)
+                for h in range(heads):
+                    base = 2 * width + j * short
+                    r.down[target, h * short : (h + 1) * short] = r.packed[
+                        h, source, base : base + short
+                    ]
+
+    per_head = width // 256
+
+    def first_norm():
+        @row_tiles
+        def _(tile, at):
+            normal, _ = normalize(r.attn_res[at, :])
+            values = normal * r.vectors[3:4, :] + r.vectors[4:5, :]
+            r.normed[at, :] = values
+            r.hidden[at, :] = values.astype(BF16)
+
+        r.turned[...] = r.hidden[...].T
+
+    def ffn_up(h):
+        @tiles(per_head, 256)
+        def _(tile, inner):
+            inner = pl.ds(pl.multiple_of(width + tile * 256, 256), 256)
+            cols = pl.ds(pl.multiple_of(h * width + tile * 256, 256), 256)
+            pre = jnp.dot(r.hidden[...], r.packed[h, :, inner], preferred_element_type=F32)
+            pre = pre + r.up_bias[:, cols]
+            below = 0.5 + 0.5 * lax.erf(pre * (0.5**0.5))
+            r.active[:, cols] = (pre * below).astype(BF16)
+            bell = jnp.exp(-0.5 * pre * pre) * (0.5 / jnp.pi) ** 0.5
+            r.slope[:, cols] = (below + pre * bell).astype(BF16)
+
+    def ffn_down():
+        @tiles(width // 256, 256)
+        def _(tile, cols):
+            sums = jnp.dot(r.active[...], r.down[:, cols], preferred_element_type=F32)
+            r.ffn_res[:, cols] = r.normed[:, cols] + sums + r.vectors[5:6, cols]
+
+    def inner_rows(tile):
+        return tile * CLUSTER // rows, pl.ds(pl.multiple_of(tile * CLUSTER % rows, CLUSTER), CLUSTER)
+
+    def second_norm():
+        @row_tiles
+        def _(tile, at):
+            normal, _ = normalize(r.ffn_res[at, :])
+            result = (normal * r.vectors[6:7, :] + r.vectors[7:8, :]).astype(BF16)
+            r.hidden[at, :] = result
+
+    def second_norm_back():
+        @row_tiles
+        def _(tile, at):
+            normal, scale = normalize(r.ffn_res[at, :])
+            m, inner = inner_rows(tile)
+            cotangent = jnp.concatenate(
+                [r.slots[1, m * splits + which, inner, :] for which in range(splits)], axis=1
+            ).astype(F32)
+            d_ffn = norm_derivative(normal, scale, cotangent, r.vectors[6:7, :])
+            low = d_ffn.astype(BF16)
+            r.g_down[at, :] = low
+            r.ffn_res[at, :] = d_ffn
+            r.vec_grads[5:6, :] += column_sum(low.astype(F32))
+            r.vec_grads[6:7, :] += column_sum(cotangent * normal)
+            r.vec_grads[7:8, :] += column_sum(cotangent)
+
+    def down_gradient():
+        @pl.loop(0, width // share)
+        def _(b):
+            wide = share * fold
+            cols = pl.ds(pl.multiple_of(b * wide, wide), wide)
+            turned = r.active[:, cols].T
+            target = piece_rows(b)
+            for which in range(2):
+                grad = jnp.dot(
+                    turned,
+                    r.g_down[:, which * width // 2 : (which + 1) * width // 2],
+                    preferred_element_type=F32,
+                ).astype(BF16)
+                for j in range(fold):
+                    for h in range(heads // 2):
+                        base = 2 * width + j * short
+                        r.packed[which * heads // 2 + h, target, base : base + short] = grad[
+                            j * share : (j + 1) * share, h * short : (h + 1) * short
+                        ]
+
+    def ffn_up_back():
+        @tiles(ff // 256, 256)
+        def _(tile, cols):
+            d_active = contract(r.g_down[...], r.down[cols, :], (1, 1))
+            low = (d_active * r.slope[:, cols].astype(F32)).astype(BF16)
+            r.slope[:, cols] = low
+            r.up_bias_grad[:, cols] = column_sum(low.astype(F32))
+
+    def norm_cotangent():
+        @tiles(width // 256, 256)
+        def _(tile, cols):
+            sums = r.ffn_res[:, cols]
+            for h in range(heads):
+                sums = sums + contract(
+                    r.slope[:, h * width : (h + 1) * width],
+                    r.packed[h, cols, width : 2 * width],
+                    (1, 1),
+                )
+            r.normed[:, cols] = sums
+
+    def up_gradient():
+        @tiles(ff // 256, 256)
+        def _(tile, cols):
+            inner = pl.ds(pl.multiple_of(width + tile % per_head * 256, 256), 256)
+            grad = jnp.dot(r.turned[...], r.slope[:, cols], preferred_element_type=F32)
+            r.packed[tile // per_head, :, inner] = grad.astype(BF16)
+
+    def first_norm_back():
+        @row_tiles
+        def _(tile, at):
+            normal, scale = normalize(r.attn_res[at, :])
+            cotangent = r.normed[at, :]
+            grad = norm_derivative(normal, scale, cotangent, r.vectors[3:4, :])
+            low = grad.astype(BF16)
+            r.attn_res[at, :] = grad
+            r.g_attn[at, :] = low
+            r.vec_grads[2:3, :] += column_sum(low.astype(F32))
+            r.vec_grads[3:4, :] += column_sum(cotangent * normal)
+            r.vec_grads[4:5, :] += column_sum(cotangent)
+
+    g_context = r.g_down
+    x_grad = r.g_down
+    g_proj = r.active
+    wide = 3 * width // heads
+
+    def out_gradient():
+        r.turned[...] = r.context[...].T
+        for h in range(heads):
+            grad = jnp.dot(
+                r.turned[...],
+                r.g_attn[:, h * short : (h + 1) * short],
+                preferred_element_type=F32,
+            )
+            r.packed[h, :, wide : wide + short] = grad.astype(BF16)
+
+    def context_cotangent():
+        @tiles(width // 256, 256)
+        def _(tile, cols):
+            g_context[:, cols] = contract(r.g_attn[...], r.out[cols, :], (1, 1)).astype(BF16)
+
+    def qkv_gradient():
+        r.turned[...] = r.x[...].T
+
+        @tiles(width // 256, 256)
+        def _(tile, at):
+            for h in range(heads):
+                grad = jnp.dot(
+                    r.turned[at, :], g_proj[:, h * wide : (h + 1) * wide], preferred_element_type=F32
+                )
+                r.packed[h, at, 0:wide] = grad.astype(BF16)
+
+        r.vec_grads[0:1, :] = column_sum(g_proj[:, 0:width].astype(F32))
+        r.vec_grads[1:2, :] = column_sum(g_proj[:, 2 * width : 3 * width].astype(F32))
+
+    def row_gradient():
+        for which in range(splits):
+            for piece in range(part // 128):
+                at = which * part + piece * 128
+                sums = r.attn_res[:, at : at + 128] + contract(
+                    g_proj[:, 0 : 3 * width], r.qkv[at : at + 128, :], (1, 1)
+                )
+                x_grad[:, at : at + 128] = sums.astype(BF16)
+
+
+    def split_vectors():
+        r.vec_split[...] = jnp.zeros_like(r.vec_split)
+        for b in range(blks):
+            r.vec_split[b, 0:8, 0:share] = r.vec_grads[:, b * share : (b + 1) * share]
+            for j in range(fold):
+                at = (b * fold + j) * share
+                r.vec_split[b, 8 + j : 9 + j, 0:share] = r.up_bias_grad[:, at : at + share]
+
+    def vec_copy(other, slot):
+        return remote(
+            r.vec_split.at[other],
+            r.vec_parts.at[slot],
+            r.vec_send.at[other],
+            r.vec_recv.at[slot],
+            (other, head),
+        )
+
+    def vec_head_copy(other, slot):
+        return remote(
+            r.vec_mid,
+            r.vec_heads.at[slot],
+            r.vec_head_send.at[other],
+            r.vec_head_recv.at[slot],
+            (blk, other),
+        )
+
+
+    enter(blk, head, blks, heads)
+    to_heads(0, row_source(r.tokens))
+    for other in range(blks):
+        sends.start(lambda other=other: gain_copy(other, blk), when=other != blk)
+    own_gain = pltpu.make_async_copy(r.small, r.full_vectors.at[blk], r.own_sem.at[0])
+    own_gain.start()
+    for p in range(2):
+        tree_step(p, 0, 0)
+        chain(p, 0)
+    own_shard = pltpu.make_async_copy(r.shard, r.packed.at[head, piece_rows(blk), :], r.own_sem.at[1])
+    own_shard.start()
+    find_destinations()
+    to_groups(0, one_hot_from_row(r.dest_row))
+    to_heads(1, row_source(r.out_grad))
+    tree_step(0, 0, 1)
+    chain(0, 1)
+    tree_step(0, 1, 0)
+    find_slots()
+    tree_step(0, 0, 2)
+    tree_step(0, 1, 1)
+    chain(0, 2)
+    tree_step(0, 2, 0)
+    to_owners(0, one_hot_from_row(r.slot_row))
+    find_segments()
+    tree_step(0, 1, 2)
+    tree_step(0, 2, 1)
+    chain(0, 3)
+    tree_step(0, 3, 0)
+    tree_step(1, 0, 1)
+    chain(1, 1)
+    tree_step(1, 1, 0)
+    tree_step(0, 2, 2)
+    tree_step(0, 3, 1)
+    to_groups(1, one_hot_from_row(r.dest_row))
+    tree_step(1, 0, 2)
+    tree_step(1, 1, 1)
+    tree_step(0, 3, 2)
+    for other in range(blks):
+
+        @pl.when(other != blk)
+        def _():
+            gain_copy(other, other).wait_recv()
+
+    own_gain.wait()
+    own_shard.wait()
+    spread_vectors()
+    for j in range(heads):
+        tree_step(0, j, 3)
+    assemble_attention(r.packed, r.qkv, r.out)
+    chain(1, 2)
+    tree_step(1, 2, 0)
+    rows_here(0)
+    take_rows()
+    project(r.x, r.qkv, r.bias_qkv, r.proj)
+    tree_step(1, 1, 2)
+    tree_step(1, 2, 1)
+    chain(1, 3)
+    tree_step(1, 3, 0)
+    to_owners(1, one_hot_from_row(r.slot_row))
+    attend(r.proj, r.probs, r.context, r.seg_col, r.seg_row)
+    tree_step(1, 2, 2)
+    tree_step(1, 3, 1)
+    leave_attention(r.x, r.context, r.out, r.vectors, r.attn_res)
+    first_norm()
+    tree_step(1, 0, 3)
+    ffn_up(arrival[0])
+    tree_step(1, 3, 2)
+    tree_step(1, 1, 3)
+    ffn_up(arrival[1])
+    tree_step(1, 2, 3)
+    ffn_up(arrival[2])
+    tree_step(1, 3, 3)
+    ffn_up(arrival[3])
+    assemble_down()
+    ffn_down()
+    second_norm()
+    sends.finish()
+    to_heads(2, own_rows(r.hidden))
+    r.vec_grads[...] = jnp.zeros_like(r.vec_grads)
+    rows_here(1)
+    second_norm_back()
+    down_gradient()
+    core_start(2)
+    ffn_up_back()
+    norm_cotangent()
+    core_add(2)
+    up_gradient()
+    core_start(1)
+    to_groups(2, one_hot_from_column(r.slot_col, group))
+    first_norm_back()
+    tree_down(2, 0)
+    context_cotangent()
+    core_add(1)
+    attend_back(r.proj, r.probs, g_context, g_proj)
+    tree_down(2, 1)
+    row_gradient()
+    to_heads(3, own_rows(x_grad))
+    to_owners(2, one_hot_from_column(r.dest_col, group))
+    tree_down(1, 0)
+    out_gradient()
+    qkv_gradient()
+    core_start(0)
+    split_vectors()
+    for other in range(blks):
+        sends.start(lambda other=other: vec_copy(other, blk), when=other != blk)
+    for i in range(heads):
+        pass_on(2, order[i])
+    tree_down(1, 1)
+    core_add(0)
+    to_groups(3, one_hot_from_column(r.slot_col, group))
+    for i in range(heads):
+        pass_on(1, order[i])
+    tree_down(0, 0)
+    r.vec_mid[...] = r.vec_split[pl.ds(blk, 1)][0]
+    for other in range(blks):
+
+        @pl.when(other != blk)
+        def _():
+            vec_copy(other, other).wait_recv()
+            r.vec_mid[...] += r.vec_parts[other]
+
+    for other in range(heads):
+        sends.start(lambda other=other: vec_head_copy(other, head), when=other != head)
+    to_owners(3, one_hot_from_column(r.dest_col, group))
+    tree_down(0, 1)
+    for i in range(heads):
+        pass_on(0, order[i])
+
+    def out_copy(source):
+        m, which = source // splits, source % splits
+        return pltpu.make_async_copy(
+            r.slots.at[0, source],
+            r.out_rows.at[m, :, which * part : (which + 1) * part],
+            r.out_sem.at[0, source],
+        )
+
+    rows_here(2)
+    for source in range(heads):
+        out_copy(source).start()
+    r.vec_sum[...] = r.vec_mid[...]
+    for other in range(heads):
+
+        @pl.when(other != head)
+        def _():
+            vec_head_copy(other, other).wait_recv()
+            r.vec_sum[...] += r.vec_heads[other]
+
+    copies = []
+    for g in range(3):
+        at = slice(g * share, (g + 1) * share)
+        r.ffn_res[at, :] = r.packed[head, piece_rows(blk), group_cols(g)].astype(F32)
+        copies.append(
+            pltpu.make_async_copy(
+                r.ffn_res.at[at, :], r.shard_grad.at[:, group_cols(g)], r.out_sem.at[1, g]
+            )
+        )
+        copies[-1].start()
+    rows_here(3)
+    for m in range(micros):
+        at = slice(m * rows, (m + 1) * rows)
+        for which in range(splits):
+            r.normed[at, which * part : (which + 1) * part] = r.slots[
+                1, m * splits + which
+            ].astype(F32)
+        copies.append(
+            pltpu.make_async_copy(r.normed.at[at, :], r.grad_rows.at[m], r.out_sem.at[2, m])
+        )
+        copies[-1].start()
+    for source in range(heads):
+        out_copy(source).wait()
+    for copy in copies:
+        copy.wait()
+    sends.finish()
+
+
+def fused(blks, heads, fold, tokens, out_grad, shard, small, perm, seq_lengths):
+    micros, rows, width = tokens.shape
+    share = shard.shape[0]
+    scratch = fused_scratch(micros, rows, width, blks, heads, share, fold)
+    any_space, vmem = pl.BlockSpec(memory_space=pl.ANY), pl.BlockSpec(memory_space=pltpu.VMEM)
+    names = ["tokens", "out_grad", "shard", "small", "perm", "seq_lengths"]
+    names += ["out_rows", "grad_rows", "shard_grad", "vec_sum", "from_core"]
+    names += list(scratch)
+    return pl.pallas_call(
+        functools.partial(fused_kernel, names, blks, heads, share, fold),
+        name="fused",
+        out_shape=(
+            jax.ShapeDtypeStruct((micros, rows, width), BF16),
+            jax.ShapeDtypeStruct((micros, rows, width), F32),
+            jax.ShapeDtypeStruct(shard.shape, F32),
+            jax.ShapeDtypeStruct((16, 128), F32),
+            jax.ShapeDtypeStruct((3, heads, blks // 2, share, width), BF16),
+        ),
+        in_specs=[any_space] * 4 + [vmem, pl.BlockSpec(memory_space=pltpu.SMEM)],
+        out_specs=(any_space, any_space, any_space, vmem, any_space),
+        scratch_shapes=list(scratch.values()),
+        compiler_params=pltpu.CompilerParams(
+            collective_id=2, has_side_effects=True, vmem_limit_bytes=64 << 20
+        ),
+    )(tokens, out_grad, shard, small, perm, seq_lengths)[:4]
+
+
 def refold(packed, share, other, fold):
     if share == other:
         return packed
@@ -1392,56 +2240,61 @@
     count = stacked.shape[0]
     vectors = jnp.pad(stacked, ((0, -count % 16), (0, lanes - share)))
     perm = cluster_perm.reshape(micros, blks, group)
-    full, full_vectors, slots_x, slots_g, dest_col, slot_col = gather_all(
-        blks, heads, tokens, out_grad, shard, vectors, perm
-    )
-
-    first = blk * group + head * rows
-    slots = first + jnp.arange(rows, dtype=jnp.int32)
-    ends = jnp.cumsum(seq_lengths, axis=1)
-    positions = jnp.arange(total_rows, dtype=jnp.int32)
-    segs = jnp.sum((positions[None, :, None] >= ends[:, None, :]).astype(jnp.int32), axis=2)
-    slot_segs = jnp.sum(
-        jnp.where(cluster_perm[:, None, :] == slots[None, :, None], segs[:, None, :], 0), axis=2
-    )
-
-    weights = full.reshape(heads, blks * share, -1)
-    tall = share if share % 16 == 0 else width // 8
-    if tall != share:
-        weights = jnp.concatenate(
-            [weights[:, :, : edges[3]], refold(weights[:, :, edges[3] :], share, tall, folds)],
-            axis=2,
-        )
-    spread = full_vectors[:, :count, :share].astype(F32)
-    vecs = spread[:, :8].transpose(1, 0, 2).reshape(8, width)
-    up_vec = spread[:, 8:count].reshape(1, -1)
-    bias_qkv = jnp.concatenate([vecs[0:1], jnp.zeros((1, width), F32), vecs[1:2]], axis=1)
-    seg_col = jnp.broadcast_to(slot_segs.reshape(-1, 1), (micros * rows, 128))
-    seg_row = slot_segs.reshape(-1, CLUSTER)
-    x, proj, probs, context, attn_res, qkv, out = forward_part(
-        slots_x, weights, bias_qkv, vecs, seg_col, seg_row
-    )
-    layer_out, d_attn, g_attn, partial_ffn, vec_ffn, up_vec_grad = ffn_part(
-        tall, attn_res, slots_g, weights, vecs, up_vec
-    )
-    x_grad, partial_attn, vec_attn = backward_part(
-        heads, rows, x, proj, probs, context, qkv, out, d_attn, g_attn
-    )
-    if tall != share:
-        partial_ffn = jnp.concatenate(
-            [partial_ffn[:, :, :width], refold(partial_ffn[:, :, width:], tall, share, folds)],
-            axis=2,
-        )
-    partial = jnp.concatenate([partial_attn, partial_ffn], axis=2).reshape(full.shape)
-    vec_grads = vec_ffn + vec_attn
-    vec_parts = jnp.concatenate(
-        [vec_grads.reshape(8, blks, share).transpose(1, 0, 2), up_vec_grad.reshape(blks, folds, share)],
-        axis=1,
-    )
-    vec_parts = jnp.pad(vec_parts, ((0, 0), (0, -count % 16), (0, lanes - share)))
-    out_rows, grad_rows, shard_grad, vec_sum = reduce_all(
-        blks, heads, layer_out, x_grad, partial, vec_parts, dest_col, slot_col
-    )
+    if share % 16 == 0:
+        out_rows, grad_rows, shard_grad, vec_sum = fused(
+            blks, heads, folds, tokens, out_grad, shard, vectors, perm, seq_lengths
+        )
+    else:
+        full, full_vectors, slots_x, slots_g, dest_col, slot_col = gather_all(
+            blks, heads, tokens, out_grad, shard, vectors, perm
+        )
+
+        first = blk * group + head * rows
+        slots = first + jnp.arange(rows, dtype=jnp.int32)
+        ends = jnp.cumsum(seq_lengths, axis=1)
+        positions = jnp.arange(total_rows, dtype=jnp.int32)
+        segs = jnp.sum((positions[None, :, None] >= ends[:, None, :]).astype(jnp.int32), axis=2)
+        slot_segs = jnp.sum(
+            jnp.where(cluster_perm[:, None, :] == slots[None, :, None], segs[:, None, :], 0), axis=2
+        )
+
+        weights = full.reshape(heads, blks * share, -1)
+        tall = share if share % 16 == 0 else width // 8
+        if tall != share:
+            weights = jnp.concatenate(
+                [weights[:, :, : edges[3]], refold(weights[:, :, edges[3] :], share, tall, folds)],
+                axis=2,
+            )
+        spread = full_vectors[:, :count, :share].astype(F32)
+        vecs = spread[:, :8].transpose(1, 0, 2).reshape(8, width)
+        up_vec = spread[:, 8:count].reshape(1, -1)
+        bias_qkv = jnp.concatenate([vecs[0:1], jnp.zeros((1, width), F32), vecs[1:2]], axis=1)
+        seg_col = jnp.broadcast_to(slot_segs.reshape(-1, 1), (micros * rows, 128))
+        seg_row = slot_segs.reshape(-1, CLUSTER)
+        x, proj, probs, context, attn_res, qkv, out = forward_part(
+            slots_x, weights, bias_qkv, vecs, seg_col, seg_row
+        )
+        layer_out, d_attn, g_attn, partial_ffn, vec_ffn, up_vec_grad = ffn_part(
+            tall, attn_res, slots_g, weights, vecs, up_vec
+        )
+        x_grad, partial_attn, vec_attn = backward_part(
+            heads, rows, x, proj, probs, context, qkv, out, d_attn, g_attn
+        )
+        if tall != share:
+            partial_ffn = jnp.concatenate(
+                [partial_ffn[:, :, :width], refold(partial_ffn[:, :, width:], tall, share, folds)],
+                axis=2,
+            )
+        partial = jnp.concatenate([partial_attn, partial_ffn], axis=2).reshape(full.shape)
+        vec_grads = vec_ffn + vec_attn
+        vec_parts = jnp.concatenate(
+            [vec_grads.reshape(8, blks, share).transpose(1, 0, 2), up_vec_grad.reshape(blks, folds, share)],
+            axis=1,
+        )
+        vec_parts = jnp.pad(vec_parts, ((0, 0), (0, -count % 16), (0, lanes - share)))
+        out_rows, grad_rows, shard_grad, vec_sum = reduce_all(
+            blks, heads, layer_out, x_grad, partial, vec_parts, dest_col, slot_col
+        )
     down_grad = shard_grad[:, edges[3] : edges[4]]
     down_grad = jnp.concatenate(
         [down_grad[:, i * short : (i + 1) * short] for i in range(folds)], axis=0

time: 471 us -> 364 us (0.77)
  Pallas kernels: 409 us -> 345 us
  local copies, waits for them, and re-layouts: 38.6 us -> 18.1 us
  other arithmetic: 19.3 us -> 0.03 us
    pallas_call x5 -> x1, Pallas kernels: 409 us -> 345 us  [fused(): pl.pallas_call(functools.partial(fused_kernel, names, blks, heads, share,...]
    unnamed x41 -> x12, local copies, waits for them, and re-layouts: 24 us -> 4.77 us
    concatenate x3 -> x0, other arithmetic: 13.2 us -> none  [the longest x1 12.5 us: body(): jnp.concatenate([partial_attn, partial_ffn], axis=2).reshape(full.shape)]
where the time goes in v3:
time: 364 us
  Pallas kernels  345 us (95%)
  local copies, waits for them, and re-layouts  18.1 us (5%)
    pallas_call x1, Pallas kernels, fused(): pl.pallas_call(functools.partial(fused_kernel, names, blks, heads, share,...  345 us

profile of v3, /device:TPU:8, one launch (start us, length us, event | category | flops | bytes accessed | tf_op | source)
XLA Modules:
  0.0 363.9 jit_solution(11933947976378313208)
XLA Ops:
  0.6 0.8 reshape.39
  1.4 0.8 concatenate.10
  2.2 0.6 pad.4.refs_3_
  2.8 1.5 copy.43
  4.3 1.1 fusion.1
  5.4 0.1 copy.40
  5.5 0.1 copy.39
  5.6 0.1 copy.38
  5.7 0.1 copy.37
  5.8 1.9 concatenate.9.refs_2_
  7.7 345.1 %fused.1 = (bf16[2,256,768]{2,1,0:T(8,128)(2,1)}, f32[2,256,768]{2,1,0:T(8,128)}, f32[96,2304]{1,0:T(8,128)}, f32[16,128]{1,0:T(8,128)}, bf16[3,4,4,96,768]{4,3,2,1,0:T(8,128)(2,1)}) custom-call(bf16[2,256,768]{2,1,0:T(8,128)(2,1)} %refs_0_.1, bf16[2,256,768]{2,1,0:T(8,128)(2,1)} %refs_1_.1, bf16[96,2304]{1,0:T(8,128)(2,1)} %concatenate.9.refs_2_, ...), custom_call_target="tpu_custom_call" | custom-call | tf_op jit(solution)/shard_map/fused/pallas_call | solution.py:2164
  352.8 0.7 slice.77
  353.5 1.5 slice_bitcast_fusion
  355.0 0.7 reshape.41
  355.6 1.7 slice.69
  357.3 0.0 copy-start.1
  357.3 1.8 slice.76
  359.1 1.9 fusion
  360.9 0.0 copy-start
  361.0 0.9 copy.36
  361.8 0.0 copy-done.1
  361.8 0.9 copy.46
  362.7 0.0 copy-done
  362.7 1.1 copy.47
  (1 shorter events, 0.0 us)
Async XLA Ops:
  357.3 4.6 %copy-start.1 = (bf16[2,256,768]{2,1,0:T(8,128)(2,1)S(1)}, bf16[2,256,768]{2,1,0:T(8,128)(2,1)}, u32[]{:S(2)}) copy-start(bf16[2,256,768]{2,1,0:T(8,128)(2,1)} %get-tuple-element.70) | copy-start | bytes 2359300
  360.9 1.8 copy-start

commit v4 on v3

--- a/solution.py
+++ b/solution.py
@@ -10,6 +10,7 @@
 
 HEAD_DIM = 64
 CLUSTER = 128
+TILE = 256
 MESH = pl.DeviceIdType.MESH
 BF16 = jnp.bfloat16
 F32 = jnp.float32
@@ -47,7 +48,7 @@
     def __init__(self):
         self.pending = []
 
-    def start(self, make, when=None):
+    def start(self, make, when=None, tag=None):
         if when is None:
             make().start()
         else:
@@ -56,12 +57,14 @@
             def _():
                 make().start()
 
-        self.pending.append((make, when))
-
-    def finish(self):
+        self.pending.append((make, when, tag))
+
+    def finish(self, *tags):
         pending, self.pending = self.pending, []
-        for make, when in pending:
-            if when is None:
+        for make, when, tag in pending:
+            if tags and tag not in tags:
+                self.pending.append((make, when, tag))
+            elif when is None:
                 make().wait_send()
             else:
 
@@ -103,26 +106,26 @@
 
 
 def permute_rows(one_hot_tile, source, target, rows):
-    @pl.loop(0, rows // CLUSTER)
+    @pl.loop(0, rows // TILE)
     def _(tile):
-        start = pl.multiple_of(tile * CLUSTER, CLUSTER)
+        start = pl.multiple_of(tile * TILE, TILE)
         chosen = jnp.dot(one_hot_tile(start), source[...], preferred_element_type=F32)
-        target[pl.ds(start, CLUSTER), :] = chosen.astype(BF16)
+        target[pl.ds(start, TILE), :] = chosen.astype(BF16)
 
 
 def one_hot_from_row(row_ref):
     def tile(start):
         row = row_ref[0:1, :]
         count = row.shape[1]
-        return jnp.where(iota((CLUSTER, count), 0) + start == row, 1.0, 0.0).astype(BF16)
+        return jnp.where(iota((TILE, count), 0) + start == row, 1.0, 0.0).astype(BF16)
 
     return tile
 
 
 def one_hot_from_column(column_ref, count):
     def tile(start):
-        column = column_ref[pl.ds(start, CLUSTER), 0:1]
-        return jnp.where(iota((CLUSTER, count), 1) == column, 1.0, 0.0).astype(BF16)
+        column = column_ref[pl.ds(start, TILE), 0:1]
+        return jnp.where(iota((TILE, count), 1) == column, 1.0, 0.0).astype(BF16)
 
     return tile
 
@@ -142,7 +145,7 @@
                 self.head_recv.at[self.tensor, step, self.head],
                 (self.blk, other),
             )
-            self.sends.start(make, when=other != self.head)
+            self.sends.start(make, when=other != self.head, tag=self.tensor)
 
             @pl.when(other == self.head)
             def _():
@@ -176,7 +179,7 @@
                 self.blk_recv.at[self.tensor, self.blk],
                 (other, self.head),
             )
-            self.sends.start(make, when=other != self.blk)
+            self.sends.start(make, when=other != self.blk, tag=self.tensor)
 
             @pl.when(other == self.blk)
             def _():
@@ -1210,11 +1213,11 @@
     )(attn_res, slots_g, weights, vectors, up_bias)
 
 
-def attend_back(proj, probs, g_context, g_proj):
+def attend_back(proj, probs, g_context, g_proj, begin=0, end=None):
     tokens, width = g_context.shape
     first = iota((CLUSTER, 128), 1) < HEAD_DIM
 
-    @pl.loop(0, tokens // CLUSTER)
+    @pl.loop(begin, tokens // CLUSTER if end is None else end)
     def _(cluster):
         rows = pl.ds(pl.multiple_of(cluster * CLUSTER, CLUSTER), CLUSTER)
         for pair in range(width // 128):
@@ -1359,6 +1362,10 @@
         rank_rows=vmem((blks, group), jnp.int32),
         seg_col=vmem((tokens, 128), F32),
         seg_row=vmem((8 * (-(-tokens // CLUSTER // 8)), CLUSTER), F32),
+        perm=vmem((micros, blks, group), jnp.int32),
+        shard=vmem((share, 3 * width), BF16),
+        small_sums=vmem((16, 128), F32),
+        small=vmem((16, 128), BF16),
         packed=vmem((heads, width, 3 * width), BF16),
         qkv=vmem((width, 3 * width), BF16),
         out=vmem((width, width), BF16),
@@ -1384,8 +1391,7 @@
         g_attn=vmem((tokens, width), BF16),
         staged=vmem((2, kept, share, width), BF16),
         from_tree=vmem((3, 2, heads, kept - 1, share, half), BF16),
-        from_left=vmem((3, heads, share, width), BF16),
-        from_right=vmem((3, heads, share, width), BF16),
+        from_head=vmem((3, heads, share, width), BF16),
         vec_split=vmem((blks, 16, 128), F32),
         vec_parts=vmem((blks, 16, 128), F32),
         vec_mid=vmem((16, 128), F32),
@@ -1409,13 +1415,11 @@
         down_recv=dma((3, 2, heads, kept)),
         left_send=dma((3, heads)),
         left_recv=dma((3, heads)),
-        right_send=dma((3, heads)),
-        right_recv=dma((3, heads)),
         vec_send=dma((blks,)),
         vec_recv=dma((blks,)),
         vec_head_send=dma((heads,)),
         vec_head_recv=dma((heads,)),
-        out_sem=dma((3, max(heads, 3))),
+        out_sem=dma((2, 3)),
     )
 
 
@@ -1521,7 +1525,25 @@
                 (other, head),
             ).wait_recv()
 
+    def forwards(j):
+        left = (arrival[j] > head) & (head > 0)
+        right = (arrival[j] < head) & (head < heads - 1)
+        return left, right
+
+    def chain_wait(p, j):
+        target = r.packed.at[arrival[j], piece_rows(blk), part_cols(p)]
+        remote(
+            target, target, r.z_send.at[p, 0, 0], r.z_recv.at[p, arrival[j]], (blk, head)
+        ).wait_recv()
+
     def tree_step(p, j, step):
+        if step == 0 and j:
+            left, right = forwards(j)
+
+            @pl.when(jnp.logical_not(left | right))
+            def _():
+                chain_wait(p, j)
+
         for which in range(2):
             dims = orders[which]
             if step:
@@ -1541,7 +1563,8 @@
                         r.tree_send.at[p, j, which, slot],
                         r.tree_recv.at[p, j, which, piece],
                         (other, head),
-                    )
+                    ),
+                    tag="weights",
                 )
 
     def chain(p, j):
@@ -1551,11 +1574,12 @@
             left, right = head > 0, head < heads - 1
         else:
             source = target
-            left = (arrival[j] > head) & (head > 0)
-            right = (arrival[j] < head) & (head < heads - 1)
-            remote(
-                target, target, r.z_send.at[p, 0, 0], r.z_recv.at[p, arrival[j]], (blk, head)
-            ).wait_recv()
+            left, right = forwards(j)
+
+            @pl.when(left | right)
+            def _():
+                chain_wait(p, j)
+
         for side, (condition, step) in enumerate(((left, -1), (right, 1))):
             sends.start(
                 lambda side=side, step=step: remote(
@@ -1566,6 +1590,7 @@
                     (blk, jnp.clip(head + step, 0, heads - 1)),
                 ),
                 when=condition,
+                tag="weights",
             )
 
     def gain_copy(other, slot):
@@ -1670,35 +1695,26 @@
         for other in order:
             tree_add(g, other, step)
 
-    def pass_on(g, goal):
-        for target, send_sem, recv_sem, step in (
-            (r.from_left.at[g, goal], r.left_send, r.left_recv, 1),
-            (r.from_right.at[g, goal], r.right_send, r.right_recv, -1),
-        ):
-            if step == 1:
-                arrives = (head > 0) & (head <= goal)
-                leaves = head < goal
-            else:
-                arrives = (head < heads - 1) & (head >= goal)
-                leaves = head > goal
-
-            @pl.when(arrives)
-            def _(target=target, send_sem=send_sem, recv_sem=recv_sem):
-                remote(
-                    target, target, send_sem.at[g, goal], recv_sem.at[g, goal], (blk, head)
-                ).wait_recv()
-                add_into(total(g, goal, 0), target, width)
-
-            sends.start(
-                lambda target=target, send_sem=send_sem, recv_sem=recv_sem, step=step: remote(
-                    total(g, goal, 0),
-                    target,
-                    send_sem.at[g, goal],
-                    recv_sem.at[g, goal],
-                    (blk, jnp.clip(head + step, 0, heads - 1)),
-                ),
-                when=leaves,
-            )
+    def direct_copy(g, goal, source):
+        return remote(
+            total(g, goal, 0),
+            r.from_head.at[g, source],
+            r.left_send.at[g, goal],
+            r.left_recv.at[g, source],
+            (blk, goal),
+        )
+
+    def direct_start(g):
+        for goal in range(heads):
+            sends.start(lambda goal=goal: direct_copy(g, goal, head), when=goal != head)
+
+    def direct_add(g):
+        for source in range(heads):
+
+            @pl.when(source != head)
+            def _():
+                direct_copy(g, source, source).wait_recv()
+                add_into(total(g, head, 0), r.from_head.at[g, source], width)
 
 
     micro = head // splits
@@ -1977,74 +1993,166 @@
             (blk, other),
         )
 
+    def place_slots():
+        for m in range(micros):
+            for b in range(blks):
+                r.perm[m, b : b + 1, :] = r.perm_rows[m : m + 1, b * group : (b + 1) * group]
+
+    def pack_shard():
+        at = 0
+        for source in (r.qkv_weight, r.out_weight, r.up_weight):
+            r.shard[:, at : at + source.shape[1]] = source[...]
+            at += source.shape[1]
+        turned = r.down_weight[...].T
+        for j in range(fold):
+            r.shard[:, at + j * short : at + (j + 1) * short] = turned[
+                j * share : (j + 1) * share
+            ]
+
+    def pack_small():
+        r.small_sums[...] = jnp.zeros_like(r.small_sums)
+        for i in range(8):
+            r.small_sums[i : i + 1, 0:share] = getattr(r, "vector%d" % i)[...].astype(F32)
+        for j in range(fold):
+            r.small_sums[8 + j : 9 + j, 0:share] = r.up_bias_here[
+                :, j * share : (j + 1) * share
+            ].astype(F32)
+        r.small[...] = r.small_sums[...].astype(BF16)
+
+    def send_small():
+        for other in range(blks):
+            sends.start(lambda other=other: gain_copy(other, blk), when=other != blk)
+        own_gain.start()
+        own_shard.start()
+
+    def take_small():
+        for other in range(blks):
+
+            @pl.when(other != blk)
+            def _():
+                gain_copy(other, other).wait_recv()
+
+        own_gain.wait()
+        own_shard.wait()
+        spread_vectors()
+
+    def send_vectors():
+        split_vectors()
+        for other in range(blks):
+            sends.start(lambda other=other: vec_copy(other, blk), when=other != blk)
+
+    def sum_vectors_over_blk():
+        r.vec_mid[...] = r.vec_split[pl.ds(blk, 1)][0]
+        for other in range(blks):
+
+            @pl.when(other != blk)
+            def _():
+                vec_copy(other, other).wait_recv()
+                r.vec_mid[...] += r.vec_parts[other]
+
+        for other in range(heads):
+            sends.start(lambda other=other: vec_head_copy(other, head), when=other != head)
+
+    def sum_vectors_over_head():
+        r.vec_sum[...] = r.vec_mid[...]
+        for other in range(heads):
+
+            @pl.when(other != head)
+            def _():
+                vec_head_copy(other, other).wait_recv()
+                r.vec_sum[...] += r.vec_heads[other]
+
+    own_gain = pltpu.make_async_copy(r.small, r.full_vectors.at[blk], r.own_sem.at[0])
+    own_shard = pltpu.make_async_copy(
+        r.shard, r.packed.at[head, piece_rows(blk), :], r.own_sem.at[1]
+    )
+
+    def start_backward():
+        r.vec_grads[...] = jnp.zeros_like(r.vec_grads)
+
+    clusters = tokens // CLUSTER
+
+    def attention_back(begin, end):
+        attend_back(r.proj, r.probs, g_context, g_proj, begin, end)
+
+    def row_copy(i):
+        return pltpu.make_async_copy(r.slots.at[i], r.row_results.at[i], r.out_sem.at[0, i])
+
+    def shard_copy(g):
+        return pltpu.make_async_copy(
+            r.packed.at[head, piece_rows(blk), group_cols(g)],
+            r.shard_grad.at[:, group_cols(g)],
+            r.out_sem.at[1, g],
+        )
+
+    def finish():
+        for i in range(2):
+            row_copy(i).wait()
+        for g in range(3):
+            shard_copy(g).wait()
+        sends.finish()
+
 
     enter(blk, head, blks, heads)
     to_heads(0, row_source(r.tokens))
-    for other in range(blks):
-        sends.start(lambda other=other: gain_copy(other, blk), when=other != blk)
-    own_gain = pltpu.make_async_copy(r.small, r.full_vectors.at[blk], r.own_sem.at[0])
-    own_gain.start()
-    for p in range(2):
-        tree_step(p, 0, 0)
-        chain(p, 0)
-    own_shard = pltpu.make_async_copy(r.shard, r.packed.at[head, piece_rows(blk), :], r.own_sem.at[1])
-    own_shard.start()
+    pack_shard()
+    chain(0, 0)
+    tree_step(0, 0, 0)
+    tree_step(1, 0, 0)
+    pack_small()
+    send_small()
+    place_slots()
     find_destinations()
-    to_groups(0, one_hot_from_row(r.dest_row))
-    to_heads(1, row_source(r.out_grad))
     tree_step(0, 0, 1)
-    chain(0, 1)
-    tree_step(0, 1, 0)
+    chain(1, 0)
+    tree_step(1, 0, 1)
     find_slots()
     tree_step(0, 0, 2)
+    tree_step(1, 0, 2)
+    find_segments()
+    chain(0, 1)
+    to_groups(0, one_hot_from_row(r.dest_row))
+    chain(0, 2)
+    chain(1, 1)
+    tree_step(0, 1, 0)
+    chain(1, 2)
+    tree_step(1, 1, 0)
+    chain(0, 3)
+    tree_step(0, 2, 0)
     tree_step(0, 1, 1)
-    chain(0, 2)
-    tree_step(0, 2, 0)
     to_owners(0, one_hot_from_row(r.slot_row))
-    find_segments()
+    chain(1, 3)
+    tree_step(0, 3, 0)
+    tree_step(1, 2, 0)
+    tree_step(0, 2, 1)
     tree_step(0, 1, 2)
-    tree_step(0, 2, 1)
-    chain(0, 3)
-    tree_step(0, 3, 0)
-    tree_step(1, 0, 1)
-    chain(1, 1)
-    tree_step(1, 1, 0)
+    to_heads(1, row_source(r.out_grad))
+    tree_step(1, 1, 1)
+    tree_step(0, 3, 1)
     tree_step(0, 2, 2)
-    tree_step(0, 3, 1)
-    to_groups(1, one_hot_from_row(r.dest_row))
-    tree_step(1, 0, 2)
-    tree_step(1, 1, 1)
+    take_small()
+    tree_step(1, 3, 0)
+    tree_step(1, 2, 1)
     tree_step(0, 3, 2)
-    for other in range(blks):
-
-        @pl.when(other != blk)
-        def _():
-            gain_copy(other, other).wait_recv()
-
-    own_gain.wait()
-    own_shard.wait()
-    spread_vectors()
-    for j in range(heads):
-        tree_step(0, j, 3)
+    tree_step(1, 1, 2)
+    tree_step(0, 0, 3)
+    tree_step(0, 1, 3)
+    tree_step(0, 2, 3)
+    tree_step(0, 3, 3)
     assemble_attention(r.packed, r.qkv, r.out)
-    chain(1, 2)
-    tree_step(1, 2, 0)
+    tree_step(1, 3, 1)
+    tree_step(1, 2, 2)
     rows_here(0)
     take_rows()
     project(r.x, r.qkv, r.bias_qkv, r.proj)
-    tree_step(1, 1, 2)
-    tree_step(1, 2, 1)
-    chain(1, 3)
-    tree_step(1, 3, 0)
-    to_owners(1, one_hot_from_row(r.slot_row))
+    to_groups(1, one_hot_from_row(r.dest_row))
+    tree_step(1, 3, 2)
     attend(r.proj, r.probs, r.context, r.seg_col, r.seg_row)
-    tree_step(1, 2, 2)
-    tree_step(1, 3, 1)
     leave_attention(r.x, r.context, r.out, r.vectors, r.attn_res)
     first_norm()
+    to_owners(1, one_hot_from_row(r.slot_row))
     tree_step(1, 0, 3)
     ffn_up(arrival[0])
-    tree_step(1, 3, 2)
     tree_step(1, 1, 3)
     ffn_up(arrival[1])
     tree_step(1, 2, 3)
@@ -2054,130 +2162,162 @@
     assemble_down()
     ffn_down()
     second_norm()
-    sends.finish()
     to_heads(2, own_rows(r.hidden))
-    r.vec_grads[...] = jnp.zeros_like(r.vec_grads)
+    start_backward()
     rows_here(1)
     second_norm_back()
+    sends.finish("weights")
     down_gradient()
     core_start(2)
     ffn_up_back()
     norm_cotangent()
+    sends.finish(0)
+    to_groups(2, one_hot_from_column(r.slot_col, group))
     core_add(2)
     up_gradient()
     core_start(1)
-    to_groups(2, one_hot_from_column(r.slot_col, group))
     first_norm_back()
+    context_cotangent()
+    to_owners(2, one_hot_from_column(r.dest_col, group))
+    attention_back(0, clusters // 2)
+    core_add(1)
+    attention_back(clusters // 2, clusters)
     tree_down(2, 0)
-    context_cotangent()
-    core_add(1)
-    attend_back(r.proj, r.probs, g_context, g_proj)
-    tree_down(2, 1)
     row_gradient()
     to_heads(3, own_rows(x_grad))
-    to_owners(2, one_hot_from_column(r.dest_col, group))
-    tree_down(1, 0)
     out_gradient()
     qkv_gradient()
     core_start(0)
-    split_vectors()
-    for other in range(blks):
-        sends.start(lambda other=other: vec_copy(other, blk), when=other != blk)
-    for i in range(heads):
-        pass_on(2, order[i])
+    send_vectors()
+    tree_down(2, 1)
+    direct_start(2)
+    tree_down(1, 0)
+    core_add(0)
+    sends.finish(1)
+    sum_vectors_over_blk()
+    to_groups(3, one_hot_from_column(r.slot_col, group))
     tree_down(1, 1)
-    core_add(0)
-    to_groups(3, one_hot_from_column(r.slot_col, group))
-    for i in range(heads):
-        pass_on(1, order[i])
+    direct_start(1)
+    direct_add(2)
+    shard_copy(2).start()
+    to_owners(3, one_hot_from_column(r.dest_col, group))
     tree_down(0, 0)
-    r.vec_mid[...] = r.vec_split[pl.ds(blk, 1)][0]
-    for other in range(blks):
-
-        @pl.when(other != blk)
-        def _():
-            vec_copy(other, other).wait_recv()
-            r.vec_mid[...] += r.vec_parts[other]
-
-    for other in range(heads):
-        sends.start(lambda other=other: vec_head_copy(other, head), when=other != head)
-    to_owners(3, one_hot_from_column(r.dest_col, group))
+    sum_vectors_over_head()
     tree_down(0, 1)
-    for i in range(heads):
-        pass_on(0, order[i])
-
-    def out_copy(source):
-        m, which = source // splits, source % splits
-        return pltpu.make_async_copy(
-            r.slots.at[0, source],
-            r.out_rows.at[m, :, which * part : (which + 1) * part],
-            r.out_sem.at[0, source],
-        )
-
+    direct_start(0)
     rows_here(2)
-    for source in range(heads):
-        out_copy(source).start()
-    r.vec_sum[...] = r.vec_mid[...]
-    for other in range(heads):
-
-        @pl.when(other != head)
-        def _():
-            vec_head_copy(other, other).wait_recv()
-            r.vec_sum[...] += r.vec_heads[other]
-
-    copies = []
-    for g in range(3):
-        at = slice(g * share, (g + 1) * share)
-        r.ffn_res[at, :] = r.packed[head, piece_rows(blk), group_cols(g)].astype(F32)
-        copies.append(
-            pltpu.make_async_copy(
-                r.ffn_res.at[at, :], r.shard_grad.at[:, group_cols(g)], r.out_sem.at[1, g]
-            )
-        )
-        copies[-1].start()
+    row_copy(0).start()
+    direct_add(1)
+    shard_copy(1).start()
+    direct_add(0)
+    shard_copy(0).start()
     rows_here(3)
-    for m in range(micros):
-        at = slice(m * rows, (m + 1) * rows)
-        for which in range(splits):
-            r.normed[at, which * part : (which + 1) * part] = r.slots[
-                1, m * splits + which
-            ].astype(F32)
-        copies.append(
-            pltpu.make_async_copy(r.normed.at[at, :], r.grad_rows.at[m], r.out_sem.at[2, m])
-        )
-        copies[-1].start()
-    for source in range(heads):
-        out_copy(source).wait()
-    for copy in copies:
-        copy.wait()
-    sends.finish()
-
-
-def fused(blks, heads, fold, tokens, out_grad, shard, small, perm, seq_lengths):
+    row_copy(1).start()
+    finish()
+
+
+def fused(blks, heads, fold, tokens, out_grad, weights, vectors, up_bias, perm, seq_lengths):
     micros, rows, width = tokens.shape
-    share = shard.shape[0]
+    share = weights[0].shape[0]
+    part = width * micros // heads
     scratch = fused_scratch(micros, rows, width, blks, heads, share, fold)
     any_space, vmem = pl.BlockSpec(memory_space=pl.ANY), pl.BlockSpec(memory_space=pltpu.VMEM)
-    names = ["tokens", "out_grad", "shard", "small", "perm", "seq_lengths"]
-    names += ["out_rows", "grad_rows", "shard_grad", "vec_sum", "from_core"]
+    names = ["tokens", "out_grad", "qkv_weight", "out_weight", "up_weight", "down_weight"]
+    names += ["vector%d" % i for i in range(8)] + ["up_bias_here", "perm_rows", "seq_lengths"]
+    names += ["row_results", "shard_grad", "vec_sum", "from_core"]
     names += list(scratch)
     return pl.pallas_call(
         functools.partial(fused_kernel, names, blks, heads, share, fold),
         name="fused",
         out_shape=(
-            jax.ShapeDtypeStruct((micros, rows, width), BF16),
-            jax.ShapeDtypeStruct((micros, rows, width), F32),
-            jax.ShapeDtypeStruct(shard.shape, F32),
+            jax.ShapeDtypeStruct((2, heads, rows, part), BF16),
+            jax.ShapeDtypeStruct((share, 3 * width), BF16),
             jax.ShapeDtypeStruct((16, 128), F32),
             jax.ShapeDtypeStruct((3, heads, blks // 2, share, width), BF16),
         ),
-        in_specs=[any_space] * 4 + [vmem, pl.BlockSpec(memory_space=pltpu.SMEM)],
-        out_specs=(any_space, any_space, any_space, vmem, any_space),
+        in_specs=[any_space] * 2 + [vmem] * 14 + [pl.BlockSpec(memory_space=pltpu.SMEM)],
+        out_specs=(any_space, any_space, vmem, any_space),
         scratch_shapes=list(scratch.values()),
         compiler_params=pltpu.CompilerParams(
             collective_id=2, has_side_effects=True, vmem_limit_bytes=64 << 20
         ),
-    )(tokens, out_grad, shard, small, perm, seq_lengths)[:4]
+    )(
+        tokens,
+        out_grad,
+        *weights[:3],
+        weights[3].T,
+        *[vector.reshape(1, -1) for vector in vectors],
+        up_bias.reshape(1, -1),
+        perm,
+        seq_lengths,
+    )[:3]
+
+
+def unpack_kernel(
+    row_results, shard, sums, layer_out, x_grad, qkv, out, up, down, up_bias, *vectors
+):
+    micros, rows, width = layer_out.shape
+    _, heads, _, part = row_results.shape
+    splits = heads // micros
+    share, short = out.shape
+    fold = down.shape[1] // share
+    for source in range(heads):
+        m, which = source // splits, source % splits
+        cols = slice(which * part, (which + 1) * part)
+        layer_out[m, :, cols] = row_results[0, source]
+        x_grad[m, :, cols] = row_results[1, source].astype(F32)
+    at = 0
+    for target in (qkv, out, up):
+        target[...] = shard[:, at : at + target.shape[1]].astype(F32)
+        at += target.shape[1]
+    pieces = [
+        shard[:, at + j * short : at + (j + 1) * short].astype(F32) for j in range(fold)
+    ]
+    down[...] = jnp.concatenate(pieces, axis=0).T
+    for i, vector in enumerate(vectors):
+        vector[...] = sums[i : i + 1, 0:share]
+    for j in range(fold):
+        up_bias[:, j * share : (j + 1) * share] = sums[8 + j : 9 + j, 0:share]
+
+
+def unpack(micros, width, widths, row_results, shard, sums):
+    _, heads, rows, part = row_results.shape
+    share = shard.shape[0]
+    vmem = pl.BlockSpec(memory_space=pltpu.VMEM)
+    shapes = [(share, widths[0]), (share, widths[1]), (share, widths[2])]
+    shapes += [(widths[1], widths[3] // widths[1] * share), (1, widths[3] // widths[1] * share)]
+    shapes += [(1, share)] * 8
+    results = pl.pallas_call(
+        unpack_kernel,
+        name="unpack",
+        out_shape=(
+            jax.ShapeDtypeStruct((micros, rows, width), BF16),
+            jax.ShapeDtypeStruct((micros, rows, width), F32),
+        )
+        + tuple(jax.ShapeDtypeStruct(shape, F32) for shape in shapes),
+        in_specs=[vmem] * 3,
+        out_specs=(vmem,) * (2 + len(shapes)),
+        compiler_params=pltpu.CompilerParams(vmem_limit_bytes=32 << 20),
+    )(row_results, shard, sums)
+    layer_out, x_grad, qkv, out, up, down, up_bias = results[:7]
+    vec = [member.reshape(-1) for member in results[7:]]
+    return (
+        layer_out,
+        x_grad,
+        qkv,
+        vec[0],
+        vec[1],
+        out,
+        vec[2],
+        vec[3],
+        vec[4],
+        up,
+        up_bias.reshape(-1),
+        down.T,
+        vec[5],
+        vec[6],
+        vec[7],
+    )
 
 
 def refold(packed, share, other, fold):
@@ -2220,12 +2360,6 @@
     widths = [qkv_weight.shape[1], out_weight.shape[1], up_weight.shape[1], folds * short]
     edges = [sum(widths[:i]) for i in range(5)]
 
-    shard = jnp.concatenate(
-        [qkv_weight, out_weight, up_weight]
-        + [down_weight[i * share : (i + 1) * share] for i in range(folds)],
-        axis=1,
-    )
-    lanes = -(-share // 128) * 128
     small = [
         query_bias,
         value_bias,
@@ -2236,65 +2370,81 @@
         ffn_gain,
         ffn_shift,
     ]
+    if share % 16 == 0:
+        results = fused(
+            blks,
+            heads,
+            folds,
+            tokens,
+            out_grad,
+            (qkv_weight, out_weight, up_weight, down_weight),
+            small,
+            up_bias,
+            cluster_perm,
+            seq_lengths,
+        )
+        return unpack(micros, width, widths, *results)
+
+    shard = jnp.concatenate(
+        [qkv_weight, out_weight, up_weight]
+        + [down_weight[i * share : (i + 1) * share] for i in range(folds)],
+        axis=1,
+    )
+    lanes = -(-share // 128) * 128
     stacked = jnp.concatenate([jnp.stack(small), up_bias.reshape(folds, share)], axis=0)
     count = stacked.shape[0]
     vectors = jnp.pad(stacked, ((0, -count % 16), (0, lanes - share)))
     perm = cluster_perm.reshape(micros, blks, group)
-    if share % 16 == 0:
-        out_rows, grad_rows, shard_grad, vec_sum = fused(
-            blks, heads, folds, tokens, out_grad, shard, vectors, perm, seq_lengths
-        )
-    else:
-        full, full_vectors, slots_x, slots_g, dest_col, slot_col = gather_all(
-            blks, heads, tokens, out_grad, shard, vectors, perm
-        )
-
-        first = blk * group + head * rows
-        slots = first + jnp.arange(rows, dtype=jnp.int32)
-        ends = jnp.cumsum(seq_lengths, axis=1)
-        positions = jnp.arange(total_rows, dtype=jnp.int32)
-        segs = jnp.sum((positions[None, :, None] >= ends[:, None, :]).astype(jnp.int32), axis=2)
-        slot_segs = jnp.sum(
-            jnp.where(cluster_perm[:, None, :] == slots[None, :, None], segs[:, None, :], 0), axis=2
-        )
-
-        weights = full.reshape(heads, blks * share, -1)
-        tall = share if share % 16 == 0 else width // 8
-        if tall != share:
-            weights = jnp.concatenate(
-                [weights[:, :, : edges[3]], refold(weights[:, :, edges[3] :], share, tall, folds)],
-                axis=2,
-            )
-        spread = full_vectors[:, :count, :share].astype(F32)
-        vecs = spread[:, :8].transpose(1, 0, 2).reshape(8, width)
-        up_vec = spread[:, 8:count].reshape(1, -1)
-        bias_qkv = jnp.concatenate([vecs[0:1], jnp.zeros((1, width), F32), vecs[1:2]], axis=1)
-        seg_col = jnp.broadcast_to(slot_segs.reshape(-1, 1), (micros * rows, 128))
-        seg_row = slot_segs.reshape(-1, CLUSTER)
-        x, proj, probs, context, attn_res, qkv, out = forward_part(
-            slots_x, weights, bias_qkv, vecs, seg_col, seg_row
-        )
-        layer_out, d_attn, g_attn, partial_ffn, vec_ffn, up_vec_grad = ffn_part(
-            tall, attn_res, slots_g, weights, vecs, up_vec
-        )
-        x_grad, partial_attn, vec_attn = backward_part(
-            heads, rows, x, proj, probs, context, qkv, out, d_attn, g_attn
-        )
-        if tall != share:
-            partial_ffn = jnp.concatenate(
-                [partial_ffn[:, :, :width], refold(partial_ffn[:, :, width:], tall, share, folds)],
-                axis=2,
-            )
-        partial = jnp.concatenate([partial_attn, partial_ffn], axis=2).reshape(full.shape)
-        vec_grads = vec_ffn + vec_attn
-        vec_parts = jnp.concatenate(
-            [vec_grads.reshape(8, blks, share).transpose(1, 0, 2), up_vec_grad.reshape(blks, folds, share)],
-            axis=1,
-        )
-        vec_parts = jnp.pad(vec_parts, ((0, 0), (0, -count % 16), (0, lanes - share)))
-        out_rows, grad_rows, shard_grad, vec_sum = reduce_all(
-            blks, heads, layer_out, x_grad, partial, vec_parts, dest_col, slot_col
-        )
+    full, full_vectors, slots_x, slots_g, dest_col, slot_col = gather_all(
+        blks, heads, tokens, out_grad, shard, vectors, perm
+    )
+
+    first = blk * group + head * rows
+    slots = first + jnp.arange(rows, dtype=jnp.int32)
+    ends = jnp.cumsum(seq_lengths, axis=1)
+    positions = jnp.arange(total_rows, dtype=jnp.int32)
+    segs = jnp.sum((positions[None, :, None] >= ends[:, None, :]).astype(jnp.int32), axis=2)
+    slot_segs = jnp.sum(
+        jnp.where(cluster_perm[:, None, :] == slots[None, :, None], segs[:, None, :], 0), axis=2
+    )
+
+    weights = full.reshape(heads, blks * share, -1)
+    tall = share if share % 16 == 0 else width // 8
+    if tall != share:
+        weights = jnp.concatenate(
+            [weights[:, :, : edges[3]], refold(weights[:, :, edges[3] :], share, tall, folds)],
+            axis=2,
+        )
+    spread = full_vectors[:, :count, :share].astype(F32)
+    vecs = spread[:, :8].transpose(1, 0, 2).reshape(8, width)
+    up_vec = spread[:, 8:count].reshape(1, -1)
+    bias_qkv = jnp.concatenate([vecs[0:1], jnp.zeros((1, width), F32), vecs[1:2]], axis=1)
+    seg_col = jnp.broadcast_to(slot_segs.reshape(-1, 1), (micros * rows, 128))
+    seg_row = slot_segs.reshape(-1, CLUSTER)
+    x, proj, probs, context, attn_res, qkv, out = forward_part(
+        slots_x, weights, bias_qkv, vecs, seg_col, seg_row
+    )
+    layer_out, d_attn, g_attn, partial_ffn, vec_ffn, up_vec_grad = ffn_part(
+        tall, attn_res, slots_g, weights, vecs, up_vec
+    )
+    x_grad, partial_attn, vec_attn = backward_part(
+        heads, rows, x, proj, probs, context, qkv, out, d_attn, g_attn
+    )
+    if tall != share:
+        partial_ffn = jnp.concatenate(
+            [partial_ffn[:, :, :width], refold(partial_ffn[:, :, width:], tall, share, folds)],
+            axis=2,
+        )
+    partial = jnp.concatenate([partial_attn, partial_ffn], axis=2).reshape(full.shape)
+    vec_grads = vec_ffn + vec_attn
+    vec_parts = jnp.concatenate(
+        [vec_grads.reshape(8, blks, share).transpose(1, 0, 2), up_vec_grad.reshape(blks, folds, share)],
+        axis=1,
+    )
+    vec_parts = jnp.pad(vec_parts, ((0, 0), (0, -count % 16), (0, lanes - share)))
+    out_rows, grad_rows, shard_grad, vec_sum = reduce_all(
+        blks, heads, layer_out, x_grad, partial, vec_parts, dest_col, slot_col
+    )
     down_grad = shard_grad[:, edges[3] : edges[4]]
     down_grad = jnp.concatenate(
         [down_grad[:, i * short : (i + 1) * short] for i in range(folds)], axis=0

time: 364 us -> 253 us (0.70)
  Pallas kernels: 345 us -> 245 us
  local copies, waits for them, and re-layouts: 18.1 us -> 4.35 us
    pallas_call x1, Pallas kernels: 345 us -> 243 us  [fused(): pl.pallas_call(functools.partial(fused_kernel, names, blks, heads, share,...]
    slice x5 -> x0, local copies, waits for them, and re-layouts: 7.05 us -> none  [the longest x1 1.89 us: body(): down_grad[:, i * short:(i + 1) * short]]
where the time goes in v4:
time: 253 us; the launch traced here: 251 us
  Pallas kernels  245 us (97%)
  local copies, waits for them, and re-layouts  4.35 us (2%)
    pallas_call x1, Pallas kernels, fused(): pl.pallas_call(functools.partial(fused_kernel, names, blks, heads, share,...  243 us

profile of v4, /device:TPU:8, one launch (start us, length us, event | category | flops | bytes accessed | tf_op | source)
XLA Modules:
  0.0 250.9 jit_solution(4643680804693282078)
XLA Ops:
  0.6 1.2 reshape.92.refs_14_
  1.9 243.2 %fused.1 = (bf16[2,4,256,384]{3,2,1,0:T(8,128)(2,1)}, bf16[96,2304]{1,0:T(8,128)(2,1)}, f32[16,128]{1,0:T(8,128)}, bf16[3,4,4,96,768]{4,3,2,1,0:T(8,128)(2,1)}) custom-call(bf16[2,256,768]{2,1,0:T(8,128)(2,1)} %refs_0_.1, bf16[2,256,768]{2,1,0:T(8,128)(2,1)} %refs_1_.1, bf16[96,576]{1,0:T(8,128)(2,1)} %refs_2_.1, bf16[96,192]{1,0:T(8,128)(2,1)} %refs_3_.1, ...), custom_call_target="tpu_custom_call" | custom-call | tf_op jit(solution)/shard_map/fused/pallas_call | solution.py:2229
  245.1 0.0 copy-start
  245.1 1.4 copy-done
  246.5 0.0 copy-start.1
  246.5 1.0 copy-done.1
  247.5 0.0 copy-start.2
  247.5 0.7 copy-done.2
  248.2 2.0 unpack.1
  250.3 0.6 reduce
Async XLA Ops:
  245.1 1.4 copy-start
  246.5 1.0 copy-start.1
  247.5 0.7 copy-start.2

commit v5 on v4

--- a/solution.py
+++ b/solution.py
@@ -47,8 +47,9 @@
 class Sends:
     def __init__(self):
         self.pending = []
-
-    def start(self, make, when=None, tag=None):
+        self.shared = {}
+
+    def start(self, make, when=None, tag=None, shared=None):
         if when is None:
             make().start()
         else:
@@ -57,7 +58,11 @@
             def _():
                 make().start()
 
-        self.pending.append((make, when, tag))
+        if shared is None:
+            self.pending.append((make, when, tag))
+        else:
+            key, wait = shared
+            self.shared[tag, key] = wait
 
     def finish(self, *tags):
         pending, self.pending = self.pending, []
@@ -71,6 +76,17 @@
                 @pl.when(when)
                 def _(make=make):
                     make().wait_send()
+
+        shared, self.shared = self.shared, {}
+        for (tag, key), wait in shared.items():
+            if tags and tag not in tags:
+                self.shared[tag, key] = wait
+            else:
+                wait()
+
+
+def await_bytes(ref, sem):
+    pltpu.make_async_copy(ref, ref, sem).wait()
 
 
 def remote(src, dst, send_sem, recv_sem, device):
@@ -136,16 +152,22 @@
         self.head_send, self.head_recv, self.blk_send, self.blk_recv, self.local = sems
         self.tensor = tensor
 
-    def over_head(self, step, source, target):
+    def over_head(self, step, source, target, all_but_one):
+        send_sem = self.head_send.at[self.tensor, step]
         for other in range(self.heads):
             make = lambda other=other: remote(
                 source(other),
                 target(self.head),
-                self.head_send.at[self.tensor, step, other],
-                self.head_recv.at[self.tensor, step, self.head],
+                send_sem,
+                self.head_recv.at[self.tensor, step],
                 (self.blk, other),
             )
-            self.sends.start(make, when=other != self.head, tag=self.tensor)
+            self.sends.start(
+                make,
+                when=other != self.head,
+                tag=self.tensor,
+                shared=(("head", step), lambda: await_bytes(all_but_one, send_sem)),
+            )
 
             @pl.when(other == self.head)
             def _():
@@ -153,33 +175,26 @@
                     source(other), target(other), self.local.at[self.tensor, step]
                 ).start()
 
-    def wait_head(self, step, target):
-        for other in range(self.heads):
-
-            @pl.when(other != self.head)
-            def _():
-                remote(
-                    target(other),
-                    target(other),
-                    self.head_send.at[self.tensor, step, other],
-                    self.head_recv.at[self.tensor, step, other],
-                    (self.blk, other),
-                ).wait_recv()
-
-        pltpu.make_async_copy(
-            target(self.head), target(self.head), self.local.at[self.tensor, step]
-        ).wait()
-
-    def over_blk(self, source, target):
+    def wait_head(self, step, target, all_but_one):
+        await_bytes(all_but_one, self.head_recv.at[self.tensor, step])
+        await_bytes(target(self.head), self.local.at[self.tensor, step])
+
+    def over_blk(self, source, target, all_but_one):
+        send_sem = self.blk_send.at[self.tensor]
         for other in range(self.blks):
             make = lambda other=other: remote(
                 source(other),
                 target(self.blk),
-                self.blk_send.at[self.tensor, other],
-                self.blk_recv.at[self.tensor, self.blk],
+                send_sem,
+                self.blk_recv.at[self.tensor],
                 (other, self.head),
             )
-            self.sends.start(make, when=other != self.blk, tag=self.tensor)
+            self.sends.start(
+                make,
+                when=other != self.blk,
+                tag=self.tensor,
+                shared=("blk", lambda: await_bytes(all_but_one, send_sem)),
+            )
 
             @pl.when(other == self.blk)
             def _():
@@ -187,27 +202,14 @@
                     source(other), target(other), self.local.at[self.tensor, 2]
                 ).start()
 
-    def wait_blk(self, target):
-        for other in range(self.blks):
-
-            @pl.when(other != self.blk)
-            def _():
-                remote(
-                    target(other),
-                    target(other),
-                    self.blk_send.at[self.tensor, other],
-                    self.blk_recv.at[self.tensor, other],
-                    (other, self.head),
-                ).wait_recv()
-
-        pltpu.make_async_copy(
-            target(self.blk), target(self.blk), self.local.at[self.tensor, 2]
-        ).wait()
+    def wait_blk(self, target, all_but_one):
+        await_bytes(all_but_one, self.blk_recv.at[self.tensor])
+        await_bytes(target(self.blk), self.local.at[self.tensor, 2])
 
 
 def exchange_sems(blks, heads):
     dma = pltpu.SemaphoreType.DMA
-    return [dma((2, 2, heads)), dma((2, 2, heads)), dma((2, blks)), dma((2, blks)), dma((2, 3))]
+    return [dma((2, 2)), dma((2, 2)), dma((2,)), dma((2,)), dma((2, 3))]
 
 
 def cumulative(ones_ref, sums_ref, count):
@@ -280,6 +282,7 @@
                 other // splits, :, (other % splits) * part : (other % splits + 1) * part
             ],
             lambda other: arrived.at[i, pl.ds(pl.multiple_of(other * rows, rows), rows), :],
+            arrived.at[i, 0 : group - rows, :],
         )
 
     send_rows(0)
@@ -404,25 +407,30 @@
 
     def to_groups(i):
         exchanges[i].wait_head(
-            0, lambda other: arrived.at[i, pl.ds(pl.multiple_of(other * rows, rows), rows), :]
+            0,
+            lambda other: arrived.at[i, pl.ds(pl.multiple_of(other * rows, rows), rows), :],
+            arrived.at[i, 0 : group - rows, :],
         )
         permute_rows(one_hot_from_row(dest_row), arrived.at[i], sorted_rows.at[i], group)
         exchanges[i].over_blk(
             lambda other: sorted_rows.at[i, pl.ds(other * pair, pair), :],
             lambda other: landed.at[i, pl.ds(pl.multiple_of(other * pair, pair), pair), :],
+            landed.at[i, 0 : group - pair, :],
         )
 
     outs = (slots_x, slots_g)
 
     def to_slots(i):
         exchanges[i].wait_blk(
-            lambda other: landed.at[i, pl.ds(pl.multiple_of(other * pair, pair), pair), :]
+            lambda other: landed.at[i, pl.ds(pl.multiple_of(other * pair, pair), pair), :],
+            landed.at[i, 0 : group - pair, :],
         )
         permute_rows(one_hot_from_row(slot_row), landed.at[i], ordered.at[i], group)
         exchanges[i].over_head(
             1,
             lambda other: ordered.at[i, pl.ds(other * rows, rows), :],
             lambda other: outs[i].at[other],
+            outs[i].at[0 : heads - 1],
         )
 
     to_groups(0)
@@ -443,7 +451,7 @@
             tree_wait(j, which, levels - 1)
 
     for i in range(2):
-        exchanges[i].wait_head(1, lambda other: outs[i].at[other])
+        exchanges[i].wait_head(1, lambda other: outs[i].at[other], outs[i].at[0 : heads - 1])
     for other in range(blks):
 
         @pl.when(other != blk)
@@ -516,9 +524,7 @@
         at = pl.ds(pl.multiple_of(i * step, step), step)
         for column in range(0, target.shape[1], width):
             cols = slice(column, column + width)
-            target[at, cols] = (
-                target[at, cols].astype(F32) + source[at, cols].astype(F32)
-            ).astype(BF16)
+            target[at, cols] = target[at, cols] + source[at, cols]
 
 
 def reduce_kernel(
@@ -610,6 +616,7 @@
             0,
             lambda other: sources[i].at[other],
             lambda other: arrived.at[i, pl.ds(pl.multiple_of(other * rows, rows), rows), :],
+            arrived.at[i, 0 : group - rows, :],
         )
 
     rows_to_heads(0)
@@ -723,23 +730,28 @@
 
     def to_groups(i):
         exchanges[i].wait_head(
-            0, lambda other: arrived.at[i, pl.ds(pl.multiple_of(other * rows, rows), rows), :]
+            0,
+            lambda other: arrived.at[i, pl.ds(pl.multiple_of(other * rows, rows), rows), :],
+            arrived.at[i, 0 : group - rows, :],
         )
         permute_rows(one_hot_from_column(slot_col, group), arrived.at[i], sorted_rows.at[i], group)
         exchanges[i].over_blk(
             lambda other: sorted_rows.at[i, pl.ds(other * pair, pair), :],
             lambda other: landed.at[i, pl.ds(pl.multiple_of(other * pair, pair), pair), :],
+            landed.at[i, 0 : group - pair, :],
         )
 
     def to_positions(i):
         exchanges[i].wait_blk(
-            lambda other: landed.at[i, pl.ds(pl.multiple_of(other * pair, pair), pair), :]
+            lambda other: landed.at[i, pl.ds(pl.multiple_of(other * pair, pair), pair), :],
+            landed.at[i, 0 : group - pair, :],
         )
         permute_rows(one_hot_from_column(dest_col, group), landed.at[i], ordered.at[i], group)
         exchanges[i].over_head(
             1,
             lambda other: ordered.at[i, pl.ds(other * rows, rows), :],
             lambda other: final.at[i, other],
+            final.at[i, 0 : heads - 1],
         )
 
     for other in order[:2]:
@@ -817,7 +829,7 @@
             vec_sum[...] += vec_heads[other]
 
     for i in range(2):
-        exchanges[i].wait_head(1, lambda other: final.at[i, other])
+        exchanges[i].wait_head(1, lambda other: final.at[i, other], final.at[i, 0 : heads - 1])
     for source in range(heads):
         micro, which = source // splits, source % splits
         out_rows[micro, :, which * part : (which + 1) * part] = final[0, source]
@@ -1396,29 +1408,25 @@
         vec_parts=vmem((blks, 16, 128), F32),
         vec_mid=vmem((16, 128), F32),
         vec_heads=vmem((heads, 16, 128), F32),
-        head_send=dma((4, 2, heads)),
-        head_recv=dma((4, 2, heads)),
-        blk_send=dma((4, blks)),
-        blk_recv=dma((4, blks)),
+        head_send=dma((4, 2)),
+        head_recv=dma((4, 2)),
+        blk_send=dma((4,)),
+        blk_recv=dma((4,)),
         local=dma((4, 3)),
         z_send=dma((2, heads, 2)),
         z_recv=dma((2, heads)),
-        tree_send=dma((2, heads, 2, blks)),
-        tree_recv=dma((2, heads, 2, blks)),
-        gain_send=dma((blks,)),
-        gain_recv=dma((blks,)),
+        tree_send=dma((2,)),
+        tree_recv=dma((2, heads, 2, levels)),
+        small_send=dma((3,)),
+        small_recv=dma((3,)),
         own_sem=dma((2,)),
-        core_send=dma((3, heads, kept)),
-        core_recv=dma((3, heads, kept)),
-        stage_sem=dma((3, heads)),
-        down_send=dma((3, 2, heads, kept)),
-        down_recv=dma((3, 2, heads, kept)),
-        left_send=dma((3, heads)),
-        left_recv=dma((3, heads)),
-        vec_send=dma((blks,)),
-        vec_recv=dma((blks,)),
-        vec_head_send=dma((heads,)),
-        vec_head_recv=dma((heads,)),
+        core_send=dma((3,)),
+        core_recv=dma((3, heads)),
+        stage_sem=dma((2,)),
+        down_send=dma((3,)),
+        down_recv=dma((3, 2, heads, levels - 1)),
+        pair_send=dma((3,)),
+        pair_recv=dma((3, heads)),
         out_sem=dma((2, 3)),
     )
 
@@ -1457,6 +1465,12 @@
     def blk_block(ref, i):
         return lambda other: ref.at[i, pl.ds(pl.multiple_of(other * pair, pair), pair), :]
 
+    def head_blocks(ref, i):
+        return ref.at[i, 0 : group - rows, :]
+
+    def blk_blocks(ref, i):
+        return ref.at[i, 0 : group - pair, :]
+
     def row_source(ref):
         return lambda other: ref.at[
             other // splits, :, (other % splits) * part : (other % splits + 1) * part
@@ -1469,22 +1483,29 @@
         ]
 
     def to_heads(i, source):
-        exchanges[i].over_head(0, source, head_block(r.arrived, i % 2))
+        exchanges[i].over_head(0, source, head_block(r.arrived, i % 2), head_blocks(r.arrived, i % 2))
 
     def to_groups(i, one_hot):
-        exchanges[i].wait_head(0, head_block(r.arrived, i % 2))
+        exchanges[i].wait_head(0, head_block(r.arrived, i % 2), head_blocks(r.arrived, i % 2))
         permute_rows(one_hot, r.arrived.at[i % 2], r.sorted_rows.at[i % 2], group)
-        exchanges[i].over_blk(blk_block(r.sorted_rows, i % 2), blk_block(r.landed, i % 2))
+        exchanges[i].over_blk(
+            blk_block(r.sorted_rows, i % 2), blk_block(r.landed, i % 2), blk_blocks(r.landed, i % 2)
+        )
 
     def to_owners(i, one_hot):
-        exchanges[i].wait_blk(blk_block(r.landed, i % 2))
+        exchanges[i].wait_blk(blk_block(r.landed, i % 2), blk_blocks(r.landed, i % 2))
         permute_rows(one_hot, r.landed.at[i % 2], r.ordered.at[i % 2], group)
         exchanges[i].over_head(
-            1, head_block(r.ordered, i % 2), lambda other: r.slots.at[i % 2, other]
+            1,
+            head_block(r.ordered, i % 2),
+            lambda other: r.slots.at[i % 2, other],
+            r.slots.at[i % 2, 0 : heads - 1],
         )
 
     def rows_here(i):
-        exchanges[i].wait_head(1, lambda other: r.slots.at[i % 2, other])
+        exchanges[i].wait_head(
+            1, lambda other: r.slots.at[i % 2, other], r.slots.at[i % 2, 0 : heads - 1]
+        )
 
 
     parts = ((0, width), (width, 2 * width))
@@ -1512,18 +1533,10 @@
         return slice(base + which * size // 2, base + (which + 1) * size // 2)
 
     def tree_wait(p, j, which, step):
-        dims = orders[which]
-        other = flip(blk, 1 << dims[step], bits)
-        for mask in submasks(dims[:step]):
-            piece = flip(blk, mask | (1 << dims[step]), bits)
-            target = r.packed.at[arrival[j], piece_rows(piece), part_cols(p, which)]
-            remote(
-                target,
-                target,
-                r.tree_send.at[p, j, which, 0],
-                r.tree_recv.at[p, j, which, piece],
-                (other, head),
-            ).wait_recv()
+        pieces = slice(0, share << step)
+        await_bytes(
+            r.packed.at[arrival[j], pieces, part_cols(p, which)], r.tree_recv.at[p, j, which, step]
+        )
 
     def forwards(j):
         left = (arrival[j] > head) & (head > 0)
@@ -1551,20 +1564,22 @@
             if step == levels:
                 continue
             other = flip(blk, 1 << dims[step], bits)
-            for index, mask in enumerate(submasks(dims[:step])):
+            sent = r.packed.at[:, 0 : (blks - 1) * share, part_cols(p)]
+            for mask in submasks(dims[:step]):
                 piece = flip(blk, mask, bits)
                 target = r.packed.at[arrival[j], piece_rows(piece), part_cols(p, which)]
                 first = j == 0 and mask == 0
                 source = r.shard.at[:, part_cols(p, which)] if first else target
                 sends.start(
-                    lambda source=source, target=target, piece=piece, other=other, which=which, slot=(1 << step) - 1 + index: remote(
+                    lambda source=source, target=target, other=other, which=which: remote(
                         source,
                         target,
-                        r.tree_send.at[p, j, which, slot],
-                        r.tree_recv.at[p, j, which, piece],
+                        r.tree_send.at[p],
+                        r.tree_recv.at[p, j, which, step],
                         (other, head),
                     ),
                     tag="weights",
+                    shared=(p, lambda: await_bytes(sent, r.tree_send.at[p])),
                 )
 
     def chain(p, j):
@@ -1595,7 +1610,7 @@
 
     def gain_copy(other, slot):
         return remote(
-            r.small, r.full_vectors.at[slot], r.gain_send.at[other], r.gain_recv.at[slot], (other, head)
+            r.small, r.full_vectors.at[slot], r.small_send.at[0], r.small_recv.at[0], (other, head)
         )
 
 
@@ -1615,35 +1630,27 @@
         return r.packed.at[other, piece_rows(flip(blk, mask, bits)), group_cols(g, which)]
 
     def core_start(g):
+        sent = r.packed.at[:, 0 : blks // 2 * share, group_cols(g)]
         for other in order:
             for mask in even:
                 sends.start(
                     lambda other=other, mask=mask: remote(
                         total(g, other, mask | 1),
                         r.from_core.at[g, other, mask // 2],
-                        r.core_send.at[g, other, mask // 2],
-                        r.core_recv.at[g, other, mask // 2],
+                        r.core_send.at[g],
+                        r.core_recv.at[g, other],
                         (sibling, head),
-                    )
+                    ),
+                    shared=(("core", g), lambda: await_bytes(sent, r.core_send.at[g])),
                 )
 
     def core_load(g, i):
-        other = order[i]
         return pltpu.make_async_copy(
-            r.from_core.at[g, other], r.staged.at[i % 2], r.stage_sem.at[g, i]
+            r.from_core.at[g, order[i]], r.staged.at[i % 2], r.stage_sem.at[i % 2]
         )
 
     def core_arrived(g, i):
-        other = order[i]
-        for mask in even:
-            target = r.from_core.at[g, other, mask // 2]
-            remote(
-                target,
-                target,
-                r.core_send.at[g, other, mask // 2],
-                r.core_recv.at[g, other, mask // 2],
-                (sibling, head),
-            ).wait_recv()
+        await_bytes(r.from_core.at[g, order[i]], r.core_recv.at[g, order[i]])
         core_load(g, i).start()
 
     def core_add(g):
@@ -1661,30 +1668,31 @@
         base = sum(1 << (levels - 2 - earlier) for earlier in range(step))
         return dims[step], [(mask, base + i) for i, mask in enumerate(submasks(dims[step + 1 :]))]
 
-    def tree_copy(g, other, which, dim, mask, slot):
-        return remote(
-            total(g, other, mask | (1 << dim), which),
-            r.from_tree.at[g, which, other, slot],
-            r.down_send.at[g, which, other, slot],
-            r.down_recv.at[g, which, other, slot],
-            (flip(blk, 1 << dim, bits), head),
-        )
-
     def tree_start(g, other, step):
+        sent = r.packed.at[:, 0 : (blks // 2 - 1) * share, group_cols(g)]
         for which in range(2):
             dim, slots = tree_slots(which, step)
             for mask, slot in slots:
                 sends.start(
-                    lambda which=which, dim=dim, mask=mask, slot=slot: tree_copy(
-                        g, other, which, dim, mask, slot
-                    )
+                    lambda which=which, dim=dim, mask=mask, slot=slot: remote(
+                        total(g, other, mask | (1 << dim), which),
+                        r.from_tree.at[g, which, other, slot],
+                        r.down_send.at[g],
+                        r.down_recv.at[g, which, other, step],
+                        (flip(blk, 1 << dim, bits), head),
+                    ),
+                    shared=(("down", g), lambda: await_bytes(sent, r.down_send.at[g])),
                 )
 
     def tree_add(g, other, step):
         for which in range(2):
-            dim, slots = tree_slots(which, step)
+            _, slots = tree_slots(which, step)
+            first, count = slots[0][1], len(slots)
+            await_bytes(
+                r.from_tree.at[g, which, other, first : first + count],
+                r.down_recv.at[g, which, other, step],
+            )
             for mask, slot in slots:
-                tree_copy(g, other, which, dim, mask, slot).wait_recv()
                 add_into(
                     total(g, other, mask, which), r.from_tree.at[g, which, other, slot], width // 2
                 )
@@ -1695,26 +1703,61 @@
         for other in order:
             tree_add(g, other, step)
 
-    def direct_copy(g, goal, source):
+    partner = head + 1 - 2 * (head % 2)
+    others = range(1, heads // 2)
+
+    def far(distance):
+        return (head + 2 * distance) % heads
+
+    def far_partner(distance):
+        return (partner + 2 * distance) % heads
+
+    def sum_copy(g, goal, slot, device):
         return remote(
             total(g, goal, 0),
-            r.from_head.at[g, source],
-            r.left_send.at[g, goal],
-            r.left_recv.at[g, source],
-            (blk, goal),
-        )
+            r.from_head.at[g, slot],
+            r.pair_send.at[g],
+            r.pair_recv.at[g, slot],
+            (blk, device),
+        )
+
+    def sum_start(g, goal, slot, device, when=None):
+        sent = r.packed.at[0, 0 : (heads - 1) * share, group_cols(g)]
+        sends.start(
+            lambda: sum_copy(g, goal, slot, device),
+            when=when,
+            shared=(("pair", g), lambda: await_bytes(sent, r.pair_send.at[g])),
+        )
+
+    def sum_add(g, goal, slot):
+        await_bytes(r.from_head.at[g, slot], r.pair_recv.at[g, slot])
+        add_into(total(g, goal, 0), r.from_head.at[g, slot], width)
 
     def direct_start(g):
         for goal in range(heads):
-            sends.start(lambda goal=goal: direct_copy(g, goal, head), when=goal != head)
+            sum_start(g, goal, head, goal, when=goal != head)
 
     def direct_add(g):
         for source in range(heads):
 
             @pl.when(source != head)
             def _():
-                direct_copy(g, source, source).wait_recv()
-                add_into(total(g, head, 0), r.from_head.at[g, source], width)
+                sum_add(g, head, source)
+
+    def pair_start(g):
+        sum_start(g, partner, 0, partner)
+        for distance in others:
+            sum_start(g, far_partner(distance), distance, partner)
+
+    def pair_forward(g):
+        for distance in others:
+            sum_add(g, far(distance), distance)
+            sum_start(g, far(distance), heads // 2 + distance, far(distance))
+
+    def pair_add(g):
+        sum_add(g, head, 0)
+        for distance in others:
+            sum_add(g, head, heads // 2 + distance)
 
 
     micro = head // splits
@@ -1979,8 +2022,8 @@
         return remote(
             r.vec_split.at[other],
             r.vec_parts.at[slot],
-            r.vec_send.at[other],
-            r.vec_recv.at[slot],
+            r.small_send.at[1],
+            r.small_recv.at[1],
             (other, head),
         )
 
@@ -1988,8 +2031,8 @@
         return remote(
             r.vec_mid,
             r.vec_heads.at[slot],
-            r.vec_head_send.at[other],
-            r.vec_head_recv.at[slot],
+            r.small_send.at[2],
+            r.small_recv.at[2],
             (blk, other),
         )
 
@@ -2013,53 +2056,64 @@
         r.small_sums[...] = jnp.zeros_like(r.small_sums)
         for i in range(8):
             r.small_sums[i : i + 1, 0:share] = getattr(r, "vector%d" % i)[...].astype(F32)
+        bias = r.up_bias_here[...].astype(F32)
+        bias = jnp.concatenate([bias[i : i + 1] for i in range(bias.shape[0])], axis=1)
         for j in range(fold):
-            r.small_sums[8 + j : 9 + j, 0:share] = r.up_bias_here[
-                :, j * share : (j + 1) * share
-            ].astype(F32)
+            r.small_sums[8 + j : 9 + j, 0:share] = bias[:, j * share : (j + 1) * share]
         r.small[...] = r.small_sums[...].astype(BF16)
 
     def send_small():
+        sent = r.full_vectors.at[0 : blks - 1]
         for other in range(blks):
-            sends.start(lambda other=other: gain_copy(other, blk), when=other != blk)
+            sends.start(
+                lambda other=other: gain_copy(other, blk),
+                when=other != blk,
+                shared=("gain", lambda: await_bytes(sent, r.small_send.at[0])),
+            )
         own_gain.start()
         own_shard.start()
 
     def take_small():
-        for other in range(blks):
-
-            @pl.when(other != blk)
-            def _():
-                gain_copy(other, other).wait_recv()
-
+        await_bytes(r.full_vectors.at[0 : blks - 1], r.small_recv.at[0])
         own_gain.wait()
         own_shard.wait()
         spread_vectors()
 
     def send_vectors():
         split_vectors()
+        sent = r.vec_parts.at[0 : blks - 1]
         for other in range(blks):
-            sends.start(lambda other=other: vec_copy(other, blk), when=other != blk)
+            sends.start(
+                lambda other=other: vec_copy(other, blk),
+                when=other != blk,
+                shared=("vec", lambda: await_bytes(sent, r.small_send.at[1])),
+            )
 
     def sum_vectors_over_blk():
-        r.vec_mid[...] = r.vec_split[pl.ds(blk, 1)][0]
+        await_bytes(r.vec_parts.at[0 : blks - 1], r.small_recv.at[1])
+        r.vec_mid[...] = jnp.zeros_like(r.vec_mid)
         for other in range(blks):
 
             @pl.when(other != blk)
             def _():
-                vec_copy(other, other).wait_recv()
                 r.vec_mid[...] += r.vec_parts[other]
 
+        r.vec_mid[...] += r.vec_split[pl.ds(blk, 1)][0]
+        sent = r.vec_heads.at[0 : heads - 1]
         for other in range(heads):
-            sends.start(lambda other=other: vec_head_copy(other, head), when=other != head)
+            sends.start(
+                lambda other=other: vec_head_copy(other, head),
+                when=other != head,
+                shared=("vec head", lambda: await_bytes(sent, r.small_send.at[2])),
+            )
 
     def sum_vectors_over_head():
+        await_bytes(r.vec_heads.at[0 : heads - 1], r.small_recv.at[2])
         r.vec_sum[...] = r.vec_mid[...]
         for other in range(heads):
 
             @pl.when(other != head)
             def _():
-                vec_head_copy(other, other).wait_recv()
                 r.vec_sum[...] += r.vec_heads[other]
 
     own_gain = pltpu.make_async_copy(r.small, r.full_vectors.at[blk], r.own_sem.at[0])
@@ -2131,7 +2185,6 @@
     tree_step(0, 3, 1)
     tree_step(0, 2, 2)
     take_small()
-    tree_step(1, 3, 0)
     tree_step(1, 2, 1)
     tree_step(0, 3, 2)
     tree_step(1, 1, 2)
@@ -2140,17 +2193,18 @@
     tree_step(0, 2, 3)
     tree_step(0, 3, 3)
     assemble_attention(r.packed, r.qkv, r.out)
-    tree_step(1, 3, 1)
     tree_step(1, 2, 2)
     rows_here(0)
     take_rows()
     project(r.x, r.qkv, r.bias_qkv, r.proj)
+    tree_step(1, 3, 0)
     to_groups(1, one_hot_from_row(r.dest_row))
+    tree_step(1, 3, 1)
+    attend(r.proj, r.probs, r.context, r.seg_col, r.seg_row)
+    to_owners(1, one_hot_from_row(r.slot_row))
     tree_step(1, 3, 2)
-    attend(r.proj, r.probs, r.context, r.seg_col, r.seg_row)
     leave_attention(r.x, r.context, r.out, r.vectors, r.attn_res)
     first_norm()
-    to_owners(1, one_hot_from_row(r.slot_row))
     tree_step(1, 0, 3)
     ffn_up(arrival[0])
     tree_step(1, 1, 3)
@@ -2170,10 +2224,10 @@
     down_gradient()
     core_start(2)
     ffn_up_back()
-    norm_cotangent()
     sends.finish(0)
     to_groups(2, one_hot_from_column(r.slot_col, group))
     core_add(2)
+    norm_cotangent()
     up_gradient()
     core_start(1)
     first_norm_back()
@@ -2190,24 +2244,26 @@
     core_start(0)
     send_vectors()
     tree_down(2, 1)
-    direct_start(2)
+    pair_start(2)
     tree_down(1, 0)
+    sends.finish(1)
+    to_groups(3, one_hot_from_column(r.slot_col, group))
     core_add(0)
-    sends.finish(1)
+    pair_forward(2)
+    tree_down(1, 1)
+    pair_start(1)
     sum_vectors_over_blk()
-    to_groups(3, one_hot_from_column(r.slot_col, group))
-    tree_down(1, 1)
-    direct_start(1)
-    direct_add(2)
-    shard_copy(2).start()
     to_owners(3, one_hot_from_column(r.dest_col, group))
+    pair_forward(1)
     tree_down(0, 0)
     sum_vectors_over_head()
+    pair_add(2)
+    shard_copy(2).start()
     tree_down(0, 1)
     direct_start(0)
     rows_here(2)
     row_copy(0).start()
-    direct_add(1)
+    pair_add(1)
     shard_copy(1).start()
     direct_add(0)
     shard_copy(0).start()
@@ -2247,25 +2303,37 @@
         *weights[:3],
         weights[3].T,
         *[vector.reshape(1, -1) for vector in vectors],
-        up_bias.reshape(1, -1),
+        up_bias.reshape(-1, 128 if up_bias.shape[0] % 128 == 0 else up_bias.shape[0]),
         perm,
         seq_lengths,
     )[:3]
 
 
 def unpack_kernel(
-    row_results, shard, sums, layer_out, x_grad, qkv, out, up, down, up_bias, *vectors
+    rows_in, shard_in, sums_in, layer_out, x_grad, qkv, out, up, down, up_bias, *rest
 ):
+    vectors, (row_results, shard, sums, sem) = rest[:8], rest[8:]
     micros, rows, width = layer_out.shape
+    copies = [
+        pltpu.make_async_copy(source, target, sem.at[i])
+        for i, (source, target) in enumerate(
+            ((sums_in, sums), (shard_in, shard), (rows_in, row_results))
+        )
+    ]
+    for copy in copies:
+        copy.start()
     _, heads, _, part = row_results.shape
     splits = heads // micros
     share, short = out.shape
     fold = down.shape[1] // share
-    for source in range(heads):
-        m, which = source // splits, source % splits
-        cols = slice(which * part, (which + 1) * part)
-        layer_out[m, :, cols] = row_results[0, source]
-        x_grad[m, :, cols] = row_results[1, source].astype(F32)
+    copies[0].wait()
+    for i, vector in enumerate(vectors):
+        vector[...] = sums[i : i + 1, 0:share]
+    bias = jnp.concatenate([sums[8 + j : 9 + j, 0:share] for j in range(fold)], axis=1)
+    lanes = up_bias.shape[1]
+    for i in range(up_bias.shape[0]):
+        up_bias[i : i + 1, :] = bias[:, i * lanes : (i + 1) * lanes]
+    copies[1].wait()
     at = 0
     for target in (qkv, out, up):
         target[...] = shard[:, at : at + target.shape[1]].astype(F32)
@@ -2274,10 +2342,12 @@
         shard[:, at + j * short : at + (j + 1) * short].astype(F32) for j in range(fold)
     ]
     down[...] = jnp.concatenate(pieces, axis=0).T
-    for i, vector in enumerate(vectors):
-        vector[...] = sums[i : i + 1, 0:share]
-    for j in range(fold):
-        up_bias[:, j * share : (j + 1) * share] = sums[8 + j : 9 + j, 0:share]
+    copies[2].wait()
+    for source in range(heads):
+        m, which = source // splits, source % splits
+        cols = slice(which * part, (which + 1) * part)
+        layer_out[m, :, cols] = row_results[0, source]
+        x_grad[m, :, cols] = row_results[1, source].astype(F32)
 
 
 def unpack(micros, width, widths, row_results, shard, sums):
@@ -2285,7 +2355,9 @@
     share = shard.shape[0]
     vmem = pl.BlockSpec(memory_space=pltpu.VMEM)
     shapes = [(share, widths[0]), (share, widths[1]), (share, widths[2])]
-    shapes += [(widths[1], widths[3] // widths[1] * share), (1, widths[3] // widths[1] * share)]
+    long = widths[3] // widths[1] * share
+    lanes = 128 if long % 128 == 0 else long
+    shapes += [(widths[1], long), (long // lanes, lanes)]
     shapes += [(1, share)] * 8
     results = pl.pallas_call(
         unpack_kernel,
@@ -2295,9 +2367,15 @@
             jax.ShapeDtypeStruct((micros, rows, width), F32),
         )
         + tuple(jax.ShapeDtypeStruct(shape, F32) for shape in shapes),
-        in_specs=[vmem] * 3,
+        in_specs=[pl.BlockSpec(memory_space=pltpu.HBM)] * 3,
         out_specs=(vmem,) * (2 + len(shapes)),
-        compiler_params=pltpu.CompilerParams(vmem_limit_bytes=32 << 20),
+        scratch_shapes=[
+            pltpu.VMEM(row_results.shape, BF16),
+            pltpu.VMEM(shard.shape, BF16),
+            pltpu.VMEM(sums.shape, F32),
+            pltpu.SemaphoreType.DMA((3,)),
+        ],
+        compiler_params=pltpu.CompilerParams(vmem_limit_bytes=62 << 20),
     )(row_results, shard, sums)
     layer_out, x_grad, qkv, out, up, down, up_bias = results[:7]
     vec = [member.reshape(-1) for member in results[7:]]

time: 253 us -> 236 us (0.933)
  Pallas kernels: 245 us -> 232 us
  local copies, waits for them, and re-layouts: 4.35 us -> 0 us
    pallas_call x1, Pallas kernels: 243 us -> 228 us  [fused(): pl.pallas_call(functools.partial(fused_kernel, names, blks, heads, share,...]
    unnamed x6 -> x0, local copies, waits for them, and re-layouts: 3.11 us -> none
where the time goes in v5:
time: 236 us; the launch traced here: 232 us
  Pallas kernels  232 us (98%)
    pallas_call x1, Pallas kernels, fused(): pl.pallas_call(functools.partial(fused_kernel, names, blks, heads, share,...  228 us

profile of v5, /device:TPU:8, one launch (start us, length us, event | category | flops | bytes accessed | tf_op | source)
XLA Modules:
  0.0 232.4 jit_solution(10645742731476721007)
XLA Ops:
  0.7 228.2 %fused.1 = (bf16[2,4,256,384]{3,2,1,0:T(8,128)(2,1)}, bf16[96,2304]{1,0:T(8,128)(2,1)}, f32[16,128]{1,0:T(8,128)}, bf16[3,4,4,96,768]{4,3,2,1,0:T(8,128)(2,1)}) custom-call(bf16[2,256,768]{2,1,0:T(8,128)(2,1)} %refs_0_.1, bf16[2,256,768]{2,1,0:T(8,128)(2,1)} %refs_1_.1, bf16[96,576]{1,0:T(8,128)(2,1)} %refs_2_.1, bf16[96,192]{1,0:T(8,128)(2,1)} %refs_3_.1, ...), custom_call_target="tpu_custom_call" | custom-call | tf_op jit(solution)/shard_map/fused/pallas_call | solution.py:2285
  228.9 3.4 %unpack.1 = (bf16[2,256,768]{2,1,0:T(8,128)(2,1)}, f32[2,256,768]{2,1,0:T(8,128)}, f32[96,576]{1,0:T(8,128)}, f32[96,192]{1,0:T(8,128)}, f32[96,768]{1,0:T(8,128...) custom-call(bf16[2,4,256,384]{3,2,1,0:T(8,128)(2,1)} %get-tuple-elem, ...), custom_call_target="tpu_custom_call" | custom-call | tf_op jit(solution)/shard_map/unpack/pallas_call | solution.py:2362

commit v6 on v5

--- a/solution.py
+++ b/solution.py
@@ -10,7 +10,7 @@
 
 HEAD_DIM = 64
 CLUSTER = 128
-TILE = 256
+TILE = 512
 MESH = pl.DeviceIdType.MESH
 BF16 = jnp.bfloat16
 F32 = jnp.float32
@@ -965,7 +965,7 @@
 
 
 def project(x, qkv, bias_qkv, proj):
-    @pl.loop(0, proj.shape[1] // 256)
+    @pl.loop(0, proj.shape[1] // 256, unroll=3)
     def _(tile):
         cols = pl.ds(pl.multiple_of(tile * 256, 256), 256)
         sums = jnp.dot(x[...], qkv[:, cols], preferred_element_type=F32)
@@ -1450,7 +1450,7 @@
 
     def tiles(count, size):
         def run(body):
-            @pl.loop(0, count)
+            @pl.loop(0, count, unroll=2 if count % 2 == 0 else 1)
             def _(tile):
                 body(tile, pl.ds(pl.multiple_of(tile * size, size), size))
 
@@ -1907,7 +1907,7 @@
             r.vec_grads[7:8, :] += column_sum(cotangent)
 
     def down_gradient():
-        @pl.loop(0, width // share)
+        @pl.loop(0, width // share, unroll=2)
         def _(b):
             wide = share * fold
             cols = pl.ds(pl.multiple_of(b * wide, wide), wide)
@@ -2194,13 +2194,13 @@
     tree_step(0, 3, 3)
     assemble_attention(r.packed, r.qkv, r.out)
     tree_step(1, 2, 2)
+    tree_step(1, 3, 0)
     rows_here(0)
     take_rows()
     project(r.x, r.qkv, r.bias_qkv, r.proj)
-    tree_step(1, 3, 0)
     to_groups(1, one_hot_from_row(r.dest_row))
+    attend(r.proj, r.probs, r.context, r.seg_col, r.seg_row)
     tree_step(1, 3, 1)
-    attend(r.proj, r.probs, r.context, r.seg_col, r.seg_row)
     to_owners(1, one_hot_from_row(r.slot_row))
     tree_step(1, 3, 2)
     leave_attention(r.x, r.context, r.out, r.vectors, r.attn_res)
@@ -2224,10 +2224,10 @@
     down_gradient()
     core_start(2)
     ffn_up_back()
+    norm_cotangent()
     sends.finish(0)
     to_groups(2, one_hot_from_column(r.slot_col, group))
     core_add(2)
-    norm_cotangent()
     up_gradient()
     core_start(1)
     first_norm_back()

time: 236 us -> 230 us (0.975); the launches traced: 232 us -> 229 us
  Pallas kernels: 232 us -> 228 us
    pallas_call x1, Pallas kernels: 228 us -> 225 us  [fused(): pl.pallas_call(functools.partial(fused_kernel, names, blks, heads, share,...]
where the time goes in v6:
time: 230 us; the launch traced here: 229 us
  Pallas kernels  228 us (99%)
    pallas_call x1, Pallas kernels, fused(): pl.pallas_call(functools.partial(fused_kernel, names, blks, heads, share,...  225 us

profile of v6, /device:TPU:8, one launch (start us, length us, event | category | flops | bytes accessed | tf_op | source)
XLA Modules:
  0.0 228.9 jit_solution(17449514564528512482)
XLA Ops:
  0.7 224.7 %fused.1 = (bf16[2,4,256,384]{3,2,1,0:T(8,128)(2,1)}, bf16[96,2304]{1,0:T(8,128)(2,1)}, f32[16,128]{1,0:T(8,128)}, bf16[3,4,4,96,768]{4,3,2,1,0:T(8,128)(2,1)}) custom-call(bf16[2,256,768]{2,1,0:T(8,128)(2,1)} %refs_0_.1, bf16[2,256,768]{2,1,0:T(8,128)(2,1)} %refs_1_.1, bf16[96,576]{1,0:T(8,128)(2,1)} %refs_2_.1, bf16[96,192]{1,0:T(8,128)(2,1)} %refs_3_.1, ...), custom_call_target="tpu_custom_call" | custom-call | tf_op jit(solution)/shard_map/fused/pallas_call | solution.py:2285
  225.4 3.4 %unpack.1 = (bf16[2,256,768]{2,1,0:T(8,128)(2,1)}, f32[2,256,768]{2,1,0:T(8,128)}, f32[96,576]{1,0:T(8,128)}, f32[96,192]{1,0:T(8,128)}, f32[96,768]{1,0:T(8,128...) custom-call(bf16[2,4,256,384]{3,2,1,0:T(8,128)(2,1)} %get-tuple-elem, ...), custom_call_target="tpu_custom_call" | custom-call | tf_op jit(solution)/shard_map/unpack/pallas_call | solution.py:2362
